TPU v7x, 32 devices: a whole 2x2x4 slice. The times are simulated.
32 devices in a mesh: dp: 4 (over x, core), expert: 2 (over y), tensor: 4 (over z).
Axes of the slice: x: 2, y: 2, z: 4, core: 2. Of those that a mesh axis runs over, the one named last changes fastest.
Arguments:
- tokens: bfloat16 [8, 256, 2048], P(('dp', 'expert')), may hold values from -6 to 6
- cotangent: bfloat16 [8, 256, 2048], P(('dp', 'expert')), may hold values from -6 to 6
- head_counts: int32 [8], P(('dp', 'expert')), may hold values from 4 to 16, as said below
- positions: int32 [8, 256], P(('dp', 'expert')), may hold values from 0 to 255, as said below
- buckets: int32 [8, 256], P(('dp', 'expert')), may hold values from 0 to 3, as said below
- in_master: float32 [3, 2048, 2048], P(None, ('dp', 'expert'), 'tensor'), may hold values from -0.13258252 to 0.13258252
- out_master: float32 [2048, 2048], P('tensor', ('dp', 'expert')), may hold values from -1.5 to 1.5
- up_master: float32 [4, 2048, 2048], P(None, ('dp', 'expert'), 'tensor'), may hold values from -0.13258252 to 0.13258252
- down_master: float32 [4, 2048, 2048], P(None, 'tensor', ('dp', 'expert')), may hold values from -0.06629126 to 0.06629126
- norm_master: float32 [4, 2048], P(None, ('dp', 'expert')), may hold values from -0.6 to 2.4
- in_first: float32 [3, 2048, 2048], P(None, ('dp', 'expert'), 'tensor'), may hold values from -32 to 32
- out_first: float32 [2048, 2048], P('tensor', ('dp', 'expert')), may hold values from -6 to 6
- up_first: float32 [4, 2048, 2048], P(None, ('dp', 'expert'), 'tensor'), may hold values from -16 to 16
- down_first: float32 [4, 2048, 2048], P(None, 'tensor', ('dp', 'expert')), may hold values from -28 to 28
- norm_first: float32 [4, 2048], P(None, ('dp', 'expert')), may hold values from -32 to 32
- in_second: float32 [3, 2048, 2048], P(None, ('dp', 'expert'), 'tensor'), may hold values from 1.024 to 16.384
- out_second: float32 [2048, 2048], P('tensor', ('dp', 'expert')), may hold values from 0.0065536 to 0.1048576
- up_second: float32 [4, 2048, 2048], P(None, ('dp', 'expert'), 'tensor'), may hold values from 0.3072 to 4.9152
- down_second: float32 [4, 2048, 2048], P(None, 'tensor', ('dp', 'expert')), may hold values from 0.9216 to 14.7456
- norm_second: float32 [4, 2048], P(None, ('dp', 'expert')), may hold values from 1.024 to 16.384
Outputs:
- output: float32 [8, 256, 2048], P(('dp', 'expert'))
- input_grad: float32 [8, 256, 2048], P(('dp', 'expert'))
- bucket_share: float32 [4], replicated
- lamb_norms: float32 [2, 8], replicated
- in_weight: float32 [3, 2048, 2048], P(None, ('dp', 'expert'), 'tensor')
- out_weight: float32 [2048, 2048], P('tensor', ('dp', 'expert'))
- up_weight: float32 [4, 2048, 2048], P(None, ('dp', 'expert'), 'tensor')
- down_weight: float32 [4, 2048, 2048], P(None, 'tensor', ('dp', 'expert'))
- norm_weight: float32 [4, 2048], P(None, ('dp', 'expert'))
- in_moment: float32 [3, 2048, 2048], P(None, ('dp', 'expert'), 'tensor')
- out_moment: float32 [2048, 2048], P('tensor', ('dp', 'expert'))
- up_moment: float32 [4, 2048, 2048], P(None, ('dp', 'expert'), 'tensor')
- down_moment: float32 [4, 2048, 2048], P(None, 'tensor', ('dp', 'expert'))
- norm_moment: float32 [4, 2048], P(None, ('dp', 'expert'))
- in_square: float32 [3, 2048, 2048], P(None, ('dp', 'expert'), 'tensor')
- out_square: float32 [2048, 2048], P('tensor', ('dp', 'expert'))
- up_square: float32 [4, 2048, 2048], P(None, ('dp', 'expert'), 'tensor')
- down_square: float32 [4, 2048, 2048], P(None, 'tensor', ('dp', 'expert'))
- norm_square: float32 [4, 2048], P(None, ('dp', 'expert'))
Inputs may be any that keep to these rules, and one draw needn't show every extreme that they name: `head_counts`: each is a whole multiple of a quarter of 16. Within each sequence positions count up by one from 0 and restart at 0 at a document's first token; each sequence's first token has position 0. `buckets`: in each sequence no bucket id is carried by more than 80 tokens; one bucket id, the same for all sequences, is carried by exactly 80 tokens of every sequence.
All inputs are finite; a program needn't handle non-finite values.
Results may differ from a plain program's by a relative error of at most 0.014.
The roundings to bfloat16 on the way count: a program that leaves them out, or rounds other values in their place, can miss the bound.
Values may be sent and summed in bfloat16 or wider, within the bound.
A program may use at most 448 MiB of HBM per device.

v0:
```python
import jax
import jax.numpy as jnp
from jax import lax
from jax.sharding import PartitionSpec as P

HEAD_DIM = 128
STEP = 10


NORM_EPS = 1e-05
BETA_FIRST = 0.9
BETA_SECOND = 0.999
ADAM_EPS = 1e-06
WEIGHT_DECAY = 0.01
LEARN_RATE = 0.25
MASKED = -1e30
ROPE_BASE = 10000.0


def layer_norm(values, gain_row, shift_row):
    center = values - jnp.mean(values, -1, keepdims=True)
    variance = jnp.mean(center * center, -1, keepdims=True)
    inv_std = lax.rsqrt(variance + NORM_EPS)
    normed = center * inv_std
    return (normed * gain_row + shift_row, normed, inv_std)


def norm_back(grad_out, normed, inv_std, gain_row):
    scaled = grad_out * gain_row
    inner_part = (
        scaled
        - jnp.mean(scaled, -1, keepdims=True)
        - normed * jnp.mean(scaled * normed, -1, keepdims=True)
    )
    return (inner_part * inv_std, jnp.sum(grad_out * normed, 0), jnp.sum(grad_out, 0))


def rope_angles(position_row):
    freq_index = jnp.arange(HEAD_DIM // 2, dtype=jnp.float32)
    inverse = jnp.exp(freq_index * (-2.0 * jnp.log(ROPE_BASE) / HEAD_DIM))
    return position_row.astype(jnp.float32)[:, None] * inverse[None, :]


def rotary(values, angles, sign_value):
    half_dim = values.shape[-1] // 2
    cosine = jnp.cos(angles)[:, None, :]
    sine_part = sign_value * jnp.sin(angles)[:, None, :]
    first_half = values[..., :half_dim]
    second_half = values[..., half_dim:]
    return jnp.concatenate(
        [
            first_half * cosine - second_half * sine_part,
            second_half * cosine + first_half * sine_part,
        ],
        -1,
    )


def block_mask(key_index, position_row, block_start, block_rows):
    query_index = block_start + jnp.arange(block_rows, dtype=jnp.int32)
    return (key_index[None, :] <= query_index[:, None]) & (
        key_index[None, :] >= (query_index - position_row)[:, None]
    )


def attend_forward(queries, key_rows, value_rows, position_row, block_rows):
    length = queries.shape[0]
    key_index = jnp.arange(length, dtype=jnp.int32)

    def one_block(block_start):
        allowed = block_mask(key_index, position_row, block_start, block_rows)
        scores = jnp.einsum("qhd,khd->hqk", queries, key_rows, preferred_element_type=jnp.float32)
        scores = jnp.where(allowed[None], scores, MASKED)
        row_peak = jnp.max(scores, -1, keepdims=True)
        exp_scores = jnp.exp(scores - row_peak)
        row_total = jnp.sum(exp_scores, -1, keepdims=True)
        attn_weights = (exp_scores / row_total).astype(jnp.bfloat16)
        block_out = jnp.einsum(
            "hqk,khd->qhd", attn_weights, value_rows, preferred_element_type=jnp.float32
        )
        return (block_out, row_peak[..., 0] + jnp.log(row_total[..., 0]))

    starts = jnp.arange(length // block_rows, dtype=jnp.int32) * block_rows
    block_outs, log_totals = lax.map(one_block, starts)
    return (block_outs.reshape(queries.shape), log_totals, starts)


def attend_backward(
    queries, key_rows, value_rows, position_row, grad_heads, log_totals, starts, block_rows
):
    length = queries.shape[0]
    key_index = jnp.arange(length, dtype=jnp.int32)

    def one_block(carried, inputs):
        block_start, block_log = inputs
        allowed = block_mask(key_index, position_row, block_start, block_rows)
        scores = jnp.einsum("qhd,khd->hqk", queries, key_rows, preferred_element_type=jnp.float32)
        scores = jnp.where(allowed[None], scores, MASKED)
        attn_probs = jnp.exp(scores - block_log[..., None])
        grad_probs = jnp.einsum(
            "qhd,khd->hqk", grad_heads, value_rows, preferred_element_type=jnp.float32
        )
        row_inner = jnp.sum(attn_probs * grad_probs, -1, keepdims=True)
        grad_scores = (attn_probs * (grad_probs - row_inner)).astype(jnp.bfloat16)
        grad_query = jnp.einsum(
            "hqk,khd->qhd", grad_scores, key_rows, preferred_element_type=jnp.float32
        )
        grad_keys = carried[0] + jnp.einsum(
            "hqk,qhd->khd", grad_scores, queries, preferred_element_type=jnp.float32
        )
        grad_values = carried[1] + jnp.einsum(
            "hqk,qhd->khd",
            attn_probs.astype(jnp.bfloat16),
            grad_heads,
            preferred_element_type=jnp.float32,
        )
        return ((grad_keys, grad_values), grad_query)

    start_state = (jnp.zeros(key_rows.shape, jnp.float32), jnp.zeros(value_rows.shape, jnp.float32))
    (grad_keys, grad_values), grad_query = lax.scan(one_block, start_state, (starts, log_totals))
    return (grad_query.reshape(queries.shape), grad_keys, grad_values)


def gather_rows(values, source_rows):
    padded = jnp.concatenate([values, jnp.zeros((1, values.shape[1]), values.dtype)], 0)
    return padded[source_rows]


def ffn_forward(rows_in, bucket, up_work, down_work):
    row_count = rows_in.shape[0]
    mixed_sum = jnp.zeros((row_count, down_work.shape[2]), jnp.float32)
    hiddens = []
    for quarter in range(4):

        def live_part():
            hidden = jnp.dot(rows_in, up_work[quarter], preferred_element_type=jnp.float32)
            squared = jnp.square(jnp.maximum(hidden, 0.0)).astype(jnp.bfloat16)
            return (
                hidden,
                jnp.dot(squared, down_work[quarter], preferred_element_type=jnp.float32),
            )

        def dead_part():
            return (
                jnp.zeros((row_count, up_work.shape[2]), jnp.float32),
                jnp.zeros_like(mixed_sum),
            )

        hidden, contribution = lax.cond(bucket >= quarter, live_part, dead_part)
        hiddens.append(hidden)
        mixed_sum = mixed_sum + contribution
    return (mixed_sum, hiddens)


def ffn_backward(rows_in, grads_in, bucket, hiddens, up_work, down_work):
    grad_rows = jnp.zeros((rows_in.shape[0], up_work.shape[1]), jnp.float32)
    grad_up = []
    grad_down = []
    for quarter in range(4):
        hidden = hiddens[quarter]

        def live_part():
            rectified = jnp.maximum(hidden, 0.0)
            squared = jnp.square(rectified).astype(jnp.bfloat16)
            grad_square = jnp.einsum(
                "rd,ud->ru", grads_in, down_work[quarter], preferred_element_type=jnp.float32
            )
            grad_hidden = (grad_square * 2.0 * rectified).astype(jnp.bfloat16)
            return (
                jnp.einsum("rd,ru->du", rows_in, grad_hidden, preferred_element_type=jnp.float32),
                jnp.einsum("ru,rd->ud", squared, grads_in, preferred_element_type=jnp.float32),
                jnp.einsum(
                    "ru,du->rd", grad_hidden, up_work[quarter], preferred_element_type=jnp.float32
                ),
            )

        def dead_part():
            return (
                jnp.zeros(up_work.shape[1:], jnp.float32),
                jnp.zeros(down_work.shape[1:], jnp.float32),
                jnp.zeros_like(grad_rows),
            )

        part_up, part_down, part_rows = lax.cond(bucket >= quarter, live_part, dead_part)
        grad_up.append(part_up)
        grad_down.append(part_down)
        grad_rows = grad_rows + part_rows
    return (grad_rows, jnp.stack(grad_up), jnp.stack(grad_down))


def ffn_total(partial_value):
    return lax.psum(partial_value, "tensor")


def ffn_grad_total(partial_value):
    return lax.psum(partial_value, "tensor")


def adam_terms(weight, gradient, first_old, second_old):
    first_new = BETA_FIRST * first_old + (1.0 - BETA_FIRST) * gradient
    second_new = BETA_SECOND * second_old + (1.0 - BETA_SECOND) * gradient * gradient
    update = (
        first_new
        / (1.0 - BETA_FIRST**STEP)
        / (jnp.sqrt(second_new / (1.0 - BETA_SECOND**STEP)) + ADAM_EPS)
        + WEIGHT_DECAY * weight
    )
    return (update, first_new, second_new)


def body(
    tokens,
    cotangent,
    head_counts,
    positions,
    buckets,
    in_master,
    out_master,
    up_master,
    down_master,
    norm_master,
    in_first,
    out_first,
    up_first,
    down_first,
    norm_first,
    in_second,
    out_second,
    up_second,
    down_second,
    norm_second,
):
    in_work, out_work, up_work, down_work, norm_work = (
        lax.all_gather(in_master.astype(jnp.bfloat16), ("dp", "expert"), axis=1, tiled=True),
        lax.all_gather(out_master.astype(jnp.bfloat16), ("dp", "expert"), axis=1, tiled=True),
        lax.all_gather(up_master.astype(jnp.bfloat16), ("dp", "expert"), axis=1, tiled=True),
        lax.all_gather(down_master.astype(jnp.bfloat16), ("dp", "expert"), axis=2, tiled=True),
        lax.all_gather(norm_master.astype(jnp.bfloat16), ("dp", "expert"), axis=1, tiled=True),
    )
    length = tokens.shape[1]
    model_width = tokens.shape[2]
    heads_here = in_work.shape[2] // HEAD_DIM
    block_rows = min(512, length)
    head_scale = HEAD_DIM ** (-0.5)
    groups_data = lax.axis_size("dp") * lax.axis_size("expert")
    tensor_count = lax.axis_size("tensor")
    experts = lax.axis_size("expert")
    norm_gains = norm_work.astype(jnp.float32)
    inputs = tokens[0].astype(jnp.float32)
    first_norm, first_hat, first_inv = layer_norm(inputs, norm_gains[0], norm_gains[1])
    first_in = first_norm.astype(jnp.bfloat16)
    projected = jnp.einsum("td,jde->jte", first_in, in_work, preferred_element_type=jnp.float32)
    projected = projected.reshape(3, length, heads_here, HEAD_DIM)
    angles = rope_angles(positions[0])
    queries = (rotary(projected[0], angles, 1.0) * head_scale).astype(jnp.bfloat16)
    key_rows = rotary(projected[1], angles, 1.0).astype(jnp.bfloat16)
    value_rows = projected[2].astype(jnp.bfloat16)
    head_ids = lax.axis_index("tensor") * heads_here + jnp.arange(heads_here, dtype=jnp.int32)
    active = (head_ids < head_counts[0]).astype(jnp.float32)
    head_outs, log_totals, starts = attend_forward(
        queries, key_rows, value_rows, positions[0], block_rows
    )
    attended = (
        (head_outs * active[None, :, None])
        .astype(jnp.bfloat16)
        .reshape(length, heads_here * HEAD_DIM)
    )
    attn_part = jnp.dot(attended, out_work, preferred_element_type=jnp.float32)
    middle = inputs + lax.psum(attn_part, "tensor")
    second_norm, second_hat, second_inv = layer_norm(middle, norm_gains[2], norm_gains[3])
    second_in = second_norm.astype(jnp.bfloat16)
    bucket_ids = buckets[0]
    onehot = (bucket_ids[:, None] == jnp.arange(4, dtype=jnp.int32)[None, :]).astype(jnp.int32)
    bucket_rank = jnp.sum((jnp.cumsum(onehot, 0) - onehot) * onehot, 1)
    local_counts = jnp.sum(onehot, 0).astype(jnp.float32)
    bucket_share = lax.psum(local_counts, ("dp", "expert")) / (length * groups_data)
    most_rows = 5 * length // 16
    owner_group = max(experts // 4, 1)
    per_owner = max(4 // experts, 1)
    slot_rows = (most_rows + owner_group - 1) // owner_group
    capacity = per_owner * slot_rows
    slot_of = (
        (bucket_ids // per_owner * owner_group + bucket_rank % owner_group) * capacity
        + bucket_ids % per_owner * slot_rows
        + bucket_rank // owner_group
    )
    slot_total = experts * capacity
    source_rows = (
        jnp.full((slot_total,), length, jnp.int32)
        .at[slot_of]
        .set(jnp.arange(length, dtype=jnp.int32))
    )
    outgoing = gather_rows(second_in, source_rows).reshape(experts, capacity, model_width)
    incoming = lax.all_to_all(outgoing, "expert", split_axis=0, concat_axis=0, tiled=True).reshape(
        experts, per_owner, slot_rows, model_width
    )
    owner_index = lax.axis_index("expert")
    owned_ids = [owner_index // owner_group * per_owner + member for member in range(per_owner)]
    ffn_inputs = [
        incoming[:, member].reshape(experts * slot_rows, model_width) for member in range(per_owner)
    ]
    results = [
        ffn_forward(ffn_inputs[member], owned_ids[member], up_work, down_work)
        for member in range(per_owner)
    ]
    partial_value = jnp.stack(
        [
            results[member][0].reshape(experts, slot_rows, model_width)
            for member in range(per_owner)
        ],
        1,
    )
    summed = ffn_total(partial_value.reshape(experts, capacity, model_width)).astype(jnp.bfloat16)
    returned = lax.all_to_all(summed, "expert", split_axis=0, concat_axis=0, tiled=True)
    branch_out = returned.reshape(slot_total, model_width)[slot_of]
    output = middle + branch_out.astype(jnp.float32)
    grad_branch = cotangent[0]
    outgoing_grad = gather_rows(grad_branch, source_rows).reshape(experts, capacity, model_width)
    incoming_grad = lax.all_to_all(
        outgoing_grad, "expert", split_axis=0, concat_axis=0, tiled=True
    ).reshape(experts, per_owner, slot_rows, model_width)
    ffn_grads = [
        incoming_grad[:, member].reshape(experts * slot_rows, model_width)
        for member in range(per_owner)
    ]
    back_parts = [
        ffn_backward(
            ffn_inputs[member],
            ffn_grads[member],
            owned_ids[member],
            results[member][1],
            up_work,
            down_work,
        )
        for member in range(len(owned_ids))
    ]
    grad_up = back_parts[0][1]
    grad_down = back_parts[0][2]
    for member in range(1, len(owned_ids)):
        grad_up = grad_up + back_parts[member][1]
        grad_down = grad_down + back_parts[member][2]
    rows_back = jnp.stack(
        [
            back_parts[member][0].reshape(experts, slot_rows, model_width)
            for member in range(per_owner)
        ],
        1,
    )
    summed_back = ffn_grad_total(rows_back.reshape(experts, capacity, model_width)).astype(
        jnp.bfloat16
    )
    returned_back = lax.all_to_all(summed_back, "expert", split_axis=0, concat_axis=0, tiled=True)
    grad_second = returned_back.reshape(slot_total, model_width)[slot_of].astype(jnp.float32)
    grad_mid_norm, gain_second, shift_second = norm_back(
        grad_second, second_hat, second_inv, norm_gains[2]
    )
    grad_middle = grad_branch.astype(jnp.float32) + grad_mid_norm
    grad_attn = grad_middle.astype(jnp.bfloat16)
    grad_attended = jnp.einsum("td,ed->te", grad_attn, out_work, preferred_element_type=jnp.float32)
    grad_out_w = jnp.einsum("te,td->ed", attended, grad_attn, preferred_element_type=jnp.float32)
    grad_heads = (
        grad_attended.astype(jnp.bfloat16).reshape(length, heads_here, HEAD_DIM)
        * active.astype(jnp.bfloat16)[None, :, None]
    )
    grad_query, grad_keys, grad_values = attend_backward(
        queries, key_rows, value_rows, positions[0], grad_heads, log_totals, starts, block_rows
    )
    grad_projected = jnp.stack(
        [
            rotary(grad_query * head_scale, angles, -1.0),
            rotary(grad_keys, angles, -1.0),
            grad_values,
        ]
    )
    grad_projected = grad_projected.reshape(3, length, heads_here * HEAD_DIM).astype(jnp.bfloat16)
    grad_in_w = jnp.einsum(
        "td,jte->jde", first_in, grad_projected, preferred_element_type=jnp.float32
    )
    grad_first_part = jnp.einsum(
        "jte,jde->td", grad_projected, in_work, preferred_element_type=jnp.float32
    )
    grad_first = lax.psum(grad_first_part, "tensor")
    grad_input_norm, gain_first, shift_first = norm_back(
        grad_first, first_hat, first_inv, norm_gains[0]
    )
    input_grad = grad_middle + grad_input_norm
    grad_norm = jnp.stack([gain_first, shift_first, gain_second, shift_second])
    in_sum, out_sum, up_sum, down_sum, norm_sum = (
        lax.psum_scatter(grad_in_w, ("dp", "expert"), scatter_dimension=1, tiled=True),
        lax.psum_scatter(grad_out_w, ("dp", "expert"), scatter_dimension=1, tiled=True),
        lax.psum_scatter(grad_up, ("dp", "expert"), scatter_dimension=1, tiled=True),
        lax.psum_scatter(grad_down, ("dp", "expert"), scatter_dimension=2, tiled=True),
        lax.psum_scatter(grad_norm, ("dp", "expert"), scatter_dimension=1, tiled=True),
    )
    masters = (in_master, out_master, up_master, down_master, norm_master)
    firsts = (in_first, out_first, up_first, down_first, norm_first)
    seconds = (in_second, out_second, up_second, down_second, norm_second)
    grad_shards = (in_sum, out_sum, up_sum, down_sum, norm_sum)
    adam_out = [
        adam_terms(masters[member], grad_shards[member], firsts[member], seconds[member])
        for member in range(5)
    ]
    weight_sq = jnp.concatenate(
        [
            jnp.stack([jnp.sum(masters[member] * masters[member]) for member in range(4)]),
            jnp.sum(norm_master * norm_master, 1) / tensor_count,
        ]
    )
    update_sq = jnp.concatenate(
        [
            jnp.stack([jnp.sum(adam_out[member][0] * adam_out[member][0]) for member in range(4)]),
            jnp.sum(adam_out[4][0] * adam_out[4][0], 1) / tensor_count,
        ]
    )
    weight_tot, update_tot = lax.psum((weight_sq, update_sq), ("dp", "expert", "tensor"))
    weight_norms = jnp.sqrt(weight_tot)
    update_norms = jnp.sqrt(update_tot)
    ratios = weight_norms / update_norms
    new_weights = [
        masters[member] - LEARN_RATE * ratios[member] * adam_out[member][0] for member in range(4)
    ]
    norm_new = norm_master - LEARN_RATE * ratios[4:, None] * adam_out[4][0]
    lamb_norms = jnp.stack([weight_norms, update_norms])
    return (
        output[None],
        input_grad[None],
        bucket_share,
        lamb_norms,
        new_weights[0],
        new_weights[1],
        new_weights[2],
        new_weights[3],
        norm_new,
        adam_out[0][1],
        adam_out[1][1],
        adam_out[2][1],
        adam_out[3][1],
        adam_out[4][1],
        adam_out[0][2],
        adam_out[1][2],
        adam_out[2][2],
        adam_out[3][2],
        adam_out[4][2],
    )


def solution(mesh):
    placed = (
        P(("dp", "expert"), None, None),
        P(("dp", "expert"), None, None),
        P(("dp", "expert")),
        P(("dp", "expert"), None),
        P(("dp", "expert"), None),
        P(None, ("dp", "expert"), "tensor"),
        P("tensor", ("dp", "expert")),
        P(None, ("dp", "expert"), "tensor"),
        P(None, "tensor", ("dp", "expert")),
        P(None, ("dp", "expert")),
        P(None, ("dp", "expert"), "tensor"),
        P("tensor", ("dp", "expert")),
        P(None, ("dp", "expert"), "tensor"),
        P(None, "tensor", ("dp", "expert")),
        P(None, ("dp", "expert")),
        P(None, ("dp", "expert"), "tensor"),
        P("tensor", ("dp", "expert")),
        P(None, ("dp", "expert"), "tensor"),
        P(None, "tensor", ("dp", "expert")),
        P(None, ("dp", "expert")),
    )
    return jax.shard_map(
        body,
        mesh=mesh,
        in_specs=placed,
        out_specs=(
            P(("dp", "expert"), None, None),
            P(("dp", "expert"), None, None),
            P(),
            P(),
            P(None, ("dp", "expert"), "tensor"),
            P("tensor", ("dp", "expert")),
            P(None, ("dp", "expert"), "tensor"),
            P(None, "tensor", ("dp", "expert")),
            P(None, ("dp", "expert")),
            P(None, ("dp", "expert"), "tensor"),
            P("tensor", ("dp", "expert")),
            P(None, ("dp", "expert"), "tensor"),
            P(None, "tensor", ("dp", "expert")),
            P(None, ("dp", "expert")),
            P(None, ("dp", "expert"), "tensor"),
            P("tensor", ("dp", "expert")),
            P(None, ("dp", "expert"), "tensor"),
            P(None, "tensor", ("dp", "expert")),
            P(None, ("dp", "expert")),
        ),
        check_vma=False,
    )
```

profile of v0, /device:TPU:0, one launch (start us, length us, event | category | flops | bytes accessed | tf_op | source)
XLA Modules:
  0.0 1334.2 jit_solution(7979301927373560953)
XLA Ops:
  12.6 17.3 %all_gather.15 = bf16[4,2048]{1,0:T(4,128)(2,1)S(1)} all-gather(bf16[4,256]{1,0:T(4,128)(2,1)S(1)} %get-tuple-element.497), channel_id=1, replica_groups=mesh['dp'=4,'expert'=2,'tensor'=4] {'dp','expert'}, dimensions={1}, use_global_device_ids=true | all-gather | bytes 18432 | tf_op jit(solution)/shard_map/all_gather | solution.py:238
  33.2 26.4 %all-gather.5.cloned.1.call-done = bf16[3,2048,512]{2,1,0:T(8,128)(2,1)} async-done(((bf16[3,256,512]{2,1,0:T(8,128)(2,1)}), bf16[3,2048,512]{2,1,0:T(8,128)(2,1)}) %all-gather.5.cloned.1.call-update) | async-done | bytes 6291472 | tf_op jit(solution)/shard_map/all_gather | solution.py:234
  67.4 22.8 %all-gather.7.cloned.1.call-done = bf16[512,2048]{1,0:T(8,128)(2,1)} async-done(((bf16[512,256]{1,0:T(8,128)(2,1)}), bf16[512,2048]{1,0:T(8,128)(2,1)}) %all-gather.7.cloned.1.call-update) | async-done | bytes 2097168 | tf_op jit(solution)/shard_map/all_gather | solution.py:235
  110.0 70.5 %all-reduce.8.cloned.1.call-done = f32[256,2048]{1,0:T(8,128)} async-done(((f32[256,2048]{1,0:T(8,128)}), f32[256,2048]{1,0:T(8,128)}) %all-reduce.8.cloned.1.call-update) | async-done | bytes 2097168 | tf_op jit(solution)/shard_map/psum | solution.py:269
  191.6 26.8 %all-to-all-done = bf16[2,160,2048]{2,1,0:T(8,128)(2,1)} async-done(((bf16[2,160,2048]{2,1,0:T(8,128)(2,1)}), bf16[2,160,2048]{2,1,0:T(8,128)(2,1)}, u32[]{:S(2)}, u32[]{:S(2)}) %all-to-all-start) | async-done | bytes 1310752 | tf_op jit(solution)/shard_map/all_to_all | solution.py:294
  219.7 27.8 %all-gather.9.cloned.1.call-done = bf16[4,2048,512]{2,1,0:T(8,128)(2,1)} async-done(((bf16[4,256,512]{2,1,0:T(8,128)(2,1)}), bf16[4,2048,512]{2,1,0:T(8,128)(2,1)}) %all-gather.9.cloned.1.call-update) | async-done | bytes 8388624 | tf_op jit(solution)/shard_map/all_gather | solution.py:236
  247.5 58.4 %all-gather.11.cloned.1.call-done = bf16[4,512,2048]{2,1,0:T(8,128)(2,1)} async-done(((bf16[4,512,256]{2,1,0:T(8,128)(2,1)}), bf16[4,512,2048]{2,1,0:T(8,128)(2,1)}) %all-gather.11.cloned.1.call-update) | async-done | bytes 8388624 | tf_op jit(solution)/shard_map/all_gather | solution.py:237
  353.6 17.8 %conditional.28 = (f32[160,2048]{1,0:T(8,128)}, f32[1,512,2048]{2,1,0:T(8,128)}, f32[1,2048,512]{2,1,0:T(8,128)}) conditional(s32[]{:T(128)} %convert_element_type.236, () %tuple.190, (bf16[4,512,2048]{2,1,0:T(8,128)(2,1)}, bf16[160,2048]{1,0:T(8,128)(2,1)S(1)}, f32[160,512]{1,0:T(8,128)}, bf16[4,2048,512]{2,1,0:T(8,128)(2,1)}, ...), branch_computations={%region_36.37_spmd, %region_37.38_spmd} | conditional | flops 1342750720 | bytes 25395224 | solution.py:184
  371.4 17.9 %conditional.29 = (f32[160,2048]{1,0:T(8,128)}, f32[1,512,2048]{2,1,0:T(8,128)}, f32[1,2048,512]{2,1,0:T(8,128)}) conditional(s32[]{:T(128)} %convert_element_type.237, () %tuple.192, (bf16[4,512,2048]{2,1,0:T(8,128)(2,1)}, bf16[160,2048]{1,0:T(8,128)(2,1)S(1)}, f32[160,512]{1,0:T(8,128)}, bf16[4,2048,512]{2,1,0:T(8,128)(2,1)}, ...), branch_computations={%region_38.39_spmd, %region_39.40_spmd} | conditional | flops 1342750720 | bytes 25395224 | solution.py:184
  401.0 17.8 %conditional.24 = (f32[160,2048]{1,0:T(8,128)}, f32[1,512,2048]{2,1,0:T(8,128)}, f32[1,2048,512]{2,1,0:T(8,128)}) conditional(s32[]{:T(128)} %convert_element_type.227, () %tuple.182, (bf16[4,512,2048]{2,1,0:T(8,128)(2,1)}, bf16[160,2048]{1,0:T(8,128)(2,1)S(1)}, f32[160,512]{1,0:T(8,128)}, bf16[4,2048,512]{2,1,0:T(8,128)(2,1)}, ...), branch_computations={%region_28.29_spmd, %region_29.30_spmd} | conditional | flops 1342750720 | bytes 25395224 | solution.py:184
  433.5 183.2 %all-reduce.11 = (bf16[2,160,2048]{2,1,0:T(8,128)(2,1)}, bf16[2,160,2048]{2,1,0:T(8,128)(2,1)}) all-reduce(f32[2,160,2048]{2,1,0:T(8,128)S(1)} %bitcast.434, f32[2,160,2048]{2,1,0:T(8,128)} %bitcast.435), channel_id=1, replica_groups=mesh['dp'=4,'expert'=2,'tensor'=4] {'tensor'}, use_global_device_ids=true, to_apply=%region_27.28 | all-reduce | flops 1310720 | bytes 7864320 | tf_op jit(solution)/shard_map/psum | solution.py:192
  616.7 64.7 %all-to-all-start.3 = ((bf16[2,160,2048]{2,1,0:T(8,128)(2,1)}), bf16[2,160,2048]{2,1,0:T(8,128)(2,1)S(1)}, u32[]{:S(2)}, u32[]{:S(2)}) async-start(bf16[2,160,2048]{2,1,0:T(8,128)(2,1)} %get-tuple-element.448), calls=%async_computation.3 | async-start | bytes 2621440 | tf_op jit(solution)/shard_map/all_to_all | solution.py:352
  681.4 15.4 %all-to-all-done.3 = bf16[2,160,2048]{2,1,0:T(8,128)(2,1)S(1)} async-done(((bf16[2,160,2048]{2,1,0:T(8,128)(2,1)}), bf16[2,160,2048]{2,1,0:T(8,128)(2,1)S(1)}, u32[]{:S(2)}, u32[]{:S(2)}) %all-to-all-start.3) | async-done | bytes 1310752 | tf_op jit(solution)/shard_map/all_to_all | solution.py:352
  735.0 85.9 %all-reduce.10.cloned.1.call-done = f32[256,2048]{1,0:T(8,128)} async-done(((f32[256,2048]{1,0:T(8,128)}), f32[256,2048]{1,0:T(8,128)}) %all-reduce.10.cloned.1.call-update) | async-done | bytes 2097168 | tf_op jit(solution)/shard_map/psum | solution.py:382
  828.7 7.6 convolution_bitcast_fusion.16
  836.4 17.8 %maximum_add_fusion = f32[4,2048,512]{2,1,0:T(8,128)} fusion(f32[1,2048,512]{2,1,0:T(8,128)} %get-tuple-element.424, f32[1,2048,512]{2,1,0:T(8,128)} %get-tuple-element.423, f32[1,2048,512]{2,1,0:T(8,128)} %get-tuple-element.422, f32[1,2048,512]{2,1,0:T(8,128)} %get-tuple-element.421, f32[1,2048,512]{2,1,0:T(8,128)} %get-tuple-element.428, ...), kind=kLoop, calls=%fused_computation.189 | loop fusion | flops 29360128 | bytes 50331648 | tf_op jit(solution)/shard_map/add | solution.py:340
  854.2 17.4 %maximum_add_fusion.1 = f32[4,512,2048]{2,1,0:T(8,128)} fusion(f32[1,512,2048]{2,1,0:T(8,128)} %get-tuple-element.359, f32[1,512,2048]{2,1,0:T(8,128)} %get-tuple-element.358, f32[1,512,2048]{2,1,0:T(8,128)} %get-tuple-element.357, f32[1,512,2048]{2,1,0:T(8,128)} %get-tuple-element.356, f32[1,512,2048]{2,1,0:T(8,128)} %get-tuple-element.363, ...), kind=kLoop, calls=%fused_computation.190 | loop fusion | flops 29360128 | bytes 50331648 | tf_op jit(solution)/shard_map/add | solution.py:341
  872.3 13.7 %psum.53 = f32[4]{0:T(128)S(1)} all-reduce(f32[4]{0:T(128)S(1)} %convert_element_type.250), channel_id=1, replica_groups=mesh['dp'=4,'expert'=2,'tensor'=4] {'dp','expert'}, use_global_device_ids=true, to_apply=%region_52.53 | all-reduce | flops 4 | bytes 32 | tf_op jit(solution)/shard_map/psum | solution.py:276
  901.3 13.5 %reduce-scatter.10.cloned.1.call-done = f32[512,256]{1,0:T(8,128)} async-done(((f32[512,2048]{1,0:T(8,128)}), f32[512,256]{1,0:T(8,128)}) %reduce-scatter.10.cloned.1.call-update) | async-done | bytes 524304 | tf_op jit(solution)/shard_map/reduce_scatter | solution.py:390
  918.3 92.9 %reduce-scatter.8.cloned.1.call-done = f32[3,256,512]{1,2,0:T(8,128)} async-done(((f32[3,2048,512]{1,2,0:T(8,128)}), f32[3,256,512]{1,2,0:T(8,128)}) %reduce-scatter.8.cloned.1.call-update) | async-done | bytes 1572880 | tf_op jit(solution)/shard_map/reduce_scatter | solution.py:389
  1019.6 111.3 %reduce-scatter.12.cloned.1.call-done = f32[4,256,512]{2,1,0:T(8,128)} async-done(((f32[4,2048,512]{2,1,0:T(8,128)}), f32[4,256,512]{2,1,0:T(8,128)}) %reduce-scatter.12.cloned.1.call-update) | async-done | bytes 2097168 | tf_op jit(solution)/shard_map/reduce_scatter | solution.py:391
  1138.1 112.8 %reduce-scatter.14.cloned.1.call-done = f32[4,512,256]{2,1,0:T(8,128)} async-done(((f32[4,512,2048]{2,1,0:T(8,128)}), f32[4,512,256]{2,1,0:T(8,128)}) %reduce-scatter.14.cloned.1.call-update) | async-done | bytes 2097168 | tf_op jit(solution)/shard_map/reduce_scatter | solution.py:392
  1250.9 7.8 multiply_reduce_fusion.2
  1266.9 39.5 %all-reduce.2 = (f32[8]{0:T(128)S(1)}, f32[8]{0:T(128)S(1)}) all-reduce(f32[8]{0:T(128)S(1)} %concatenate.36, f32[8]{0:T(128)S(1)} %concatenate.35), channel_id=1, replica_groups=mesh['dp'=4,'expert'=2,'tensor'=4] {'dp','expert','tensor'}, use_global_device_ids=true, to_apply=%region_73.74 | all-reduce | flops 16 | bytes 128 | tf_op jit(solution)/shard_map/psum | solution.py:415
  (348 shorter events, 331.7 us)
Async XLA Ops:
  7.2 52.3 %all-gather.5.cloned.1.call-start = ((), (), s32[]{:S(2)}) async-start(), calls=%async_computation.9 | async-start | bytes 7077888 | tf_op jit(solution)/shard_map/all_gather | solution.py:234
  11.1 79.1 %all-gather.7.cloned.1.call-start = ((), (), s32[]{:S(2)}) async-start(), calls=%async_computation.10 | async-start | bytes 2359296 | tf_op jit(solution)/shard_map/all_gather | solution.py:235
  11.9 168.6 %all-reduce.8.cloned.1.call-start = ((), (), s32[]{:S(2)}) async-start(), calls=%async_computation.11 | async-start | bytes 4194304 | tf_op jit(solution)/shard_map/psum | solution.py:269
  93.9 153.6 %all-gather.9.cloned.1.call-start = ((), (), s32[]{:S(2)}) async-start(), calls=%async_computation.12 | async-start | bytes 9437184 | tf_op jit(solution)/shard_map/all_gather | solution.py:236
  96.6 209.4 %all-gather.11.cloned.1.call-start = ((), (), s32[]{:S(2)}) async-start(), calls=%async_computation.13 | async-start | bytes 9437184 | tf_op jit(solution)/shard_map/all_gather | solution.py:237
  106.4 80.4 %all-to-all-start.2 = ((bf16[2,160,2048]{2,1,0:T(8,128)(2,1)}), bf16[2,160,2048]{2,1,0:T(8,128)(2,1)S(1)}, u32[]{:S(2)}, u32[]{:S(2)}) async-start(bf16[2,160,2048]{2,1,0:T(8,128)(2,1)} %bitcast.85), calls=%async_computation.2 | async-start | bytes 2621440 | tf_op jit(solution)/shard_map/all_to_all | solution.py:319
  182.7 520.2 %copy-start.59 = (f32[256]{0:T(256)}, f32[256]{0:T(256)S(1)}, u32[]{:S(2)}) copy-start(f32[256]{0:T(256)S(1)} %add_rsqrt_fusion) | copy-start | bytes 3076
  186.8 31.5 %all-to-all-start = ((bf16[2,160,2048]{2,1,0:T(8,128)(2,1)}), bf16[2,160,2048]{2,1,0:T(8,128)(2,1)}, u32[]{:S(2)}, u32[]{:S(2)}) async-start(bf16[2,160,2048]{2,1,0:T(8,128)(2,1)} %bitcast.75), calls=%async_computation | async-start | bytes 2621440 | tf_op jit(solution)/shard_map/all_to_all | solution.py:294
  616.7 80.1 %all-to-all-start.3 = ((bf16[2,160,2048]{2,1,0:T(8,128)(2,1)}), bf16[2,160,2048]{2,1,0:T(8,128)(2,1)S(1)}, u32[]{:S(2)}, u32[]{:S(2)}) async-start(bf16[2,160,2048]{2,1,0:T(8,128)(2,1)} %get-tuple-element.448), calls=%async_computation.3 | async-start | bytes 2621440 | tf_op jit(solution)/shard_map/all_to_all | solution.py:352
  696.8 17.8 %all-to-all-start.1 = ((bf16[2,160,2048]{2,1,0:T(8,128)(2,1)}), bf16[2,160,2048]{2,1,0:T(8,128)(2,1)S(1)}, u32[]{:S(2)}, u32[]{:S(2)}) async-start(bf16[2,160,2048]{2,1,0:T(8,128)(2,1)} %get-tuple-element.447), calls=%async_computation.1 | async-start | bytes 2621440 | tf_op jit(solution)/shard_map/all_to_all | solution.py:314
  700.4 120.6 %all-reduce.10.cloned.1.call-start = ((), (), s32[]{:S(2)}) async-start(), calls=%async_computation.14 | async-start | bytes 4194304 | tf_op jit(solution)/shard_map/psum | solution.py:382
  734.9 86.0 %copy-start.61 = (f32[256]{0:T(256)S(1)}, f32[256]{0:T(256)}, u32[]{:S(2)}) copy-start(f32[256]{0:T(256)} %copy-done.60) | copy-start | bytes 3076
  735.0 88.6 %copy-start.55 = (f32[2048]{0:T(1024)S(1)}, f32[2048]{0:T(1024)}, u32[]{:S(2)}) copy-start(f32[2048]{0:T(1024)} %get-tuple-element.431) | copy-start | bytes 24580
  735.0 88.6 %copy-start.56 = (f32[2048]{0:T(1024)S(1)}, f32[2048]{0:T(1024)}, u32[]{:S(2)}) copy-start(f32[2048]{0:T(1024)} %get-tuple-element.440) | copy-start | bytes 24580
  735.0 90.0 %copy-start.5 = (f32[256,2048]{1,0:T(8,128)S(1)}, f32[256,2048]{1,0:T(8,128)}, u32[]{:S(2)}) copy-start(f32[256,2048]{1,0:T(8,128)} %copy-done.4) | copy-start | bytes 6291460
  735.0 90.0 %copy-start.34 = (bf16[256,512]{0,1:T(8,128)(2,1)S(1)}, bf16[256,512]{0,1:T(8,128)(2,1)}, u32[]{:S(2)}) copy-start(bf16[256,512]{0,1:T(8,128)(2,1)} %copy-done.33) | copy-start | bytes 786436
  735.0 164.4 %reduce-scatter.16.cloned.1.call-start = ((), (), s32[]{:S(2)}) async-start(), calls=%async_computation.19 | async-start | bytes 1179648
  825.0 89.8 %reduce-scatter.10.cloned.1.call-start = ((), (), s32[]{:S(2)}) async-start(), calls=%async_computation.16 | async-start | bytes 4718592 | tf_op jit(solution)/shard_map/reduce_scatter | solution.py:390
  827.7 183.4 %reduce-scatter.8.cloned.1.call-start = ((), (), s32[]{:S(2)}) async-start(), calls=%async_computation.15 | async-start | bytes 14155776 | tf_op jit(solution)/shard_map/reduce_scatter | solution.py:389
  836.3 294.7 %reduce-scatter.12.cloned.1.call-start = ((), (), s32[]{:S(2)}) async-start(), calls=%async_computation.17 | async-start | bytes 18874368 | tf_op jit(solution)/shard_map/reduce_scatter | solution.py:391
  854.1 396.8 %reduce-scatter.14.cloned.1.call-start = ((), (), s32[]{:S(2)}) async-start(), calls=%async_computation.18 | async-start | bytes 18874368 | tf_op jit(solution)/shard_map/reduce_scatter | solution.py:392
  899.4 111.7 %copy-start.11 = (f32[3,256,512]{1,2,0:T(8,128)S(1)}, f32[3,256,512]{1,2,0:T(8,128)}, u32[]{:S(2)}) copy-start(f32[3,256,512]{1,2,0:T(8,128)} %copy.157) | copy-start | bytes 4718596
  899.4 111.7 %copy-start.17 = (f32[3,256,512]{1,2,0:T(8,128)S(1)}, f32[3,256,512]{1,2,0:T(8,128)}, u32[]{:S(2)}) copy-start(f32[3,256,512]{1,2,0:T(8,128)} %copy.154) | copy-start | bytes 4718596
  1016.5 114.5 %copy-start.9 = (f32[4,256,512]{2,1,0:T(8,128)S(1)}, f32[4,256,512]{2,1,0:T(8,128)}, u32[]{:S(2)}) copy-start(f32[4,256,512]{2,1,0:T(8,128)} %param.59) | copy-start | bytes 6291460
  (61 other events, 579.3 us)
Sparse Core Ops, SparseCore 0:
  11.2 48.2 all-gather.4
  62.0 28.1 all-gather.6
  94.0 86.4 all-reduce.7
  182.9 64.5 all-gather.8
  250.0 55.9 all-gather.10
  735.1 85.8 all-reduce.9
  825.1 34.9 reduce-scatter.15
  863.5 51.2 reduce-scatter.9
  918.7 92.4 reduce-scatter.7
  1015.0 115.9 reduce-scatter.11
  1135.0 115.9 reduce-scatter.13
where the time goes:
time: 1350 us; the launch traced here: 1330 us
  waiting for transfers between devices  672 us (50%)
  blocking collectives  254 us (19%)
  other arithmetic  117 us (9%)
  local copies, waits for them, and re-layouts  115 us (9%)
  matrix products  80 us (6%)
  starting transfers between devices  77.4 us (6%)
  between operations  18.8 us (1%)
    psum x1, blocking collectives, ffn_total(): return lax.psum(partial_value, 'tensor')  183 us
    reduce_scatter x1, waiting for transfers between devices, body(): lax.psum_scatter(grad_down, ('dp', 'expert'), scatter_dimension=2, tiled=...  113 us
    reduce_scatter x1, waiting for transfers between devices, body(): lax.psum_scatter(grad_up, ('dp', 'expert'), scatter_dimension=1, tiled=True)  111 us
    reduce_scatter x1, waiting for transfers between devices, body(): lax.psum_scatter(grad_in_w, ('dp', 'expert'), scatter_dimension=1, tiled=...  92.9 us
    psum x1, waiting for transfers between devices, body(): grad_first = lax.psum(grad_first_part, 'tensor')  85.9 us
    psum x1, waiting for transfers between devices, body(): middle = inputs + lax.psum(attn_part, 'tensor')  70.5 us
    all_to_all x1, starting transfers between devices, body(): lax.all_to_all(summed_back, 'expert', split_axis=0, concat_axis=0, tiled=...  64.7 us
    all_gather x1, waiting for transfers between devices, body(): lax.all_gather(down_master.astype(jnp.bfloat16), ('dp', 'expert'), axis=2...  58.4 us
  transfers between devices with their start and end apart: 15, of which 13 were waited for; matrix products, arithmetic and copies ran while one was open for 9% of the time, Pallas kernels for 0%

commit v1 on v0

--- a/solution.py
+++ b/solution.py
@@ -1,6 +1,8 @@
 import jax
 import jax.numpy as jnp
 from jax import lax
+from jax.experimental import pallas as pl
+from jax.experimental.pallas import tpu as pltpu
 from jax.sharding import PartitionSpec as P
 
 HEAD_DIM = 128
@@ -25,7 +27,7 @@
     return (normed * gain_row + shift_row, normed, inv_std)
 
 
-def norm_back(grad_out, normed, inv_std, gain_row):
+def norm_back_rows(grad_out, normed, inv_std, gain_row):
     scaled = grad_out * gain_row
     inner_part = (
         scaled
@@ -206,6 +208,56 @@
         + WEIGHT_DECAY * weight
     )
     return (update, first_new, second_new)
+
+
+def finish(output, input_grad, bucket_share, masters, firsts, seconds, grad_shards, tensor_count):
+    norm_master = masters[4]
+    adam_out = [
+        adam_terms(masters[member], grad_shards[member], firsts[member], seconds[member])
+        for member in range(5)
+    ]
+    weight_sq = jnp.concatenate(
+        [
+            jnp.stack([jnp.sum(masters[member] * masters[member]) for member in range(4)]),
+            jnp.sum(norm_master * norm_master, 1) / tensor_count,
+        ]
+    )
+    update_sq = jnp.concatenate(
+        [
+            jnp.stack([jnp.sum(adam_out[member][0] * adam_out[member][0]) for member in range(4)]),
+            jnp.sum(adam_out[4][0] * adam_out[4][0], 1) / tensor_count,
+        ]
+    )
+    weight_tot, update_tot = lax.psum((weight_sq, update_sq), ("dp", "expert", "tensor"))
+    weight_norms = jnp.sqrt(weight_tot)
+    update_norms = jnp.sqrt(update_tot)
+    ratios = weight_norms / update_norms
+    new_weights = [
+        masters[member] - LEARN_RATE * ratios[member] * adam_out[member][0] for member in range(4)
+    ]
+    norm_new = norm_master - LEARN_RATE * ratios[4:, None] * adam_out[4][0]
+    lamb_norms = jnp.stack([weight_norms, update_norms])
+    return (
+        output[None],
+        input_grad[None],
+        bucket_share,
+        lamb_norms,
+        new_weights[0],
+        new_weights[1],
+        new_weights[2],
+        new_weights[3],
+        norm_new,
+        adam_out[0][1],
+        adam_out[1][1],
+        adam_out[2][1],
+        adam_out[3][1],
+        adam_out[4][1],
+        adam_out[0][2],
+        adam_out[1][2],
+        adam_out[2][2],
+        adam_out[3][2],
+        adam_out[4][2],
+    )
 
 
 def body(
@@ -351,7 +403,7 @@
     )
     returned_back = lax.all_to_all(summed_back, "expert", split_axis=0, concat_axis=0, tiled=True)
     grad_second = returned_back.reshape(slot_total, model_width)[slot_of].astype(jnp.float32)
-    grad_mid_norm, gain_second, shift_second = norm_back(
+    grad_mid_norm, gain_second, shift_second = norm_back_rows(
         grad_second, second_hat, second_inv, norm_gains[2]
     )
     grad_middle = grad_branch.astype(jnp.float32) + grad_mid_norm
@@ -380,7 +432,7 @@
         "jte,jde->td", grad_projected, in_work, preferred_element_type=jnp.float32
     )
     grad_first = lax.psum(grad_first_part, "tensor")
-    grad_input_norm, gain_first, shift_first = norm_back(
+    grad_input_norm, gain_first, shift_first = norm_back_rows(
         grad_first, first_hat, first_inv, norm_gains[0]
     )
     input_grad = grad_middle + grad_input_norm
@@ -396,51 +448,997 @@
     firsts = (in_first, out_first, up_first, down_first, norm_first)
     seconds = (in_second, out_second, up_second, down_second, norm_second)
     grad_shards = (in_sum, out_sum, up_sum, down_sum, norm_sum)
-    adam_out = [
-        adam_terms(masters[member], grad_shards[member], firsts[member], seconds[member])
-        for member in range(5)
+    return finish(output, input_grad, bucket_share, masters, firsts, seconds, grad_shards, tensor_count)
+
+
+MESH = pl.DeviceIdType.MESH
+ANY = pl.BlockSpec(memory_space=pl.ANY)
+VM = pl.BlockSpec(memory_space=pltpu.VMEM)
+F32 = jnp.float32
+BF16 = jnp.bfloat16
+SUM_ONE = BF16
+SUM_TWO = BF16
+SUM_FFN = BF16
+SUM_THREE = BF16
+CHUNK = 256
+HALF = 128
+ROWS = 64
+
+
+class Here:
+    def __init__(self):
+        d = lax.axis_index("dp")
+        self.x, self.c = d // 2, lax.rem(d, 2)
+        self.y = lax.axis_index("expert")
+        self.z = lax.axis_index("tensor")
+
+    def plane(self, dx, dc, dy):
+        x = 1 - self.x if dx else self.x
+        c = 1 - self.c if dc else self.c
+        y = 1 - self.y if dy else self.y
+        return (x * 2 + c, y, self.z)
+
+    def chunk(self, dx, dc, dy):
+        x = 1 - self.x if dx else self.x
+        c = 1 - self.c if dc else self.c
+        y = 1 - self.y if dy else self.y
+        return (x * 2 + c) * 2 + y
+
+    def chunk_of(self, dx, dy, core):
+        x = 1 - self.x if dx else self.x
+        y = 1 - self.y if dy else self.y
+        return (x * 2 + core) * 2 + y
+
+    def along(self, step):
+        return (self.x * 2 + self.c, self.y, lax.rem(self.z + step, 4))
+
+    def behind(self, step):
+        return lax.rem(self.z + 4 - step, 4)
+
+
+PARTNER = (0, 1, 0)
+PLANE = [(a, b, g) for a in (0, 1) for b in (0, 1) for g in (0, 1) if a + b + g > 0]
+SIDES = [(1, 0, 0), (1, 1, 0), (0, 0, 1), (0, 1, 1)]
+
+
+def greet(here, plane_peers, tensor_peers):
+    barrier = pltpu.get_barrier_semaphore()
+    for peer in plane_peers:
+        pl.semaphore_signal(barrier, inc=1, device_id=here.plane(*peer), device_id_type=MESH)
+    for step in tensor_peers:
+        pl.semaphore_signal(barrier, inc=1, device_id=here.along(step), device_id_type=MESH)
+    pl.semaphore_wait(barrier, len(plane_peers) + len(tensor_peers))
+
+
+def push(src, dst, send, recv, device):
+    copy = pltpu.make_async_remote_copy(
+        src_ref=src, dst_ref=dst, send_sem=send, recv_sem=recv, device_id=device, device_id_type=MESH
+    )
+    copy.start()
+    return copy
+
+
+def block(index, size):
+    return pl.ds(pl.multiple_of(index * size, size), size)
+
+
+def rows_chunk(ref, k):
+    return ref.at[:, block(k, CHUNK), :]
+
+
+def rows_part(ref, k, part):
+    return ref.at[:, pl.ds(pl.multiple_of(k * CHUNK + part * HALF, HALF), HALF), :]
+
+
+def cols_chunk(ref, k):
+    return ref.at[:, :, block(k, CHUNK)]
+
+
+def cols_part(ref, k, part):
+    return ref.at[:, part * HALF : part * HALF + HALF, block(k, CHUNK)]
+
+
+class Gather:
+    def __init__(self, here, by_rows, shard, whole, first, relay, local):
+        self.here, self.by_rows, self.shard, self.whole = here, by_rows, shard, whole
+        self.first, self.relay, self.local = first, relay, local
+        self.copies = []
+
+    def half(self, core):
+        if self.by_rows:
+            return self.shard.at[:, :, block(core, CHUNK)]
+        return self.shard.at[:, block(core, CHUNK), :]
+
+    def chunk(self, k):
+        return rows_chunk(self.whole, k) if self.by_rows else cols_chunk(self.whole, k)
+
+    def part(self, k, part):
+        return rows_part(self.whole, k, part) if self.by_rows else cols_part(self.whole, k, part)
+
+    def start(self):
+        here = self.here
+        mine = self.chunk(here.chunk(0, 0, 0))
+        for index, side in enumerate(SIDES + [PARTNER]):
+            core = 1 - here.c if side[1] else here.c
+            self.copies.append(
+                push(
+                    self.half(core),
+                    mine,
+                    self.first.at[0, index],
+                    self.first.at[1, index],
+                    here.plane(*side),
+                )
+            )
+        self.own = pltpu.make_async_copy(self.half(here.c), mine, self.local)
+        self.own.start()
+
+    def forward(self):
+        here = self.here
+        self.onward = []
+        for index in range(4):
+            side = SIDES[index]
+            self.copies[index].wait_recv()
+            part = 0 if side[0] else 1
+            where = self.part(here.chunk(*side), part)
+            target = (0, 0, 1) if side[0] else (1, 0, 0)
+            self.onward.append(
+                push(
+                    where,
+                    where,
+                    self.relay.at[0, index],
+                    self.relay.at[1, index],
+                    here.plane(*target),
+                )
+            )
+
+    def finish(self):
+        for index in range(4):
+            self.copies[index].wait_send()
+        self.copies[4].wait()
+        self.own.wait()
+        for copy in self.onward:
+            copy.wait()
+
+
+def gather_sems():
+    return [
+        pltpu.SemaphoreType.DMA((2, 5)),
+        pltpu.SemaphoreType.DMA((2, 4)),
+        pltpu.SemaphoreType.DMA,
     ]
-    weight_sq = jnp.concatenate(
+
+
+class Scatter:
+    def __init__(self, here, by_rows, grad, total, bufs):
+        self.here, self.by_rows, self.grad, self.total = here, by_rows, grad, total
+        (self.own, self.got, self.got_two, self.final) = bufs[:4]
+        (self.load_sem, self.one_sem, self.two_sem, self.last_sem, self.local) = bufs[4:]
+
+    def part(self, k, part):
+        return rows_part(self.grad, k, part) if self.by_rows else cols_part(self.grad, k, part)
+
+    def start(self):
+        here = self.here
+        self.first = []
+        for side in (0, 1):
+            near, far = ((1, 0), (1, 1)) if side == 0 else ((0, 1), (1, 1))
+            target = here.plane(1, 0, 0) if side == 0 else here.plane(0, 0, 1)
+            for slot in range(4):
+                chip = far if slot >= 2 else near
+                src = self.part(here.chunk_of(chip[0], chip[1], slot % 2), side)
+                index = side * 4 + slot
+                self.first.append(
+                    push(
+                        src,
+                        self.got.at[index],
+                        self.one_sem.at[0, index],
+                        self.one_sem.at[1, index],
+                        target,
+                    )
+                )
+        self.loads = []
+        for side in (0, 1):
+            for slot in range(4):
+                chip = (0, 0) if slot < 2 else ((0, 1) if side == 0 else (1, 0))
+                src = self.part(here.chunk_of(chip[0], chip[1], slot % 2), side)
+                index = side * 4 + slot
+                copy = pltpu.make_async_copy(src, self.own.at[index], self.load_sem.at[index])
+                copy.start()
+                self.loads.append(copy)
+
+    def middle(self):
+        here = self.here
+        self.second = []
+        for side in (0, 1):
+            target = here.plane(0, 0, 1) if side == 0 else here.plane(1, 0, 0)
+            for slot in (2, 3):
+                index = side * 4 + slot
+                self.loads[index].wait()
+                self.first[index].wait_recv()
+                self.own[index] = (
+                    self.own[index].astype(F32) + self.got[index].astype(F32)
+                ).astype(BF16)
+                two = side * 2 + slot - 2
+                self.second.append(
+                    push(
+                        self.own.at[index],
+                        self.got_two.at[two],
+                        self.two_sem.at[0, two],
+                        self.two_sem.at[1, two],
+                        target,
+                    )
+                )
+
+    def last(self):
+        here = self.here
+        for side in (0, 1):
+            for slot in (0, 1):
+                index = side * 4 + slot
+                two = side * 2 + slot
+                self.loads[index].wait()
+                self.first[index].wait_recv()
+                self.second[two].wait_recv()
+                self.final[slot, :, side * HALF : side * HALF + HALF, :] = (
+                    self.own[index].astype(F32) + self.got[index].astype(F32)
+                ) + self.got_two[two].astype(F32)
+        if self.by_rows:
+            where = self.total.at[:, :, block(here.c, CHUNK)]
+        else:
+            where = self.total.at[:, block(here.c, CHUNK), :]
+        self.keep = pltpu.make_async_copy(self.final.at[here.c], where, self.local)
+        self.keep.start()
+        self.give = push(
+            self.final.at[1 - here.c],
+            where,
+            self.last_sem.at[0],
+            self.last_sem.at[1],
+            here.plane(*PARTNER),
+        )
+
+    def finish(self):
+        for copy in self.first:
+            copy.wait_send()
+        for copy in self.second:
+            copy.wait_send()
+        self.keep.wait()
+        self.give.wait()
+
+
+def scatter_scratch(width):
+    return [
+        pltpu.VMEM((8, width, HALF, CHUNK), BF16),
+        pltpu.VMEM((8, width, HALF, CHUNK), BF16),
+        pltpu.VMEM((4, width, HALF, CHUNK), BF16),
+        pltpu.VMEM((2, width, CHUNK, CHUNK), F32),
+        pltpu.SemaphoreType.DMA((8,)),
+        pltpu.SemaphoreType.DMA((2, 8)),
+        pltpu.SemaphoreType.DMA((2, 4)),
+        pltpu.SemaphoreType.DMA((2,)),
+        pltpu.SemaphoreType.DMA,
+    ]
+
+
+SCATTER = 9
+
+
+class TensorSum:
+    def __init__(self, here, part, bufs):
+        self.here, self.part = here, part
+        self.pair, self.out, self.inn, self.pair_sem, self.sem = bufs
+
+    def start(self):
+        here = self.here
+        self.swap = push(
+            self.part.at[1 - here.c],
+            self.pair,
+            self.pair_sem.at[0],
+            self.pair_sem.at[1],
+            here.plane(*PARTNER),
+        )
+
+    def spread(self):
+        here = self.here
+        self.swap.wait_recv()
+        self.sent = []
+        for step in (2, 1, 3):
+            rows = block(lax.rem(here.z + step, 4), ROWS)
+            self.out[step - 1] = (
+                self.part[here.c, rows, :].astype(F32) + self.pair[rows, :].astype(F32)
+            ).astype(self.out.dtype)
+            self.sent.append(
+                push(
+                    self.out.at[step - 1],
+                    self.inn.at[step - 1],
+                    self.sem.at[0, step - 1],
+                    self.sem.at[1, step - 1],
+                    here.along(step),
+                )
+            )
+
+    def result(self):
+        here = self.here
+        rows = block(here.z, ROWS)
+        total = self.part[here.c, rows, :].astype(F32) + self.pair[rows, :].astype(F32)
+        for copy in self.sent:
+            copy.wait_recv()
+        for step in (1, 2, 3):
+            total = total + self.inn[step - 1].astype(F32)
+        return total
+
+    def finish(self):
+        self.swap.wait_send()
+        for copy in self.sent:
+            copy.wait_send()
+
+
+def sum_scratch(length, width, kind):
+    return [
+        pltpu.VMEM((length, width), kind),
+        pltpu.VMEM((3, ROWS, width), kind),
+        pltpu.VMEM((3, ROWS, width), kind),
+        pltpu.SemaphoreType.DMA((2,)),
+        pltpu.SemaphoreType.DMA((2, 3)),
+    ]
+
+
+class TensorGather:
+    def __init__(self, here, mine, whole, sem, pair_sem, local):
+        self.here, self.mine, self.whole = here, mine, whole
+        self.sem, self.pair_sem, self.local = sem, pair_sem, local
+
+    def start(self):
+        here = self.here
+        place = self.whole.at[here.c, block(here.z, ROWS), :]
+        self.sent = []
+        for step in (2, 1, 3):
+            self.sent.append(
+                push(
+                    self.mine,
+                    place,
+                    self.sem.at[0, step - 1],
+                    self.sem.at[1, step - 1],
+                    here.along(step),
+                )
+            )
+        self.shared = [
+            push(
+                self.mine,
+                place,
+                self.pair_sem.at[0, 0],
+                self.pair_sem.at[1, 0],
+                here.plane(*PARTNER),
+            )
+        ]
+        self.own = pltpu.make_async_copy(self.mine, place, self.local)
+        self.own.start()
+
+    def forward(self):
+        here = self.here
+        for index, step in enumerate((2, 1, 3)):
+            self.sent[index].wait_recv()
+            place = self.whole.at[here.c, block(here.behind(step), ROWS), :]
+            self.shared.append(
+                push(
+                    place,
+                    place,
+                    self.pair_sem.at[0, step],
+                    self.pair_sem.at[1, step],
+                    here.plane(*PARTNER),
+                )
+            )
+
+    def finish(self):
+        for copy in self.sent:
+            copy.wait_send()
+        for copy in self.shared:
+            copy.wait()
+        self.own.wait()
+
+
+def normed(values):
+    center = values - jnp.mean(values, -1, keepdims=True)
+    variance = jnp.mean(center * center, -1, keepdims=True)
+    inv_std = lax.rsqrt(variance + NORM_EPS)
+    return (center * inv_std, inv_std)
+
+
+def norm_row(packs, row):
+    return jnp.concatenate([packs[k, row : row + 1, :] for k in range(8)], 1)
+
+
+def params(ident, limit=60):
+    return pltpu.CompilerParams(
+        collective_id=ident, has_side_effects=True, vmem_limit_bytes=limit << 20
+    )
+
+
+def first_kernel(
+    tok, cot, table, pack, wq, wo,
+    n1, both_cot, tables, packs, wq_all, wo_all,
+    n1_own, small, pair, local, q0, q1, q2, o0, o1, o2,
+):
+    here = Here()
+    greet(here, PLANE, ())
+    me = here.chunk(0, 0, 0)
+    packed = []
+    for index, peer in enumerate(PLANE):
+        packed.append(
+            push(pack, packs.at[me], small.at[0, index], small.at[1, index], here.plane(*peer))
+        )
+    packs[pl.ds(me, 1)] = pack[...][None]
+    gather_q = Gather(here, True, wq, wq_all, q0, q1, q2)
+    gather_o = Gather(here, False, wo, wo_all, o0, o1, o2)
+    gather_q.start()
+    gather_o.start()
+    partner = here.plane(*PARTNER)
+    shared = [
+        push(table, tables.at[here.c], pair.at[0, 0], pair.at[1, 0], partner),
+        push(cot, both_cot.at[here.c], pair.at[0, 1], pair.at[1, 1], partner),
+    ]
+    kept = [
+        pltpu.make_async_copy(table, tables.at[here.c], local.at[0]),
+        pltpu.make_async_copy(cot, both_cot.at[here.c], local.at[1]),
+    ]
+    for copy in kept:
+        copy.start()
+    for copy in packed:
+        copy.wait()
+    gain, shift = norm_row(packs, 0), norm_row(packs, 1)
+
+    def rows_step(i, carry):
+        rows = block(i, 32)
+        hat, _ = normed(tok[rows, :].astype(F32))
+        n1_own[rows, :] = (hat * gain + shift).astype(BF16)
+        return carry
+
+    lax.fori_loop(0, tok.shape[0] // 32, rows_step, 0)
+    shared.append(push(n1_own, n1.at[here.c], pair.at[0, 2], pair.at[1, 2], partner))
+    kept.append(pltpu.make_async_copy(n1_own, n1.at[here.c], local.at[2]))
+    kept[2].start()
+    gather_q.forward()
+    gather_o.forward()
+    gather_q.finish()
+    gather_o.finish()
+    for copy in kept:
+        copy.wait()
+    for copy in shared:
+        copy.wait()
+
+
+def first_call(tok, cot, table, pack, wq, wo):
+    length, width = tok.shape
+    return pl.pallas_call(
+        first_kernel,
+        out_shape=(
+            jax.ShapeDtypeStruct((2, length, width), BF16),
+            jax.ShapeDtypeStruct((2, length, width), BF16),
+            jax.ShapeDtypeStruct((2,) + table.shape, F32),
+            jax.ShapeDtypeStruct((8,) + pack.shape, F32),
+            jax.ShapeDtypeStruct((wq.shape[0], width, CHUNK), BF16),
+            jax.ShapeDtypeStruct((1, CHUNK, width), BF16),
+        ),
+        in_specs=[VM, ANY, ANY, VM, ANY, ANY],
+        out_specs=(ANY, ANY, ANY, VM, ANY, ANY),
+        scratch_shapes=[
+            pltpu.VMEM((length, width), BF16),
+            pltpu.SemaphoreType.DMA((2, 7)),
+            pltpu.SemaphoreType.DMA((2, 3)),
+            pltpu.SemaphoreType.DMA((3,)),
+        ]
+        + gather_sems()
+        + gather_sems(),
+        compiler_params=params(1),
+        name="gather_attention",
+    )(tok, cot, table, pack, wq, wo)
+
+
+def second_kernel(
+    part, tok, packs, wu, wd,
+    n2, mid, wu_all, wd_all,
+    n2_own, s0, s1, s2, s3, s4, tg, tgp, tgl, u0, u1, u2, d0, d1, d2,
+):
+    here = Here()
+    greet(here, SIDES + [PARTNER], (1, 2, 3))
+    total = TensorSum(here, part, (s0, s1, s2, s3, s4))
+    total.start()
+    gather_u = Gather(here, True, wu, wu_all, u0, u1, u2)
+    gather_d = Gather(here, False, wd, wd_all, d0, d1, d2)
+    gather_u.start()
+    gather_d.start()
+    total.spread()
+    middle = tok[...].astype(F32) + total.result()
+    mid[...] = middle
+    hat, _ = normed(middle)
+    n2_own[...] = (hat * norm_row(packs, 2) + norm_row(packs, 3)).astype(BF16)
+    gather = TensorGather(here, n2_own, n2, tg, tgp, tgl)
+    gather.start()
+    gather.forward()
+    gather_u.forward()
+    gather_d.forward()
+    total.finish()
+    gather.finish()
+    gather_u.finish()
+    gather_d.finish()
+
+
+def tensor_gather_sems():
+    return [
+        pltpu.SemaphoreType.DMA((2, 3)),
+        pltpu.SemaphoreType.DMA((2, 4)),
+        pltpu.SemaphoreType.DMA,
+    ]
+
+
+def second_call(part, tok, packs, wu, wd):
+    _, length, width = part.shape
+    return pl.pallas_call(
+        second_kernel,
+        out_shape=(
+            jax.ShapeDtypeStruct((2, length, width), BF16),
+            jax.ShapeDtypeStruct((ROWS, width), F32),
+            jax.ShapeDtypeStruct((wu.shape[0], width, CHUNK), BF16),
+            jax.ShapeDtypeStruct((wd.shape[0], CHUNK, width), BF16),
+        ),
+        in_specs=[VM, VM, VM, ANY, ANY],
+        out_specs=(ANY, VM, ANY, ANY),
+        scratch_shapes=[pltpu.VMEM((ROWS, width), BF16)]
+        + sum_scratch(length, width, part.dtype)
+        + tensor_gather_sems()
+        + gather_sems()
+        + gather_sems(),
+        compiler_params=params(2),
+        name="gather_ffn",
+    )(part, tok, packs, wu, wd)
+
+
+def norm_back(grad_out, hat, inv_std, gain):
+    scaled = grad_out * gain
+    inner = (
+        scaled
+        - jnp.mean(scaled, -1, keepdims=True)
+        - hat * jnp.mean(scaled * hat, -1, keepdims=True)
+    )
+    return (
+        inner * inv_std,
+        jnp.sum(grad_out * hat, 0, keepdims=True),
+        jnp.sum(grad_out, 0, keepdims=True),
+    )
+
+
+def third_kernel(
+    dn2, ffn, mid, cot, packs, gu, gd,
+    gm, dmid, out_own, sums, up_sum, down_sum,
+    gm_own, *rest,
+):
+    here = Here()
+    greet(here, [(1, 0, 0), (0, 0, 1), PARTNER], (1, 2, 3))
+    back = TensorSum(here, dn2, rest[0:5])
+    branch = TensorSum(here, ffn, rest[5:10])
+    scatter_u = Scatter(here, True, gu, up_sum, rest[13 : 13 + SCATTER])
+    scatter_d = Scatter(here, False, gd, down_sum, rest[13 + SCATTER : 13 + 2 * SCATTER])
+    back.start()
+    branch.start()
+    scatter_u.start()
+    scatter_d.start()
+    back.spread()
+    branch.spread()
+    grad_n2 = back.result().astype(BF16).astype(F32)
+    middle = mid[...]
+    hat, inv_std = normed(middle)
+    grad_mid, gain_sum, shift_sum = norm_back(grad_n2, hat, inv_std, norm_row(packs, 2))
+    grad_mid = cot[...].astype(F32) + grad_mid
+    dmid[...] = grad_mid
+    gm_own[...] = grad_mid.astype(BF16)
+    gather = TensorGather(here, gm_own, gm, *rest[10:13])
+    gather.start()
+    sums[0:1, :] = gain_sum
+    sums[1:2, :] = shift_sum
+    scatter_u.middle()
+    scatter_d.middle()
+    out_own[...] = (mid[...] + branch.result().astype(BF16).astype(F32)).astype(BF16)
+    gather.forward()
+    scatter_u.last()
+    scatter_d.last()
+    back.finish()
+    branch.finish()
+    gather.finish()
+    scatter_u.finish()
+    scatter_d.finish()
+
+
+def third_call(dn2, ffn, mid, cot, packs, gu, gd):
+    _, length, width = dn2.shape
+    return pl.pallas_call(
+        third_kernel,
+        out_shape=(
+            jax.ShapeDtypeStruct((2, length, width), BF16),
+            jax.ShapeDtypeStruct((ROWS, width), F32),
+            jax.ShapeDtypeStruct((ROWS, width), BF16),
+            jax.ShapeDtypeStruct((2, width), F32),
+            jax.ShapeDtypeStruct((gu.shape[0], CHUNK, 2 * CHUNK), F32),
+            jax.ShapeDtypeStruct((gd.shape[0], 2 * CHUNK, CHUNK), F32),
+        ),
+        in_specs=[VM, VM, VM, VM, VM, ANY, ANY],
+        out_specs=(ANY, VM, VM, VM, ANY, ANY),
+        scratch_shapes=[pltpu.VMEM((ROWS, width), BF16)]
+        + sum_scratch(length, width, dn2.dtype)
+        + sum_scratch(length, width, ffn.dtype)
+        + tensor_gather_sems()
+        + scatter_scratch(gu.shape[0])
+        + scatter_scratch(gd.shape[0]),
+        compiler_params=params(3),
+        name="scatter_ffn",
+    )(dn2, ffn, mid, cot, packs, gu, gd)
+
+
+def fourth_kernel(
+    dn1, tok, dmid, out_own, sums, packs, gq, go,
+    output, igrad, norm_total, q_sum, o_sum,
+    ig_own, out_all, ig_all, slices, heard, plane_sum, heard_z, og, ig, ns, nz, *rest,
+):
+    here = Here()
+    greet(here, PLANE, (1, 2, 3))
+    back = TensorSum(here, dn1, rest[0:5])
+    scatter_q = Scatter(here, True, gq, q_sum, rest[5 : 5 + SCATTER])
+    scatter_o = Scatter(here, False, go, o_sum, rest[5 + SCATTER : 5 + 2 * SCATTER])
+    back.start()
+    scatter_q.start()
+    scatter_o.start()
+    back.spread()
+    copies = []
+
+    def spread_rows(mine, whole, sem):
+        made = []
+        for step in (2, 1, 3):
+            made.append(
+                push(
+                    mine,
+                    whole.at[block(here.z, ROWS), :],
+                    sem.at[0, step - 1],
+                    sem.at[1, step - 1],
+                    here.along(step),
+                )
+            )
+        return made
+
+    copies += spread_rows(out_own, out_all, og)
+    grad_n1 = back.result()
+    hat, inv_std = normed(tok[...].astype(F32))
+    grad_in, gain_sum, shift_sum = norm_back(grad_n1, hat, inv_std, norm_row(packs, 0))
+    ig_own[...] = (dmid[...] + grad_in).astype(BF16)
+    copies += spread_rows(ig_own, ig_all, ig)
+    for k in range(8):
+        cols = slice(k * CHUNK, (k + 1) * CHUNK)
+        slices[k, 0:1, :] = gain_sum[:, cols]
+        slices[k, 1:2, :] = shift_sum[:, cols]
+        slices[k, 2:4, :] = sums[:, cols]
+        slices[k, 4:8, :] = jnp.zeros((4, CHUNK), F32)
+    norm_copies = []
+    for index, peer in enumerate(PLANE):
+        norm_copies.append(
+            push(
+                slices.at[here.chunk(*peer)],
+                heard.at[index],
+                ns.at[0, index],
+                ns.at[1, index],
+                here.plane(*peer),
+            )
+        )
+    scatter_q.middle()
+    scatter_o.middle()
+    mine = slices[here.chunk(0, 0, 0)]
+    for index in range(7):
+        norm_copies[index].wait()
+        mine = mine + heard[index]
+    plane_sum[...] = mine
+    z_copies = []
+    for step in (1, 2, 3):
+        z_copies.append(
+            push(
+                plane_sum,
+                heard_z.at[here.z],
+                nz.at[0, step - 1],
+                nz.at[1, step - 1],
+                here.along(step),
+            )
+        )
+    heard_z[pl.ds(here.z, 1)] = mine[None]
+    scatter_q.last()
+    scatter_o.last()
+    for copy in z_copies:
+        copy.wait()
+    norm_total[...] = ((heard_z[0] + heard_z[1]) + heard_z[2]) + heard_z[3]
+    for copy in copies:
+        copy.wait()
+    out_all[block(here.z, ROWS), :] = out_own[...]
+    ig_all[block(here.z, ROWS), :] = ig_own[...]
+    output[...] = out_all[...].astype(F32)
+    igrad[...] = ig_all[...].astype(F32)
+    back.finish()
+    scatter_q.finish()
+    scatter_o.finish()
+
+
+def fourth_call(dn1, tok, dmid, out_own, sums, packs, gq, go):
+    _, length, width = dn1.shape
+    return pl.pallas_call(
+        fourth_kernel,
+        out_shape=(
+            jax.ShapeDtypeStruct((length, width), F32),
+            jax.ShapeDtypeStruct((length, width), F32),
+            jax.ShapeDtypeStruct((8, CHUNK), F32),
+            jax.ShapeDtypeStruct((gq.shape[0], CHUNK, 2 * CHUNK), F32),
+            jax.ShapeDtypeStruct((1, 2 * CHUNK, CHUNK), F32),
+        ),
+        in_specs=[VM] * 6 + [ANY, ANY],
+        out_specs=(VM, VM, VM, ANY, ANY),
+        scratch_shapes=[
+            pltpu.VMEM((ROWS, width), BF16),
+            pltpu.VMEM((length, width), BF16),
+            pltpu.VMEM((length, width), BF16),
+            pltpu.VMEM((8, 8, CHUNK), F32),
+            pltpu.VMEM((7, 8, CHUNK), F32),
+            pltpu.VMEM((8, CHUNK), F32),
+            pltpu.VMEM((4, 8, CHUNK), F32),
+            pltpu.SemaphoreType.DMA((2, 3)),
+            pltpu.SemaphoreType.DMA((2, 3)),
+            pltpu.SemaphoreType.DMA((2, 7)),
+            pltpu.SemaphoreType.DMA((2, 3)),
+        ]
+        + sum_scratch(length, width, dn1.dtype)
+        + scatter_scratch(gq.shape[0])
+        + scatter_scratch(1),
+        compiler_params=params(4),
+        name="scatter_attention",
+    )(dn1, tok, dmid, out_own, sums, packs, gq, go)
+
+
+def turn(values, cosine, sine):
+    return values * cosine + pltpu.roll(values, HEAD_DIM // 2, 1) * sine
+
+
+def dot(left, right, dims=((1,), (0,))):
+    return lax.dot_general(left, right, (dims, ((), ())), preferred_element_type=F32)
+
+
+def attention_weights(queries, key_rows, lowest):
+    scores = dot(queries, key_rows, ((1,), (1,)))
+    row = lax.broadcasted_iota(jnp.int32, scores.shape, 0)
+    col = lax.broadcasted_iota(jnp.int32, scores.shape, 1)
+    allowed = (col <= row) & (col.astype(F32) >= lowest)
+    scores = jnp.where(allowed, scores, MASKED)
+    exp_scores = jnp.exp(scores - jnp.max(scores, -1, keepdims=True))
+    return exp_scores / jnp.sum(exp_scores, -1, keepdims=True)
+
+
+def attend_kernel(head0, n1, wq, wo, tables, q_out, k_out, v_out, a_out, part):
+    length = tables.shape[2]
+    rows_in = n1[...]
+    projected = [dot(rows_in, wq[j]) for j in range(3)]
+    for s in range(2):
+        rows = slice(s * length, (s + 1) * length)
+        cosine, sine = tables[s, 0], tables[s, 1]
+        lowest = tables[s, 2, :, 0:1]
+        for h in range(2):
+            cols = slice(h * HEAD_DIM, (h + 1) * HEAD_DIM)
+            queries = (turn(projected[0][rows, cols], cosine, sine) * HEAD_DIM ** (-0.5)).astype(BF16)
+            key_rows = turn(projected[1][rows, cols], cosine, sine).astype(BF16)
+            value_rows = projected[2][rows, cols].astype(BF16)
+            weights = attention_weights(queries, key_rows, lowest).astype(BF16)
+            heads = dot(weights, value_rows)
+            active = tables[s, 4] > (head0[0] + h).astype(F32)
+            q_out[rows, cols] = queries
+            k_out[rows, cols] = key_rows
+            v_out[rows, cols] = value_rows
+            a_out[rows, cols] = jnp.where(active, heads, 0.0).astype(BF16)
+    for s in range(2):
+        rows = slice(s * length, (s + 1) * length)
+        part[s] = dot(a_out[rows, :], wo[0]).astype(part.dtype)
+
+
+SM = pl.BlockSpec(memory_space=pltpu.SMEM)
+
+
+def local_params():
+    return pltpu.CompilerParams(vmem_limit_bytes=60 << 20)
+
+
+def attend_call(head0, n1, wq, wo, tables):
+    _, length, width = n1.shape
+    thin = jax.ShapeDtypeStruct((2 * length, CHUNK), BF16)
+    return pl.pallas_call(
+        attend_kernel,
+        out_shape=(thin, thin, thin, thin, jax.ShapeDtypeStruct((2, length, width), SUM_ONE)),
+        in_specs=[SM, VM, VM, VM, VM],
+        out_specs=(VM,) * 5,
+        compiler_params=local_params(),
+        name="attend",
+    )(head0, n1.reshape(2 * length, width), wq, wo, tables)
+
+
+def ffn_kernel(n2, cot, bucket, wu, wd, dn2, ffn, gu, gd, back_sum, ffn_sum):
+    quarter = pl.program_id(0)
+
+    @pl.when(quarter == 0)
+    def _():
+        back_sum[...] = jnp.zeros_like(back_sum)
+        ffn_sum[...] = jnp.zeros_like(ffn_sum)
+
+    rows_in = n2[...]
+    grads_in = cot[...]
+    hidden = dot(rows_in, wu[0])
+    live = bucket[:, 0:1] >= quarter.astype(F32)
+    rectified = jnp.maximum(jnp.where(live, hidden, 0.0), 0.0)
+    squared = (rectified * rectified).astype(BF16)
+    grad_square = dot(grads_in, wd[0], ((1,), (1,)))
+    grad_hidden = (grad_square * 2.0 * rectified).astype(BF16)
+    ffn_sum[...] += dot(squared, wd[0])
+    back_sum[...] += dot(grad_hidden, wu[0], ((1,), (1,)))
+    gu[0] = dot(rows_in, grad_hidden, ((0,), (0,))).astype(BF16)
+    gd[0] = dot(squared, grads_in, ((0,), (0,))).astype(BF16)
+
+    @pl.when(quarter == 3)
+    def _():
+        dn2[...] = back_sum[...].astype(dn2.dtype)
+        ffn[...] = ffn_sum[...].astype(ffn.dtype)
+
+
+def ffn_call(n2, cot, bucket, wu, wd):
+    _, length, width = n2.shape
+    total = 2 * length
+    whole = lambda shape: pl.BlockSpec(shape, lambda r: (0,) * len(shape))
+    per = lambda shape: pl.BlockSpec((1,) + shape, lambda r: (r, 0, 0))
+    dn2, ffn, gu, gd = pl.pallas_call(
+        ffn_kernel,
+        grid=(4,),
+        out_shape=(
+            jax.ShapeDtypeStruct((total, width), SUM_TWO),
+            jax.ShapeDtypeStruct((total, width), SUM_FFN),
+            jax.ShapeDtypeStruct((4, width, CHUNK), BF16),
+            jax.ShapeDtypeStruct((4, CHUNK, width), BF16),
+        ),
+        in_specs=[
+            whole((total, width)),
+            whole((total, width)),
+            whole((total, HALF)),
+            per((width, CHUNK)),
+            per((CHUNK, width)),
+        ],
+        out_specs=(
+            whole((total, width)),
+            whole((total, width)),
+            per((width, CHUNK)),
+            per((CHUNK, width)),
+        ),
+        scratch_shapes=[pltpu.VMEM((total, width), F32), pltpu.VMEM((total, width), F32)],
+        compiler_params=local_params(),
+        name="ffn",
+    )(n2.reshape(total, width), cot.reshape(total, width), bucket, wu, wd)
+    return dn2.reshape(2, length, width), ffn.reshape(2, length, width), gu, gd
+
+
+def attend_back_kernel(
+    head0, gm, n1, a_rows, q_rows, k_rows, v_rows, wq, wo, tables,
+    dn1, gq, go, dp,
+):
+    length = tables.shape[2]
+    grads = gm[...]
+    go[0] = dot(a_rows[...], grads, ((0,), (0,))).astype(BF16)
+    grad_att = dot(grads, wo[0], ((1,), (1,))).astype(BF16)
+    for s in range(2):
+        rows = slice(s * length, (s + 1) * length)
+        cosine, sine = tables[s, 0], tables[s, 1]
+        lowest = tables[s, 2, :, 0:1]
+        for h in range(2):
+            cols = slice(h * HEAD_DIM, (h + 1) * HEAD_DIM)
+            active = tables[s, 4] > (head0[0] + h).astype(F32)
+            grad_heads = jnp.where(active, grad_att[rows, cols].astype(F32), 0.0).astype(BF16)
+            queries, key_rows, value_rows = q_rows[rows, cols], k_rows[rows, cols], v_rows[rows, cols]
+            weights = attention_weights(queries, key_rows, lowest)
+            grad_weights = dot(grad_heads, value_rows, ((1,), (1,)))
+            inner = jnp.sum(weights * grad_weights, -1, keepdims=True)
+            grad_scores = (weights * (grad_weights - inner)).astype(BF16)
+            grad_query = dot(grad_scores, key_rows) * HEAD_DIM ** (-0.5)
+            grad_keys = dot(grad_scores, queries, ((0,), (0,)))
+            grad_values = dot(weights.astype(BF16), grad_heads, ((0,), (0,)))
+            dp[0, rows, cols] = turn(grad_query, cosine, -sine).astype(BF16)
+            dp[1, rows, cols] = turn(grad_keys, cosine, -sine).astype(BF16)
+            dp[2, rows, cols] = grad_values.astype(BF16)
+    for s in range(2):
+        rows = slice(s * length, (s + 1) * length)
+        total = dot(dp[0, rows, :], wq[0], ((1,), (1,)))
+        total = total + dot(dp[1, rows, :], wq[1], ((1,), (1,)))
+        total = total + dot(dp[2, rows, :], wq[2], ((1,), (1,)))
+        dn1[s] = total.astype(dn1.dtype)
+    rows_in = n1[...]
+    for j in range(3):
+        gq[j] = dot(rows_in, dp[j], ((0,), (0,))).astype(BF16)
+
+
+def attend_back_call(head0, gm, n1, a_rows, q_rows, k_rows, v_rows, wq, wo, tables):
+    _, length, width = n1.shape
+    return pl.pallas_call(
+        attend_back_kernel,
+        out_shape=(
+            jax.ShapeDtypeStruct((2, length, width), SUM_THREE),
+            jax.ShapeDtypeStruct((3, width, CHUNK), BF16),
+            jax.ShapeDtypeStruct((1, CHUNK, width), BF16),
+        ),
+        in_specs=[SM] + [VM] * 9,
+        out_specs=(VM,) * 3,
+        scratch_shapes=[pltpu.VMEM((3, 2 * length, CHUNK), BF16)],
+        compiler_params=local_params(),
+        name="attend_back",
+    )(
+        head0, gm.reshape(2 * length, width), n1.reshape(2 * length, width),
+        a_rows, q_rows, k_rows, v_rows, wq, wo, tables,
+    )
+
+
+def make_table(positions, buckets, head_count):
+    length = positions.shape[0]
+    angles = rope_angles(positions)
+    cosine, sine = jnp.cos(angles), jnp.sin(angles)
+    lowest = (jnp.arange(length, dtype=jnp.int32) - positions).astype(F32)
+    wide = lambda column: jnp.broadcast_to(column, (length, HALF))
+    return jnp.stack(
         [
-            jnp.stack([jnp.sum(masters[member] * masters[member]) for member in range(4)]),
-            jnp.sum(norm_master * norm_master, 1) / tensor_count,
+            jnp.concatenate([cosine, cosine], 1),
+            jnp.concatenate([-sine, sine], 1),
+            wide(lowest[:, None]),
+            wide(buckets.astype(F32)[:, None]),
+            wide(head_count.astype(F32)),
         ]
     )
-    update_sq = jnp.concatenate(
+
+
+def fast_body(
+    tokens, cotangent, head_counts, positions, buckets,
+    in_master, out_master, up_master, down_master, norm_master,
+    in_first, out_first, up_first, down_first, norm_first,
+    in_second, out_second, up_second, down_second, norm_second,
+):
+    length = tokens.shape[1]
+    groups_data = lax.axis_size("dp") * lax.axis_size("expert")
+    tensor_count = lax.axis_size("tensor")
+    tok, cot = tokens[0], cotangent[0]
+    table = make_table(positions[0], buckets[0], head_counts)
+    onehot = (buckets[0][:, None] == jnp.arange(CHUNK, dtype=jnp.int32)[None, :]).astype(F32)
+    pack = jnp.concatenate(
         [
-            jnp.stack([jnp.sum(adam_out[member][0] * adam_out[member][0]) for member in range(4)]),
-            jnp.sum(adam_out[4][0] * adam_out[4][0], 1) / tensor_count,
-        ]
-    )
-    weight_tot, update_tot = lax.psum((weight_sq, update_sq), ("dp", "expert", "tensor"))
-    weight_norms = jnp.sqrt(weight_tot)
-    update_norms = jnp.sqrt(update_tot)
-    ratios = weight_norms / update_norms
-    new_weights = [
-        masters[member] - LEARN_RATE * ratios[member] * adam_out[member][0] for member in range(4)
-    ]
-    norm_new = norm_master - LEARN_RATE * ratios[4:, None] * adam_out[4][0]
-    lamb_norms = jnp.stack([weight_norms, update_norms])
-    return (
-        output[None],
-        input_grad[None],
-        bucket_share,
-        lamb_norms,
-        new_weights[0],
-        new_weights[1],
-        new_weights[2],
-        new_weights[3],
-        norm_new,
-        adam_out[0][1],
-        adam_out[1][1],
-        adam_out[2][1],
-        adam_out[3][1],
-        adam_out[4][1],
-        adam_out[0][2],
-        adam_out[1][2],
-        adam_out[2][2],
-        adam_out[3][2],
-        adam_out[4][2],
+            lax.reduce_precision(norm_master, 8, 7),
+            jnp.sum(onehot, 0, keepdims=True),
+            jnp.zeros((3, CHUNK), F32),
+        ],
+        0,
+    )
+    n1, both_cot, tables, packs, wq, wo = first_call(
+        tok, cot, table, pack, in_master.astype(BF16), out_master.astype(BF16)[None]
+    )
+    bucket_share = jnp.sum(packs[:, 4, :4], 0) / (length * groups_data)
+    heads_here = 2 * CHUNK // HEAD_DIM
+    core = lax.rem(lax.axis_index("dp"), 2)
+    head0 = (lax.axis_index("tensor") * heads_here + core * (heads_here // 2))[None].astype(jnp.int32)
+    q_rows, k_rows, v_rows, a_rows, part = attend_call(head0, n1, wq, wo, tables)
+    place = lax.axis_index("tensor") * ROWS
+    tok_own = lax.dynamic_slice_in_dim(tok, place, ROWS, 0)
+    cot_own = lax.dynamic_slice_in_dim(cot, place, ROWS, 0)
+    n2, mid, wu, wd = second_call(
+        part, tok_own, packs, up_master.astype(BF16), down_master.astype(BF16)
+    )
+    bucket = tables[:, 3].reshape(2 * length, HALF)
+    dn2, ffn, gu, gd = ffn_call(n2, both_cot, bucket, wu, wd)
+    gm, dmid, out_own, sums, up_sum, down_sum = third_call(dn2, ffn, mid, cot_own, packs, gu, gd)
+    dn1, gq, go = attend_back_call(head0, gm, n1, a_rows, q_rows, k_rows, v_rows, wq, wo, tables)
+    output, input_grad, norm_sum, in_sum, out_sum = fourth_call(
+        dn1, tok_own, dmid, out_own, sums, packs, gq, go
+    )
+    masters = (in_master, out_master, up_master, down_master, norm_master)
+    firsts = (in_first, out_first, up_first, down_first, norm_first)
+    seconds = (in_second, out_second, up_second, down_second, norm_second)
+    grad_shards = (in_sum, out_sum[0], up_sum, down_sum, norm_sum[:4])
+    return finish(
+        output, input_grad, bucket_share, masters, firsts, seconds, grad_shards, tensor_count
     )
 
 
@@ -467,8 +1465,10 @@
         P(None, "tensor", ("dp", "expert")),
         P(None, ("dp", "expert")),
     )
+    shape = dict(mesh.shape)
+    fits = shape == {"dp": 4, "expert": 2, "tensor": 4}
     return jax.shard_map(
-        body,
+        fast_body if fits else body,
         mesh=mesh,
         in_specs=placed,
         out_specs=(

time: 1350 us -> 463 us (0.34); the launches traced: 1330 us -> 462 us
  waiting for transfers between devices: 672 us -> 0 us
  Pallas kernels: 0 us -> 363 us
  blocking collectives: 254 us -> 38.3 us
  local copies, waits for them, and re-layouts: 115 us -> 13.7 us
  matrix products: 80 us -> 0 us
  starting transfers between devices: 77.4 us -> 0 us
  other arithmetic: 117 us -> 42.7 us
  between operations: 18.8 us -> 4.42 us
    pallas_call x0 -> x7, Pallas kernels: none -> 363 us  [the longest x1 83.5 us: fourth_call(): pl.pallas_call(fourth_kernel, out_shape=(jax.ShapeDtypeStruct((length, wi...]
    reduce_scatter x4 -> x0, waiting for transfers between devices: 331 us -> none  [the longest x1 113 us: body(): lax.psum_scatter(grad_down, ('dp', 'expert'), scatter_dimension=2, tiled=...]
    psum x3 -> x1, blocking collectives: 236 us -> 38.3 us  [finish(): lax.psum((weight_sq, update_sq), ('dp', 'expert', 'tensor'))]
    psum x2 -> x0, waiting for transfers between devices: 156 us -> none  [the longest x1 85.9 us: body(): grad_first = lax.psum(grad_first_part, 'tensor')]
    all_gather x4 -> x0, waiting for transfers between devices: 135 us -> none  [the longest x1 58.4 us: body(): lax.all_gather(down_master.astype(jnp.bfloat16), ('dp', 'expert'), axis=2...]
    dot_general x30 -> x0, matrix products: 80 us -> none  [the longest x3 11.3 us: live_part(): jnp.einsum('ru,rd->ud', squared, grads_in, preferred_element_type=jnp.flo...]
    all_to_all x4 -> x0, starting transfers between devices: 76.5 us -> none  [the longest x1 64.7 us: body(): lax.all_to_all(summed_back, 'expert', split_axis=0, concat_axis=0, tiled=...]
    all_to_all x4 -> x0, waiting for transfers between devices: 49.1 us -> none  [the longest x1 26.8 us: body(): lax.all_to_all(outgoing, 'expert', split_axis=0, concat_axis=0, tiled=True)]
  transfers between devices with their start and end apart: 15 -> 0, of which waited for: 13 -> 0; matrix products, arithmetic and copies ran while one was open for 9% -> 0% of each run, Pallas kernels for 0% -> 0%
where the time goes in v1:
time: 463 us; the launch traced here: 462 us
  Pallas kernels  363 us (78%)
  other arithmetic  42.7 us (9%)
  blocking collectives  38.3 us (8%)
  local copies, waits for them, and re-layouts  13.7 us (3%)
    pallas_call x1, Pallas kernels, fourth_call(): pl.pallas_call(fourth_kernel, out_shape=(jax.ShapeDtypeStruct((length, wi...  83.5 us
    pallas_call x1, Pallas kernels, second_call(): pl.pallas_call(second_kernel, out_shape=(jax.ShapeDtypeStruct((2, length,...  81.5 us
    pallas_call x1, Pallas kernels, third_call(): pl.pallas_call(third_kernel, out_shape=(jax.ShapeDtypeStruct((2, length,...  80.5 us
    pallas_call x1, Pallas kernels, first_call(): pl.pallas_call(first_kernel, out_shape=(jax.ShapeDtypeStruct((2, length,...  74.9 us
    psum x1, blocking collectives, finish(): lax.psum((weight_sq, update_sq), ('dp', 'expert', 'tensor'))  38.3 us
    pallas_call x1, Pallas kernels, ffn_call(): pl.pallas_call(ffn_kernel, grid=(4,), out_shape=(jax.ShapeDtypeStruct((to...  20.5 us
    reduce_sum x4, other arithmetic, finish(): jnp.sum(masters[member] * masters[member])  17.1 us
    pallas_call x1, Pallas kernels, attend_back_call(): pl.pallas_call(attend_back_kernel, out_shape=(jax.ShapeDtypeStruct((2, le...  13.5 us

profile of v1, /device:TPU:0, one launch (start us, length us, event | category | flops | bytes accessed | tf_op | source)
XLA Modules:
  0.0 462.5 jit_solution(16803569919490248056)
XLA Ops:
  6.8 2.4 convert_element_type.39.wq
  9.9 74.9 %gather_attention.1 = (bf16[2,256,2048]{2,1,0:T(8,128)(2,1)}, bf16[2,256,2048]{2,1,0:T(8,128)(2,1)}, f32[2,5,256,128]{3,2,1,0:T(8,128)}, f32[8,8,256]{2,1,0:T(8,...) custom-call(bf16[256,2048]{1,0:T(8,128)(2,1)} %bitcast.62, bf16[256,2048]{1,0:T(8,128)(2,1)} %bitcast.63, ...), custom_call_target="tpu_custom_call" | custom-call | tf_op jit(solution)/shard_map/gather_attention/pallas_call | solution.py:910
  84.9 9.0 %attend.1 = (bf16[512,256]{1,0:T(8,128)(2,1)}, bf16[512,256]{1,0:T(8,128)(2,1)}, bf16[512,256]{1,0:T(8,128)(2,1)}, bf16[512,256]{1,0:T(8,128)(2,1)}, bf16[2,256,2048]{2,1,0:T(8,128)(2,1)}) custom-call(s32[1]{0:T(128)} %bitcast.head0, bf16[512,2048]{1,0:T(8,128)(2,1)} %bitcast.53, bf16[3,2048,256]{2,1,0:T(8,128)(2,1)} %get-tuple-element.53.wq, ...), custom_call_target="tpu_custom_call" | custom-call | tf_op jit(solution)/shard_map/attend/pallas_call | solution.py:1249
  93.8 2.0 dynamic-slice_bitcast_fusion
  95.8 2.7 convert_element_type.41.wu
  99.6 81.5 %gather_ffn.1 = (bf16[2,256,2048]{2,1,0:T(8,128)(2,1)}, f32[64,2048]{1,0:T(8,128)}, bf16[4,2048,256]{2,1,0:T(8,128)(2,1)}, bf16[4,256,2048]{2,1,0:T(8,128)(2,1)}) custom-call(bf16[2,256,2048]{2,1,0:T(8,128)(2,1)} %get-tuple-element.56.part, bf16[64,2048]{1,0:T(8,128)(2,1)} %get-tuple-element.120.tok, f32[8,8,256]{2,1,0:T(8,128)} %get-tuple-element.57.packs, ...), custom_call_target="tpu_custom_call" | custom-call | tf_op jit(solution)/shard_map/gather_ffn/pallas_call | solution.py:974
  181.1 1.7 slice.24
  182.8 20.5 %ffn.1 = (bf16[512,2048]{1,0:T(8,128)(2,1)}, bf16[512,2048]{1,0:T(8,128)(2,1)}, bf16[4,2048,256]{2,1,0:T(8,128)(2,1)}, bf16[4,256,2048]{2,1,0:T(8,128)(2,1)}) custom-call(bf16[512,2048]{1,0:T(8,128)(2,1)} %bitcast.58, bf16[512,2048]{1,0:T(8,128)(2,1)} %bitcast.55, f32[512,128]{1,0:T(8,128)} %bitcast.64, bf16[4,2048,256]{2,1,0:T(8,128)(2,1)} %get-tuple-element.60.wu, ...), custom_call_target="tpu_custom_call" | custom-call | tf_op jit(solution)/shard_map/ffn/pallas_call | solution.py:1291
  203.3 80.5 %scatter_ffn.1 = (bf16[2,256,2048]{2,1,0:T(8,128)(2,1)}, f32[64,2048]{1,0:T(8,128)}, bf16[64,2048]{1,0:T(8,128)(2,1)}, f32[2,2048]{1,0:T(2,128)}, f32[4,256,512]{2,1,0:T(8,128)}, /*index=5*/f32[4,512,256]{2,1,0:T(8,128)}) custom-call(bf16[2,256,2048]{2,1,0:T(8,128)(2,1)} %bitcast.56, bf16[2,256,2048]{2,1,0:T(8,128)(2,1)} %bitcast.57, ...), custom_call_target="tpu_custom_call" | custom-call | tf_op jit(solution)/shard_map/scatter_ffn/pallas_call | solution.py:1051
  283.8 13.5 %attend_back.1 = (bf16[2,256,2048]{2,1,0:T(8,128)(2,1)}, bf16[3,2048,256]{2,1,0:T(8,128)(2,1)}, bf16[1,256,2048]{2,1,0:T(8,128)(2,1)}) custom-call(s32[1]{0:T(128)} %bitcast.head0, bf16[512,2048]{1,0:T(8,128)(2,1)} %bitcast.61, bf16[512,2048]{1,0:T(8,128)(2,1)} %bitcast.54, bf16[512,256]{1,0:T(8,128)(2,1)} %get-tuple-element.68.a_rows, ...), custom_call_target="tpu_custom_call" | custom-call | tf_op jit(solution)/shard_map/attend_back/pallas_call | solution.py:1360
  297.3 83.5 %scatter_attention.1 = (f32[256,2048]{1,0:T(8,128)}, f32[256,2048]{1,0:T(8,128)}, f32[8,256]{1,0:T(8,128)}, f32[3,256,512]{2,1,0:T(8,128)}, f32[1,512,256]{2,1,0:T(8,128)}) custom-call(bf16[2,256,2048]{2,1,0:T(8,128)(2,1)} %get-tuple-element.72.dn1, bf16[64,2048]{1,0:T(8,128)(2,1)} %get-tuple-element.120.tok, f32[64,2048]{1,0:T(8,128)} %get-tuple-element.73.dmid, ...), custom_call_target="tpu_custom_call" | custom-call | tf_op jit(solution)/shard_map/scatter_attention/pallas_call | solution.py:1164
  380.8 6.7 %multiply_reduce_fusion.5 = (f32[]{:T(128)}, f32[]{:T(128)}, f32[3,256,512]{2,1,0:T(8,128)}, f32[3,256,512]{2,1,0:T(8,128)}) fusion(f32[3,256,512]{2,1,0:T(8,128)} %param.25, f32[3,256,512]{2,1,0:T(8,128)} %get-tuple-element.80, f32[3,256,512]{2,1,0:T(8,128)} %param.30, f32[3,256,512]{2,1,0:T(8,128)} %param.35), kind=kLoop, calls=%fused_computation.20 | loop fusion | flops 6684670 | bytes 9437192 | tf_op jit(solution)/shard_map/reduce_sum | solution.py:221
  387.6 1.8 multiply_reduce_fusion.7
  389.4 4.3 multiply_reduce_fusion.3
  393.8 4.3 multiply_reduce_fusion.2
  398.1 2.7 concatenate.18
  401.5 2.7 concatenate.19
  404.2 38.3 %all-reduce = (f32[8]{0:T(128)S(1)}, f32[8]{0:T(128)S(1)}) all-reduce(f32[8]{0:T(128)S(1)} %concatenate.19, f32[8]{0:T(128)S(1)} %concatenate.18), channel_id=1, replica_groups=mesh['dp'=4,'expert'=2,'tensor'=4] {'dp','expert','tensor'}, use_global_device_ids=true, to_apply=%region_13.0 | all-reduce | flops 16 | bytes 128 | tf_op jit(solution)/shard_map/psum | solution.py:231
  444.5 4.8 %multiply_subtract_fusion = f32[4,512,256]{2,1,0:T(8,128)} fusion(f32[4,512,256]{2,1,0:T(8,128)S(1)} %copy-done, f32[]{:T(128)} %bitcast.35, f32[4,512,256]{2,1,0:T(8,128)} %get-tuple-element.157, f32[4,512,256]{2,1,0:T(8,128)} %get-tuple-element.152), kind=kLoop, calls=%fused_computation.5 | loop fusion | flops 4194304 | bytes 8388612 | tf_op jit(solution)/shard_map/sub | solution.py:236
  450.0 2.4 multiply_subtract_fusion.1
  453.2 1.1 multiply_subtract_fusion.3
  455.0 2.0 multiply_subtract_fusion.2
  458.8 1.3 copy.46
  461.2 1.3 copy.47
  (81 shorter events, 12.3 us)
Async XLA Ops:
  0.7 8.6 %copy-start.8 = (f32[512,256]{1,0:T(8,128)S(1)}, f32[512,256]{1,0:T(8,128)}, u32[]{:S(2)}) copy-start(f32[512,256]{1,0:T(8,128)} %param.26) | copy-start | bytes 1572868
  4.4 5.5 %copy-start.19 = (f32[5,256,128]{2,1,0:T(8,128)}, f32[5,256,128]{2,1,0:T(8,128)S(1)}, u32[]{:S(2)}) copy-start(f32[5,256,128]{2,1,0:T(8,128)S(1)} %broadcast_dynamic-update-slice_fusion.table) | copy-start | bytes 1966084
  93.8 4.7 %copy-start = (f32[4,512,256]{2,1,0:T(8,128)S(1)}, f32[4,512,256]{2,1,0:T(8,128)}, u32[]{:S(2)}) copy-start(f32[4,512,256]{2,1,0:T(8,128)} %param.28) | copy-start | bytes 6291460
  380.8 6.8 %copy-start.20 = (f32[512,256]{1,0:T(8,128)S(1)}, f32[512,256]{1,0:T(8,128)}, u32[]{:S(2)}) copy-start(f32[512,256]{1,0:T(8,128)} %param.31) | copy-start | bytes 1572868
  380.8 6.8 %copy-start.21 = (f32[512,256]{1,0:T(8,128)S(1)}, f32[512,256]{1,0:T(8,128)}, u32[]{:S(2)}) copy-start(f32[512,256]{1,0:T(8,128)} %param.36) | copy-start | bytes 1572868
  380.8 6.8 %copy-start.22 = (f32[1,512,256]{2,1,0:T(8,128)S(1)}, f32[1,512,256]{2,1,0:T(8,128)}, u32[]{:S(2)}) copy-start(f32[1,512,256]{2,1,0:T(8,128)} %get-tuple-element.81) | copy-start | bytes 1572868
  380.8 8.6 %copy-start.9 = (f32[4,256,512]{2,1,0:T(8,128)S(1)}, f32[4,256,512]{2,1,0:T(8,128)}, u32[]{:S(2)}) copy-start(f32[4,256,512]{2,1,0:T(8,128)} %param.32) | copy-start | bytes 6291460
  380.8 8.6 %copy-start.10 = (f32[4,256,512]{2,1,0:T(8,128)S(1)}, f32[4,256,512]{2,1,0:T(8,128)}, u32[]{:S(2)}) copy-start(f32[4,256,512]{2,1,0:T(8,128)} %param.37) | copy-start | bytes 6291460
  380.8 8.6 %copy-start.14 = (f32[4,256,512]{2,1,0:T(8,128)S(1)}, f32[4,256,512]{2,1,0:T(8,128)}, u32[]{:S(2)}) copy-start(f32[4,256,512]{2,1,0:T(8,128)} %get-tuple-element.82) | copy-start | bytes 6291460
  389.4 63.8 %copy-start.17 = (f32[512,256]{1,0:T(8,128)}, f32[512,256]{1,0:T(8,128)S(1)}, u32[]{:S(2)}) copy-start(f32[512,256]{1,0:T(8,128)S(1)} %get-tuple-element.150) | copy-start | bytes 1572868
  389.4 4.3 copy-start.11
  389.4 4.3 copy-start.12
  389.4 4.3 copy-start.13
  393.7 7.0 %copy-start.23 = (f32[4,256]{1,0:T(4,128)S(1)}, f32[4,256]{1,0:T(4,128)}, u32[]{:S(2)}) copy-start(f32[4,256]{1,0:T(4,128)} %param.29) | copy-start | bytes 12292
  393.7 7.0 %copy-start.24 = (f32[4,256]{1,0:T(4,128)S(1)}, f32[4,256]{1,0:T(4,128)}, u32[]{:S(2)}) copy-start(f32[4,256]{1,0:T(4,128)} %param.34) | copy-start | bytes 12292
  393.8 7.0 %copy-start.25 = (f32[4,256]{1,0:T(4,128)S(1)}, f32[4,256]{1,0:T(4,128)}, u32[]{:S(2)}) copy-start(f32[4,256]{1,0:T(4,128)} %param.39) | copy-start | bytes 12292
  393.8 7.0 %copy-start.26 = (f32[8,256]{1,0:T(8,128)S(1)}, f32[8,256]{1,0:T(8,128)}, u32[]{:S(2)}) copy-start(f32[8,256]{1,0:T(8,128)} %get-tuple-element.84) | copy-start | bytes 24580
  444.5 5.5 %copy-start.2 = (f32[4,256,512]{2,1,0:T(8,128)S(1)}, f32[4,256,512]{2,1,0:T(8,128)}, u32[]{:S(2)}) copy-start(f32[4,256,512]{2,1,0:T(8,128)} %param.27) | copy-start | bytes 6291460
  444.5 5.5 %copy-start.4 = (f32[4,256,512]{2,1,0:T(8,128)S(1)}, f32[4,256,512]{2,1,0:T(8,128)}, u32[]{:S(2)}) copy-start(f32[4,256,512]{2,1,0:T(8,128)} %get-tuple-element.151) | copy-start | bytes 6291460
  444.5 5.5 %copy-start.5 = (f32[4,256,512]{2,1,0:T(8,128)S(1)}, f32[4,256,512]{2,1,0:T(8,128)}, u32[]{:S(2)}) copy-start(f32[4,256,512]{2,1,0:T(8,128)} %get-tuple-element.156) | copy-start | bytes 6291460
  450.0 3.2 copy-start.18
  450.0 5.0 %copy-start.6 = (f32[3,256,512]{2,1,0:T(8,128)S(1)}, f32[3,256,512]{2,1,0:T(8,128)}, u32[]{:S(2)}) copy-start(f32[3,256,512]{2,1,0:T(8,128)} %get-tuple-element.149) | copy-start | bytes 4718596
  450.0 5.0 %copy-start.7 = (f32[3,256,512]{2,1,0:T(8,128)S(1)}, f32[3,256,512]{2,1,0:T(8,128)}, u32[]{:S(2)}) copy-start(f32[3,256,512]{2,1,0:T(8,128)} %get-tuple-element.154) | copy-start | bytes 4718596
  455.0 3.8 copy-start.16
  (3 other events, 6.7 us)

commit v2 on v1

--- a/solution.py
+++ b/solution.py
@@ -1,3 +1,5 @@
+import math
+
 import jax
 import jax.numpy as jnp
 from jax import lax
@@ -454,12 +456,9 @@
 MESH = pl.DeviceIdType.MESH
 ANY = pl.BlockSpec(memory_space=pl.ANY)
 VM = pl.BlockSpec(memory_space=pltpu.VMEM)
+SM = pl.BlockSpec(memory_space=pltpu.SMEM)
 F32 = jnp.float32
 BF16 = jnp.bfloat16
-SUM_ONE = BF16
-SUM_TWO = BF16
-SUM_FFN = BF16
-SUM_THREE = BF16
 CHUNK = 256
 HALF = 128
 ROWS = 64
@@ -771,11 +770,11 @@
             copy.wait_send()
 
 
-def sum_scratch(length, width, kind):
+def sum_scratch(length, width):
     return [
-        pltpu.VMEM((length, width), kind),
-        pltpu.VMEM((3, ROWS, width), kind),
-        pltpu.VMEM((3, ROWS, width), kind),
+        pltpu.VMEM((length, width), BF16),
+        pltpu.VMEM((3, ROWS, width), BF16),
+        pltpu.VMEM((3, ROWS, width), BF16),
         pltpu.SemaphoreType.DMA((2,)),
         pltpu.SemaphoreType.DMA((2, 3)),
     ]
@@ -852,113 +851,158 @@
     )
 
 
-def first_kernel(
-    tok, cot, table, pack, wq, wo,
-    n1, both_cot, tables, packs, wq_all, wo_all,
-    n1_own, small, pair, local, q0, q1, q2, o0, o1, o2,
-):
+def cast_rows(raw, shard):
+    count, rows, _ = raw.shape
+    for j in range(count):
+
+        def step(i, carry):
+            at = pl.ds(pl.multiple_of(i * 32, 32), 32)
+            shard[j, at, :] = raw[j, at, :].astype(BF16)
+            return carry
+
+        lax.fori_loop(0, rows // 32, step, 0)
+
+
+def front_kernel(*refs):
+    head_count, position, bucket, tok, cot, norm_master = refs[:6]
+    masters = refs[6:10]
+    n1, both_cot, tables, packs, n2, mid, q_out, k_out, v_out, a_out = refs[10:20]
+    wholes = refs[20:24]
+    raws, shards = refs[24:28], refs[28:32]
+    raw_sem, n2_own, part, small, pair, local = refs[32:38]
+    sums, tensor_sems, gather_refs = refs[38:43], refs[43:46], refs[46:58]
     here = Here()
-    greet(here, PLANE, ())
+    loads = []
+    for i in range(4):
+        loads.append(pltpu.make_async_copy(masters[i], raws[i], raw_sem.at[i]))
+        loads[i].start()
+    table = tables.at[here.c]
+    fill_table(table, position[...], bucket[...], head_count[0])
     me = here.chunk(0, 0, 0)
+    lane = lax.broadcasted_iota(jnp.int32, (1, CHUNK), 1)
+    counts = jnp.zeros((1, CHUNK), F32)
+    for c in range(4):
+        count = jnp.sum((bucket[...] == c).astype(F32), 1, keepdims=True)
+        counts = counts + jnp.where(lane == c, count, 0.0)
+    packs[pl.ds(me, 1)] = jnp.concatenate(
+        [norm_master[...].astype(BF16).astype(F32), counts, jnp.zeros((3, CHUNK), F32)], 0
+    )[None]
+    greet(here, PLANE, (1, 2, 3))
+    gathers = [
+        Gather(here, i in (0, 2), shards[i], wholes[i], *gather_refs[i * 3 : i * 3 + 3])
+        for i in range(4)
+    ]
+    loads[0].wait()
+    cast_rows(raws[0], shards[0])
+    gathers[0].start()
     packed = []
     for index, peer in enumerate(PLANE):
         packed.append(
-            push(pack, packs.at[me], small.at[0, index], small.at[1, index], here.plane(*peer))
+            push(
+                packs.at[me], packs.at[me],
+                small.at[0, index], small.at[1, index], here.plane(*peer),
+            )
         )
-    packs[pl.ds(me, 1)] = pack[...][None]
-    gather_q = Gather(here, True, wq, wq_all, q0, q1, q2)
-    gather_o = Gather(here, False, wo, wo_all, o0, o1, o2)
-    gather_q.start()
-    gather_o.start()
     partner = here.plane(*PARTNER)
     shared = [
-        push(table, tables.at[here.c], pair.at[0, 0], pair.at[1, 0], partner),
+        push(table, table, pair.at[0, 0], pair.at[1, 0], partner),
         push(cot, both_cot.at[here.c], pair.at[0, 1], pair.at[1, 1], partner),
     ]
-    kept = [
-        pltpu.make_async_copy(table, tables.at[here.c], local.at[0]),
-        pltpu.make_async_copy(cot, both_cot.at[here.c], local.at[1]),
-    ]
-    for copy in kept:
-        copy.start()
+    keep = pltpu.make_async_copy(cot, both_cot.at[here.c], local)
+    keep.start()
+    for i in range(1, 4):
+        loads[i].wait()
+        cast_rows(raws[i], shards[i])
     for copy in packed:
         copy.wait()
     gain, shift = norm_row(packs, 0), norm_row(packs, 1)
+    mine = n1.at[here.c]
 
     def rows_step(i, carry):
         rows = block(i, 32)
         hat, _ = normed(tok[rows, :].astype(F32))
-        n1_own[rows, :] = (hat * gain + shift).astype(BF16)
+        mine[rows, :] = (hat * gain + shift).astype(BF16)
         return carry
 
     lax.fori_loop(0, tok.shape[0] // 32, rows_step, 0)
-    shared.append(push(n1_own, n1.at[here.c], pair.at[0, 2], pair.at[1, 2], partner))
-    kept.append(pltpu.make_async_copy(n1_own, n1.at[here.c], local.at[2]))
-    kept[2].start()
-    gather_q.forward()
-    gather_o.forward()
-    gather_q.finish()
-    gather_o.finish()
-    for copy in kept:
-        copy.wait()
-    for copy in shared:
-        copy.wait()
-
-
-def first_call(tok, cot, table, pack, wq, wo):
-    length, width = tok.shape
-    return pl.pallas_call(
-        first_kernel,
-        out_shape=(
-            jax.ShapeDtypeStruct((2, length, width), BF16),
-            jax.ShapeDtypeStruct((2, length, width), BF16),
-            jax.ShapeDtypeStruct((2,) + table.shape, F32),
-            jax.ShapeDtypeStruct((8,) + pack.shape, F32),
-            jax.ShapeDtypeStruct((wq.shape[0], width, CHUNK), BF16),
-            jax.ShapeDtypeStruct((1, CHUNK, width), BF16),
-        ),
-        in_specs=[VM, ANY, ANY, VM, ANY, ANY],
-        out_specs=(ANY, ANY, ANY, VM, ANY, ANY),
-        scratch_shapes=[
-            pltpu.VMEM((length, width), BF16),
-            pltpu.SemaphoreType.DMA((2, 7)),
-            pltpu.SemaphoreType.DMA((2, 3)),
-            pltpu.SemaphoreType.DMA((3,)),
-        ]
-        + gather_sems()
-        + gather_sems(),
-        compiler_params=params(1),
-        name="gather_attention",
-    )(tok, cot, table, pack, wq, wo)
-
-
-def second_kernel(
-    part, tok, packs, wu, wd,
-    n2, mid, wu_all, wd_all,
-    n2_own, s0, s1, s2, s3, s4, tg, tgp, tgl, u0, u1, u2, d0, d1, d2,
-):
-    here = Here()
-    greet(here, SIDES + [PARTNER], (1, 2, 3))
-    total = TensorSum(here, part, (s0, s1, s2, s3, s4))
+    shared.append(push(mine, mine, pair.at[0, 2], pair.at[1, 2], partner))
+    gathers[0].forward()
+    gathers[1].start()
+    gathers[0].finish()
+    gathers[1].forward()
+    gathers[2].start()
+    gathers[3].start()
+    shared[0].wait_recv()
+    shared[2].wait_recv()
+    head0 = here.z * 4 + here.c * 2
+    attend_body(head0, n1, wholes[0], wholes[1], tables, q_out, k_out, v_out, a_out, part)
+    gathers[1].finish()
+    total = TensorSum(here, part, sums)
+    attend_out(a_out, wholes[1], part, 1 - here.c)
     total.start()
-    gather_u = Gather(here, True, wu, wu_all, u0, u1, u2)
-    gather_d = Gather(here, False, wd, wd_all, d0, d1, d2)
-    gather_u.start()
-    gather_d.start()
+    attend_out(a_out, wholes[1], part, here.c)
     total.spread()
-    middle = tok[...].astype(F32) + total.result()
+    rows = block(here.z, ROWS)
+    middle = tok[rows, :].astype(F32) + total.result()
     mid[...] = middle
     hat, _ = normed(middle)
     n2_own[...] = (hat * norm_row(packs, 2) + norm_row(packs, 3)).astype(BF16)
-    gather = TensorGather(here, n2_own, n2, tg, tgp, tgl)
+    gather = TensorGather(here, n2_own, n2, *tensor_sems)
     gather.start()
+    gathers[2].forward()
+    gathers[3].forward()
     gather.forward()
-    gather_u.forward()
-    gather_d.forward()
     total.finish()
     gather.finish()
-    gather_u.finish()
-    gather_d.finish()
+    gathers[2].finish()
+    gathers[3].finish()
+    keep.wait()
+    shared[0].wait_send()
+    shared[1].wait()
+    shared[2].wait_send()
+
+
+def front_call(head_count, position, bucket, tok, cot, norm_master, masters):
+    length, width = tok.shape
+    both = jax.ShapeDtypeStruct((2, length, width), BF16)
+    thin = jax.ShapeDtypeStruct((2 * length, CHUNK), BF16)
+    wholes = [
+        jax.ShapeDtypeStruct((3, width, CHUNK), BF16),
+        jax.ShapeDtypeStruct((1, CHUNK, width), BF16),
+        jax.ShapeDtypeStruct((4, width, CHUNK), BF16),
+        jax.ShapeDtypeStruct((4, CHUNK, width), BF16),
+    ]
+    results = pl.pallas_call(
+        front_kernel,
+        out_shape=[
+            both,
+            both,
+            jax.ShapeDtypeStruct((2, 5, length, HALF), F32),
+            jax.ShapeDtypeStruct((8, 8, CHUNK), F32),
+            both,
+            jax.ShapeDtypeStruct((ROWS, width), F32),
+            thin, thin, thin, thin,
+        ]
+        + wholes,
+        in_specs=[SM, VM, VM, VM, VM, VM] + [ANY] * 4,
+        out_specs=[VM, ANY, VM, VM, ANY, VM, VM, VM, VM, VM, VM, VM, ANY, ANY],
+        scratch_shapes=[pltpu.VMEM(master.shape, F32) for master in masters]
+        + [pltpu.VMEM(master.shape, BF16) for master in masters]
+        + [
+            pltpu.SemaphoreType.DMA((4,)),
+            pltpu.VMEM((ROWS, width), BF16),
+            pltpu.VMEM((2, length, width), BF16),
+            pltpu.SemaphoreType.DMA((2, 7)),
+            pltpu.SemaphoreType.DMA((2, 3)),
+            pltpu.SemaphoreType.DMA,
+        ]
+        + sum_scratch(length, width)
+        + tensor_gather_sems()
+        + gather_sems() * 4,
+        compiler_params=params(1),
+        name="front",
+    )(head_count, position, bucket, tok, cot, norm_master, *masters)
+    return results[:10], results[10:]
 
 
 def tensor_gather_sems():
@@ -967,28 +1011,6 @@
         pltpu.SemaphoreType.DMA((2, 4)),
         pltpu.SemaphoreType.DMA,
     ]
-
-
-def second_call(part, tok, packs, wu, wd):
-    _, length, width = part.shape
-    return pl.pallas_call(
-        second_kernel,
-        out_shape=(
-            jax.ShapeDtypeStruct((2, length, width), BF16),
-            jax.ShapeDtypeStruct((ROWS, width), F32),
-            jax.ShapeDtypeStruct((wu.shape[0], width, CHUNK), BF16),
-            jax.ShapeDtypeStruct((wd.shape[0], CHUNK, width), BF16),
-        ),
-        in_specs=[VM, VM, VM, ANY, ANY],
-        out_specs=(ANY, VM, ANY, ANY),
-        scratch_shapes=[pltpu.VMEM((ROWS, width), BF16)]
-        + sum_scratch(length, width, part.dtype)
-        + tensor_gather_sems()
-        + gather_sems()
-        + gather_sems(),
-        compiler_params=params(2),
-        name="gather_ffn",
-    )(part, tok, packs, wu, wd)
 
 
 def norm_back(grad_out, hat, inv_std, gain):
@@ -1061,8 +1083,8 @@
         in_specs=[VM, VM, VM, VM, VM, ANY, ANY],
         out_specs=(ANY, VM, VM, VM, ANY, ANY),
         scratch_shapes=[pltpu.VMEM((ROWS, width), BF16)]
-        + sum_scratch(length, width, dn2.dtype)
-        + sum_scratch(length, width, ffn.dtype)
+        + sum_scratch(length, width)
+        + sum_scratch(length, width)
         + tensor_gather_sems()
         + scatter_scratch(gu.shape[0])
         + scatter_scratch(gd.shape[0]),
@@ -1072,9 +1094,9 @@
 
 
 def fourth_kernel(
-    dn1, tok, dmid, out_own, sums, packs, gq, go,
-    output, igrad, norm_total, q_sum, o_sum,
-    ig_own, out_all, ig_all, slices, heard, plane_sum, heard_z, og, ig, ns, nz, *rest,
+    dn1, tok, dmid, sums, packs, gq, go,
+    ig_own, norm_total, q_sum, o_sum,
+    slices, heard, plane_sum, heard_z, ns, nz, *rest,
 ):
     here = Here()
     greet(here, PLANE, (1, 2, 3))
@@ -1085,28 +1107,10 @@
     scatter_q.start()
     scatter_o.start()
     back.spread()
-    copies = []
-
-    def spread_rows(mine, whole, sem):
-        made = []
-        for step in (2, 1, 3):
-            made.append(
-                push(
-                    mine,
-                    whole.at[block(here.z, ROWS), :],
-                    sem.at[0, step - 1],
-                    sem.at[1, step - 1],
-                    here.along(step),
-                )
-            )
-        return made
-
-    copies += spread_rows(out_own, out_all, og)
     grad_n1 = back.result()
     hat, inv_std = normed(tok[...].astype(F32))
     grad_in, gain_sum, shift_sum = norm_back(grad_n1, hat, inv_std, norm_row(packs, 0))
     ig_own[...] = (dmid[...] + grad_in).astype(BF16)
-    copies += spread_rows(ig_own, ig_all, ig)
     for k in range(8):
         cols = slice(k * CHUNK, (k + 1) * CHUNK)
         slices[k, 0:1, :] = gain_sum[:, cols]
@@ -1148,49 +1152,230 @@
     for copy in z_copies:
         copy.wait()
     norm_total[...] = ((heard_z[0] + heard_z[1]) + heard_z[2]) + heard_z[3]
-    for copy in copies:
-        copy.wait()
-    out_all[block(here.z, ROWS), :] = out_own[...]
-    ig_all[block(here.z, ROWS), :] = ig_own[...]
-    output[...] = out_all[...].astype(F32)
-    igrad[...] = ig_all[...].astype(F32)
     back.finish()
     scatter_q.finish()
     scatter_o.finish()
 
 
-def fourth_call(dn1, tok, dmid, out_own, sums, packs, gq, go):
+def fourth_call(dn1, tok, dmid, sums, packs, gq, go):
     _, length, width = dn1.shape
     return pl.pallas_call(
         fourth_kernel,
         out_shape=(
-            jax.ShapeDtypeStruct((length, width), F32),
-            jax.ShapeDtypeStruct((length, width), F32),
+            jax.ShapeDtypeStruct((ROWS, width), BF16),
             jax.ShapeDtypeStruct((8, CHUNK), F32),
             jax.ShapeDtypeStruct((gq.shape[0], CHUNK, 2 * CHUNK), F32),
             jax.ShapeDtypeStruct((1, 2 * CHUNK, CHUNK), F32),
         ),
-        in_specs=[VM] * 6 + [ANY, ANY],
-        out_specs=(VM, VM, VM, ANY, ANY),
+        in_specs=[VM] * 5 + [ANY, ANY],
+        out_specs=(VM, VM, ANY, ANY),
         scratch_shapes=[
-            pltpu.VMEM((ROWS, width), BF16),
-            pltpu.VMEM((length, width), BF16),
-            pltpu.VMEM((length, width), BF16),
             pltpu.VMEM((8, 8, CHUNK), F32),
             pltpu.VMEM((7, 8, CHUNK), F32),
             pltpu.VMEM((8, CHUNK), F32),
             pltpu.VMEM((4, 8, CHUNK), F32),
-            pltpu.SemaphoreType.DMA((2, 3)),
-            pltpu.SemaphoreType.DMA((2, 3)),
             pltpu.SemaphoreType.DMA((2, 7)),
             pltpu.SemaphoreType.DMA((2, 3)),
         ]
-        + sum_scratch(length, width, dn1.dtype)
+        + sum_scratch(length, width)
         + scatter_scratch(gq.shape[0])
         + scatter_scratch(1),
         compiler_params=params(4),
         name="scatter_attention",
-    )(dn1, tok, dmid, out_own, sums, packs, gq, go)
+    )(dn1, tok, dmid, sums, packs, gq, go)
+
+
+FIRST_SCALE = 1.0 / (1.0 - BETA_FIRST**STEP)
+SECOND_SCALE = 1.0 / (1.0 - BETA_SECOND**STEP)
+
+
+def folded(values):
+    rows, cols = values.shape
+    total = None
+    for i in range(rows // 8):
+        for j in range(cols // 128):
+            tile = values[i * 8 : i * 8 + 8, j * 128 : j * 128 + 128]
+            total = tile if total is None else total + tile
+    return total
+
+
+def updated(weight, gradient, first_old, second_old):
+    first_new = BETA_FIRST * first_old + (1.0 - BETA_FIRST) * gradient
+    second_new = BETA_SECOND * second_old + (1.0 - BETA_SECOND) * gradient * gradient
+    update = first_new * FIRST_SCALE / (
+        jnp.sqrt(second_new * SECOND_SCALE) + ADAM_EPS
+    ) + WEIGHT_DECAY * weight
+    return (update, first_new, second_new)
+
+
+def adam_kernel(*refs):
+    sources = [refs[kind * 5 : kind * 5 + 4] for kind in range(4)]
+    norm_grad, norm_master, norm_first, norm_second = [refs[kind * 5 + 4] for kind in range(4)]
+    outs = [refs[20 + kind * 5 : 24 + kind * 5] for kind in range(3)]
+    norm_outs = [refs[24 + kind * 5] for kind in range(3)]
+    tile = refs[35]
+    held = [refs[36 + kind * 4 : 40 + kind * 4] for kind in range(4)]
+    load_sem, store_sem = refs[52:54]
+    blocks = [(i, j) for i in range(4) for j in range(sources[0][i].shape[0])]
+    loads = []
+    for index, (i, j) in enumerate(blocks):
+        loads.append([])
+        for kind in range(4):
+            copy = pltpu.make_async_copy(
+                sources[kind][i].at[j], held[kind][i].at[j], load_sem.at[kind, index]
+            )
+            copy.start()
+            loads[index].append(copy)
+    weight = norm_master[...]
+    update, first_new, second_new = updated(
+        weight, norm_grad[0:4, :], norm_first[...], norm_second[...]
+    )
+    for out, value in zip(norm_outs, (update, first_new, second_new)):
+        out[...] = value
+    for row, value in ((4, weight), (12, update)):
+        square = value * value * 0.25
+        tile[row : row + 4, :] = square[:, :128] + square[:, 128:]
+    stores = []
+    sums = None
+    for index, (i, j) in enumerate(blocks):
+        if j == 0:
+            sums = (jnp.zeros((8, 128), F32), jnp.zeros((8, 128), F32))
+        for copy in loads[index]:
+            copy.wait()
+        grads, masters, firsts, seconds = [held[kind][i] for kind in range(4)]
+
+        def step(k, carry):
+            at = pl.ds(pl.multiple_of(k * 16, 16), 16)
+            weight = masters[j, at, :]
+            update, first_new, second_new = updated(
+                weight, grads[j, at, :], firsts[j, at, :], seconds[j, at, :]
+            )
+            grads[j, at, :] = update
+            firsts[j, at, :] = first_new
+            seconds[j, at, :] = second_new
+            return (carry[0] + folded(weight * weight), carry[1] + folded(update * update))
+
+        sums = lax.fori_loop(0, grads.shape[1] // 16, step, sums)
+        for kind, source in enumerate((grads, firsts, seconds)):
+            copy = pltpu.make_async_copy(
+                source.at[j], outs[kind][i].at[j], store_sem.at[kind, index]
+            )
+            copy.start()
+            stores.append(copy)
+        if j == grads.shape[0] - 1:
+            tile[i : i + 1, :] = jnp.sum(sums[0], 0, keepdims=True)
+            tile[8 + i : 9 + i, :] = jnp.sum(sums[1], 0, keepdims=True)
+    for copy in stores:
+        copy.wait()
+
+
+def adam_call(grads, masters, firsts, seconds):
+    shapes = [master.shape for master in masters]
+    like = [jax.ShapeDtypeStruct(shape, F32) for shape in shapes]
+    specs = [ANY] * 4 + [VM]
+    count = sum(shape[0] for shape in shapes[:4])
+    results = pl.pallas_call(
+        adam_kernel,
+        out_shape=like * 3 + [jax.ShapeDtypeStruct((16, 128), F32)],
+        in_specs=specs * 4,
+        out_specs=specs * 3 + [VM],
+        scratch_shapes=[pltpu.VMEM(shape, F32) for shape in shapes[:4]] * 4
+        + [pltpu.SemaphoreType.DMA((4, count)), pltpu.SemaphoreType.DMA((3, count))],
+        compiler_params=local_params(),
+        name="adam",
+    )(*grads, *masters, *firsts, *seconds)
+    return results[0:5], results[5:10], results[10:15], results[15]
+
+
+def total_kernel(tile, norms, tiles_z, plane_tile, tiles, zs, ps):
+    here = Here()
+    greet(here, PLANE, (1, 2, 3))
+    sent = []
+    for step in (2, 1, 3):
+        sent.append(
+            push(tile, tiles_z.at[here.z], zs.at[0, step - 1], zs.at[1, step - 1], here.along(step))
+        )
+    tiles_z[pl.ds(here.z, 1)] = tile[...][None]
+    for copy in sent:
+        copy.wait()
+    plane_tile[...] = ((tiles_z[0] + tiles_z[1]) + tiles_z[2]) + tiles_z[3]
+    me = here.chunk(0, 0, 0)
+    sent = []
+    for index, peer in enumerate(PLANE):
+        sent.append(
+            push(plane_tile, tiles.at[me], ps.at[0, index], ps.at[1, index], here.plane(*peer))
+        )
+    tiles[pl.ds(me, 1)] = plane_tile[...][None]
+    for copy in sent:
+        copy.wait()
+    total = tiles[0]
+    for k in range(1, 8):
+        total = total + tiles[k]
+    roots = jnp.sqrt(jnp.sum(total, 1, keepdims=True))
+    norms[...] = jnp.broadcast_to(roots, norms.shape)
+
+
+def total_call(tile):
+    return pl.pallas_call(
+        total_kernel,
+        out_shape=jax.ShapeDtypeStruct((16, 128), F32),
+        in_specs=[VM],
+        out_specs=VM,
+        scratch_shapes=[
+            pltpu.VMEM((4, 16, 128), F32),
+            pltpu.VMEM((16, 128), F32),
+            pltpu.VMEM((8, 16, 128), F32),
+            pltpu.SemaphoreType.DMA((2, 3)),
+            pltpu.SemaphoreType.DMA((2, 7)),
+        ],
+        compiler_params=params(5),
+        name="norm_totals",
+    )(tile)
+
+
+def weight_kernel(*refs):
+    norms, updates, masters = refs[0], refs[1:6], refs[6:11]
+    outs = refs[11:16]
+    held = (refs[16:20], refs[20:24])
+    load_sem, store_sem = refs[24:26]
+    blocks = [(i, j) for i in range(4) for j in range(updates[i].shape[0])]
+    loads = []
+    for index, (i, j) in enumerate(blocks):
+        loads.append([])
+        for kind, source in enumerate((updates, masters)):
+            copy = pltpu.make_async_copy(
+                source[i].at[j], held[kind][i].at[j], load_sem.at[kind, index]
+            )
+            copy.start()
+            loads[index].append(copy)
+    scales = LEARN_RATE * (norms[0:8, 0:1] / norms[8:16, 0:1])
+    outs[4][...] = masters[4][...] - scales[4:8, :] * updates[4][...]
+    stores = []
+    for index, (i, j) in enumerate(blocks):
+        for copy in loads[index]:
+            copy.wait()
+        held[1][i][j] = held[1][i][j] - scales[i : i + 1, :] * held[0][i][j]
+        copy = pltpu.make_async_copy(held[1][i].at[j], outs[i].at[j], store_sem.at[index])
+        copy.start()
+        stores.append(copy)
+    for copy in stores:
+        copy.wait()
+
+
+def weight_call(norms, updates, masters):
+    shapes = [master.shape for master in masters]
+    specs = [ANY] * 4 + [VM]
+    count = sum(shape[0] for shape in shapes[:4])
+    return pl.pallas_call(
+        weight_kernel,
+        out_shape=[jax.ShapeDtypeStruct(shape, F32) for shape in shapes],
+        in_specs=[VM] + specs * 2,
+        out_specs=specs,
+        scratch_shapes=[pltpu.VMEM(shape, F32) for shape in shapes[:4]] * 2
+        + [pltpu.SemaphoreType.DMA((2, count)), pltpu.SemaphoreType.DMA((count,))],
+        compiler_params=local_params(),
+        name="new_weights",
+    )(norms, *updates, *masters)
 
 
 def turn(values, cosine, sine):
@@ -1211,9 +1396,9 @@
     return exp_scores / jnp.sum(exp_scores, -1, keepdims=True)
 
 
-def attend_kernel(head0, n1, wq, wo, tables, q_out, k_out, v_out, a_out, part):
+def attend_body(head0, n1, wq, wo, tables, q_out, k_out, v_out, a_out, part):
     length = tables.shape[2]
-    rows_in = n1[...]
+    rows_in = n1[...].reshape(2 * length, n1.shape[2])
     projected = [dot(rows_in, wq[j]) for j in range(3)]
     for s in range(2):
         rows = slice(s * length, (s + 1) * length)
@@ -1226,34 +1411,43 @@
             value_rows = projected[2][rows, cols].astype(BF16)
             weights = attention_weights(queries, key_rows, lowest).astype(BF16)
             heads = dot(weights, value_rows)
-            active = tables[s, 4] > (head0[0] + h).astype(F32)
+            active = tables[s, 4] > (head0 + h).astype(F32)
             q_out[rows, cols] = queries
             k_out[rows, cols] = key_rows
             v_out[rows, cols] = value_rows
             a_out[rows, cols] = jnp.where(active, heads, 0.0).astype(BF16)
-    for s in range(2):
-        rows = slice(s * length, (s + 1) * length)
-        part[s] = dot(a_out[rows, :], wo[0]).astype(part.dtype)
-
-
-SM = pl.BlockSpec(memory_space=pltpu.SMEM)
+
+
+def attend_out(a_out, wo, part, s):
+    length = part.shape[1]
+    part[s] = dot(a_out[pl.ds(pl.multiple_of(s * length, length), length), :], wo[0]).astype(BF16)
+
+
+def fill_table(table, position, bucket, head_count):
+    length = table.shape[1]
+    row = lax.broadcasted_iota(jnp.int32, (length, length), 0)
+    col = lax.broadcasted_iota(jnp.int32, (length, length), 1)
+
+    def column(values):
+        return jnp.sum(jnp.where(row == col, values.astype(F32), 0.0), 1, keepdims=True)
+
+    place = column(position)
+    lane = lax.broadcasted_iota(jnp.int32, (length, HALF), 1)
+    half = HEAD_DIM // 2
+    second = lane >= half
+    freq_index = jnp.where(second, lane - half, lane).astype(F32)
+    angles = place * jnp.exp(freq_index * (-2.0 * math.log(ROPE_BASE) / HEAD_DIM))
+    table[0] = jnp.cos(angles)
+    sine = jnp.sin(angles)
+    table[1] = jnp.where(second, sine, -sine)
+    index = lax.broadcasted_iota(jnp.int32, (length, HALF), 0).astype(F32)
+    table[2] = index - place
+    table[3] = jnp.broadcast_to(column(bucket), (length, HALF))
+    table[4] = jnp.broadcast_to(head_count.astype(F32), (length, HALF))
 
 
 def local_params():
     return pltpu.CompilerParams(vmem_limit_bytes=60 << 20)
-
-
-def attend_call(head0, n1, wq, wo, tables):
-    _, length, width = n1.shape
-    thin = jax.ShapeDtypeStruct((2 * length, CHUNK), BF16)
-    return pl.pallas_call(
-        attend_kernel,
-        out_shape=(thin, thin, thin, thin, jax.ShapeDtypeStruct((2, length, width), SUM_ONE)),
-        in_specs=[SM, VM, VM, VM, VM],
-        out_specs=(VM,) * 5,
-        compiler_params=local_params(),
-        name="attend",
-    )(head0, n1.reshape(2 * length, width), wq, wo, tables)
 
 
 def ffn_kernel(n2, cot, bucket, wu, wd, dn2, ffn, gu, gd, back_sum, ffn_sum):
@@ -1292,8 +1486,8 @@
         ffn_kernel,
         grid=(4,),
         out_shape=(
-            jax.ShapeDtypeStruct((total, width), SUM_TWO),
-            jax.ShapeDtypeStruct((total, width), SUM_FFN),
+            jax.ShapeDtypeStruct((total, width), BF16),
+            jax.ShapeDtypeStruct((total, width), BF16),
             jax.ShapeDtypeStruct((4, width, CHUNK), BF16),
             jax.ShapeDtypeStruct((4, CHUNK, width), BF16),
         ),
@@ -1360,7 +1554,7 @@
     return pl.pallas_call(
         attend_back_kernel,
         out_shape=(
-            jax.ShapeDtypeStruct((2, length, width), SUM_THREE),
+            jax.ShapeDtypeStruct((2, length, width), BF16),
             jax.ShapeDtypeStruct((3, width, CHUNK), BF16),
             jax.ShapeDtypeStruct((1, CHUNK, width), BF16),
         ),
@@ -1375,23 +1569,6 @@
     )
 
 
-def make_table(positions, buckets, head_count):
-    length = positions.shape[0]
-    angles = rope_angles(positions)
-    cosine, sine = jnp.cos(angles), jnp.sin(angles)
-    lowest = (jnp.arange(length, dtype=jnp.int32) - positions).astype(F32)
-    wide = lambda column: jnp.broadcast_to(column, (length, HALF))
-    return jnp.stack(
-        [
-            jnp.concatenate([cosine, cosine], 1),
-            jnp.concatenate([-sine, sine], 1),
-            wide(lowest[:, None]),
-            wide(buckets.astype(F32)[:, None]),
-            wide(head_count.astype(F32)),
-        ]
-    )
-
-
 def fast_body(
     tokens, cotangent, head_counts, positions, buckets,
     in_master, out_master, up_master, down_master, norm_master,
@@ -1400,45 +1577,43 @@
 ):
     length = tokens.shape[1]
     groups_data = lax.axis_size("dp") * lax.axis_size("expert")
-    tensor_count = lax.axis_size("tensor")
     tok, cot = tokens[0], cotangent[0]
-    table = make_table(positions[0], buckets[0], head_counts)
-    onehot = (buckets[0][:, None] == jnp.arange(CHUNK, dtype=jnp.int32)[None, :]).astype(F32)
-    pack = jnp.concatenate(
-        [
-            lax.reduce_precision(norm_master, 8, 7),
-            jnp.sum(onehot, 0, keepdims=True),
-            jnp.zeros((3, CHUNK), F32),
-        ],
-        0,
-    )
-    n1, both_cot, tables, packs, wq, wo = first_call(
-        tok, cot, table, pack, in_master.astype(BF16), out_master.astype(BF16)[None]
+    (n1, both_cot, tables, packs, n2, mid, q_rows, k_rows, v_rows, a_rows), (wq, wo, wu, wd) = front_call(
+        head_counts, positions, buckets, tok, cot, norm_master,
+        (in_master, out_master[None], up_master, down_master),
     )
     bucket_share = jnp.sum(packs[:, 4, :4], 0) / (length * groups_data)
     heads_here = 2 * CHUNK // HEAD_DIM
     core = lax.rem(lax.axis_index("dp"), 2)
     head0 = (lax.axis_index("tensor") * heads_here + core * (heads_here // 2))[None].astype(jnp.int32)
-    q_rows, k_rows, v_rows, a_rows, part = attend_call(head0, n1, wq, wo, tables)
     place = lax.axis_index("tensor") * ROWS
     tok_own = lax.dynamic_slice_in_dim(tok, place, ROWS, 0)
     cot_own = lax.dynamic_slice_in_dim(cot, place, ROWS, 0)
-    n2, mid, wu, wd = second_call(
-        part, tok_own, packs, up_master.astype(BF16), down_master.astype(BF16)
-    )
     bucket = tables[:, 3].reshape(2 * length, HALF)
     dn2, ffn, gu, gd = ffn_call(n2, both_cot, bucket, wu, wd)
     gm, dmid, out_own, sums, up_sum, down_sum = third_call(dn2, ffn, mid, cot_own, packs, gu, gd)
     dn1, gq, go = attend_back_call(head0, gm, n1, a_rows, q_rows, k_rows, v_rows, wq, wo, tables)
-    output, input_grad, norm_sum, in_sum, out_sum = fourth_call(
-        dn1, tok_own, dmid, out_own, sums, packs, gq, go
-    )
-    masters = (in_master, out_master, up_master, down_master, norm_master)
-    firsts = (in_first, out_first, up_first, down_first, norm_first)
-    seconds = (in_second, out_second, up_second, down_second, norm_second)
-    grad_shards = (in_sum, out_sum[0], up_sum, down_sum, norm_sum[:4])
-    return finish(
-        output, input_grad, bucket_share, masters, firsts, seconds, grad_shards, tensor_count
+    gather_tensor = lambda rows: lax.all_gather(rows, "tensor", axis=0, tiled=True).astype(F32)
+    output = gather_tensor(out_own)
+    ig_own, norm_sum, in_sum, out_sum = fourth_call(dn1, tok_own, dmid, sums, packs, gq, go)
+    input_grad = gather_tensor(ig_own)
+    masters = (in_master, out_master[None], up_master, down_master, norm_master)
+    firsts = (in_first, out_first[None], up_first, down_first, norm_first)
+    seconds = (in_second, out_second[None], up_second, down_second, norm_second)
+    updates, moments, squares, tile = adam_call(
+        (in_sum, out_sum, up_sum, down_sum, norm_sum), masters, firsts, seconds
+    )
+    norms = total_call(tile)
+    weights = weight_call(norms, updates, masters)
+    flat = lambda group: (group[0], group[1][0], group[2], group[3], group[4])
+    return (
+        output[None],
+        input_grad[None],
+        bucket_share,
+        norms[:, 0].reshape(2, 8),
+        *flat(weights),
+        *flat(moments),
+        *flat(squares),
     )
 
 

time: 463 us -> 363 us (0.78)
  Pallas kernels: 363 us -> 323 us
  blocking collectives: 38.3 us -> 0 us
  other arithmetic: 42.7 us -> 6.88 us
  waiting for transfers between devices: 0 us -> 12.9 us
  between operations: 4.42 us -> 14.8 us
  local copies, waits for them, and re-layouts: 13.7 us -> 5 us
    psum x1 -> x0, blocking collectives: 38.3 us -> none  [finish(): lax.psum((weight_sq, update_sq), ('dp', 'expert', 'tensor'))]
    pallas_call x4 -> x5, Pallas kernels: 249 us -> 212 us  [the longest x1 123 us: front_call(): pl.pallas_call(front_kernel, out_shape=[both, both, jax.ShapeDtypeStruct(...]
    reduce_sum x7 -> x0, other arithmetic: 19.5 us -> none  [the longest x4 17.1 us: finish(): jnp.sum(masters[member] * masters[member])]
    all_gather x0 -> x2, waiting for transfers between devices: none -> 12.2 us  [fast_body(): lax.all_gather(rows, 'tensor', axis=0, tiled=True).astype(F32)]
    sub x5 -> x0, other arithmetic: 10.9 us -> none  [the longest x4 10.2 us: finish(): masters[member] - LEARN_RATE * ratios[member] * adam_out[member][0]]
    convert_element_type x6 -> x0, other arithmetic: 8.26 us -> none  [the longest x1 2.69 us: fast_body(): up_master.astype(BF16)]
    concatenate x3 -> x0, local copies, waits for them, and re-layouts: 5.41 us -> none  [the longest x1 2.67 us: finish(): jnp.concatenate([jnp.stack([jnp.sum(adam_out[member][0] * adam_out[member...]
    broadcast_in_dim x1 -> x2, other arithmetic: 0.73 us -> 5.58 us  [the longest x1 2.79 us: fast_body(): input_grad[None]]
  transfers between devices with their start and end apart: 0 -> 2, of which waited for: 0 -> 1; matrix products, arithmetic and copies ran while one was open for 0% -> 2% of each run, Pallas kernels for 0% -> 12%
where the time goes in v2:
time: 363 us
  Pallas kernels  323 us (89%)
  between operations  14.8 us (4%)
  waiting for transfers between devices  12.9 us (4%)
  other arithmetic  6.88 us (2%)
  local copies, waits for them, and re-layouts  5 us (1%)
    pallas_call x1, Pallas kernels, front_call(): pl.pallas_call(front_kernel, out_shape=[both, both, jax.ShapeDtypeStruct(...  123 us
    pallas_call x1, Pallas kernels, third_call(): pl.pallas_call(third_kernel, out_shape=(jax.ShapeDtypeStruct((2, length,...  77.6 us
    pallas_call x1, Pallas kernels, fourth_call(): pl.pallas_call(fourth_kernel, out_shape=(jax.ShapeDtypeStruct((ROWS, widt...  46.5 us
    pallas_call x1, Pallas kernels, ffn_call(): pl.pallas_call(ffn_kernel, grid=(4,), out_shape=(jax.ShapeDtypeStruct((to...  20.4 us
    pallas_call x1, Pallas kernels, adam_call(): pl.pallas_call(adam_kernel, out_shape=like * 3 + [jax.ShapeDtypeStruct((1...  17.9 us
    pallas_call x1, Pallas kernels, total_call(): pl.pallas_call(total_kernel, out_shape=jax.ShapeDtypeStruct((16, 128), F3...  15.7 us
    pallas_call x1, Pallas kernels, attend_back_call(): pl.pallas_call(attend_back_kernel, out_shape=(jax.ShapeDtypeStruct((2, le...  13.5 us
    all_gather x2, waiting for transfers between devices, fast_body(): lax.all_gather(rows, 'tensor', axis=0, tiled=True).astype(F32)  12.2 us
  transfers between devices with their start and end apart: 2, of which 1 were waited for; matrix products, arithmetic and copies ran while one was open for 2% of the time, Pallas kernels for 12%

profile of v2, /device:TPU:0, one launch (start us, length us, event | category | flops | bytes accessed | tf_op | source)
XLA Modules:
  0.0 362.9 jit_solution(13587440124866241167)
XLA Ops:
  7.2 0.0 all-gather.5.cloned.1.call-start
  7.9 122.6 %front.1 = (bf16[2,256,2048]{2,1,0:T(8,128)(2,1)}, bf16[2,256,2048]{2,1,0:T(8,128)(2,1)}, f32[2,5,256,128]{3,2,1,0:T(8,128)}, f32[8,8,256]{2,1,0:T(8,128)}, bf16...) custom-call(s32[1]{0:T(128)S(6)} %copy.39.refs_0_, ...), custom_call_target="tpu_custom_call" | custom-call | tf_op jit(solution)/shard_map/front/pallas_call | solution.py:975
  130.5 1.7 slice.9
  132.2 1.9 dynamic-slice_bitcast_fusion
  134.0 20.4 %ffn.1 = (bf16[512,2048]{1,0:T(8,128)(2,1)}, bf16[512,2048]{1,0:T(8,128)(2,1)}, bf16[4,2048,256]{2,1,0:T(8,128)(2,1)}, bf16[4,256,2048]{2,1,0:T(8,128)(2,1)}) custom-call(bf16[512,2048]{1,0:T(8,128)(2,1)} %bitcast.30, bf16[512,2048]{1,0:T(8,128)(2,1)} %bitcast.29, f32[512,128]{1,0:T(8,128)} %bitcast.37, bf16[4,2048,256]{2,1,0:T(8,128)(2,1)} %get-tuple-element.74.wu, ...), custom_call_target="tpu_custom_call" | custom-call | tf_op jit(solution)/shard_map/ffn/pallas_call | solution.py:1485
  154.5 77.6 %scatter_ffn.1 = (bf16[2,256,2048]{2,1,0:T(8,128)(2,1)}, f32[64,2048]{1,0:T(8,128)}, bf16[64,2048]{1,0:T(8,128)(2,1)}, f32[2,2048]{1,0:T(2,128)}, f32[4,256,512]{2,1,0:T(8,128)}, /*index=5*/f32[4,512,256]{2,1,0:T(8,128)}) custom-call(bf16[2,256,2048]{2,1,0:T(8,128)(2,1)} %bitcast.31, bf16[2,256,2048]{2,1,0:T(8,128)(2,1)} %bitcast.32, ...), custom_call_target="tpu_custom_call" | custom-call | tf_op jit(solution)/shard_map/scatter_ffn/pallas_call | solution.py:1073
  232.1 13.5 %attend_back.1 = (bf16[2,256,2048]{2,1,0:T(8,128)(2,1)}, bf16[3,2048,256]{2,1,0:T(8,128)(2,1)}, bf16[1,256,2048]{2,1,0:T(8,128)(2,1)}) custom-call(s32[1]{0:T(128)} %bitcast.10.head0, bf16[512,2048]{1,0:T(8,128)(2,1)} %bitcast.34, bf16[512,2048]{1,0:T(8,128)(2,1)} %bitcast.33, bf16[512,256]{1,0:T(8,128)(2,1)} %get-tuple-element.85.a_rows, ...), custom_call_target="tpu_custom_call" | custom-call | tf_op jit(solution)/shard_map/attend_back/pallas_call | solution.py:1554
  245.6 46.5 %scatter_attention.1 = (bf16[64,2048]{1,0:T(8,128)(2,1)}, f32[8,256]{1,0:T(8,128)}, f32[3,256,512]{2,1,0:T(8,128)}, f32[1,512,256]{2,1,0:T(8,128)}) custom-call(bf16[2,256,2048]{2,1,0:T(8,128)(2,1)} %get-tuple-element.91.dn1, bf16[64,2048]{1,0:T(8,128)(2,1)} %get-tuple-element.123.tok, f32[64,2048]{1,0:T(8,128)} %get-tuple-element.92.dmid, ...), custom_call_target="tpu_custom_call" | custom-call | tf_op jit(solution)/shard_map/scatter_attention/pallas_call | solution.py:1162
  292.2 0.0 all-gather.5.cloned.1.call-update
  292.2 0.0 all-gather.3.cloned.1.call-start
  292.2 0.7 all-gather.3.cloned.1.call-update
  292.9 17.9 %adam.1 = (f32[3,256,512]{2,1,0:T(8,128)}, f32[1,512,256]{2,1,0:T(8,128)}, f32[4,256,512]{2,1,0:T(8,128)}, f32[4,512,256]{2,1,0:T(8,128)}, f32[4,256]{1,0:T(4,12...) custom-call(f32[3,256,512]{2,1,0:T(8,128)} %get-tuple-element.97.ref, ...), custom_call_target="tpu_custom_call" | custom-call | tf_op jit(solution)/shard_map/adam/pallas_call | solution.py:1277
  310.9 15.7 %norm_totals.1.refs_0_ = f32[16,128]{1,0:T(8,128)} custom-call(f32[16,128]{1,0:T(8,128)} %get-tuple-element.102.tile), custom_call_target="tpu_custom_call" | custom-call | tf_op jit(solution)/shard_map/norm_totals/pallas_call | solution.py:1319
  326.6 0.8 slice_reduce_fusion
  327.5 0.6 reshape_squeeze.7
  328.1 8.9 %new_weights.1 = (f32[3,256,512]{2,1,0:T(8,128)}, f32[1,512,256]{2,1,0:T(8,128)}, f32[4,256,512]{2,1,0:T(8,128)}, f32[4,512,256]{2,1,0:T(8,128)}, f32[4,256]{1,0:T(4,128)}) custom-call(f32[16,128]{1,0:T(8,128)} %norm_totals.1.refs_0_, f32[3,256,512]{2,1,0:T(8,128)} %get-tuple-element.103.refs_1_, f32[1,512,256]{2,1,0:T(8,128)} %get-tuple-element.104.refs_2_, ...), custom_call_target="tpu_custom_call" | custom-call | tf_op jit(solution)/shard_map/new_weights/pallas_call | solution.py:1369
  337.0 0.8 slice_reduce_fusion.1
  337.8 0.5 broadcast_multiply_fusion
  338.3 0.0 all-gather.5.cloned.1.call-done
  338.3 2.8 bitcast_convert_fusion
  341.1 12.2 %all-gather.3.cloned.1.call-done = bf16[256,2048]{1,0:T(8,128)(2,1)} async-done(((bf16[64,2048]{1,0:T(8,128)(2,1)}), bf16[256,2048]{1,0:T(8,128)(2,1)}) %all-gather.3.cloned.1.call-update) | async-done | bytes 1048592 | tf_op jit(solution)/shard_map/all_gather | solution.py:1596
  353.3 2.8 bitcast_convert_fusion.1
Async XLA Ops:
  7.2 331.1 %all-gather.5.cloned.1.call-start = ((), (), s32[]{:S(2)}) async-start(), calls=%async_computation.1 | async-start | bytes 1310720 | tf_op jit(solution)/shard_map/all_gather | solution.py:1596
  292.2 61.1 %all-gather.3.cloned.1.call-start = ((), (), s32[]{:S(2)}) async-start(), calls=%async_computation | async-start | bytes 1310720 | tf_op jit(solution)/shard_map/all_gather | solution.py:1596
Sparse Core Ops, SparseCore 0:
  292.3 32.3 all-gather.4
  326.3 26.9 all-gather.2

commit v3 on v2

--- a/solution.py
+++ b/solution.py
@@ -457,6 +457,7 @@
 ANY = pl.BlockSpec(memory_space=pl.ANY)
 VM = pl.BlockSpec(memory_space=pltpu.VMEM)
 SM = pl.BlockSpec(memory_space=pltpu.SMEM)
+
 F32 = jnp.float32
 BF16 = jnp.bfloat16
 CHUNK = 256
@@ -610,11 +611,13 @@
 class Scatter:
     def __init__(self, here, by_rows, grad, total, bufs):
         self.here, self.by_rows, self.grad, self.total = here, by_rows, grad, total
-        (self.own, self.got, self.got_two, self.final) = bufs[:4]
-        (self.load_sem, self.one_sem, self.two_sem, self.last_sem, self.local) = bufs[4:]
-
-    def part(self, k, part):
-        return rows_part(self.grad, k, part) if self.by_rows else cols_part(self.grad, k, part)
+        self.got, self.got_two = bufs[:2]
+        self.one_sem, self.two_sem, self.last_sem, self.local = bufs[2:6]
+        self.final = bufs[6]
+
+    def part(self, dx, dy, core, side):
+        k = self.here.chunk_of(dx, dy, core)
+        return rows_part(self.grad, k, side) if self.by_rows else cols_part(self.grad, k, side)
 
     def start(self):
         here = self.here
@@ -624,43 +627,32 @@
             target = here.plane(1, 0, 0) if side == 0 else here.plane(0, 0, 1)
             for slot in range(4):
                 chip = far if slot >= 2 else near
-                src = self.part(here.chunk_of(chip[0], chip[1], slot % 2), side)
                 index = side * 4 + slot
                 self.first.append(
                     push(
-                        src,
+                        self.part(chip[0], chip[1], slot % 2, side),
                         self.got.at[index],
                         self.one_sem.at[0, index],
                         self.one_sem.at[1, index],
                         target,
                     )
                 )
-        self.loads = []
-        for side in (0, 1):
-            for slot in range(4):
-                chip = (0, 0) if slot < 2 else ((0, 1) if side == 0 else (1, 0))
-                src = self.part(here.chunk_of(chip[0], chip[1], slot % 2), side)
-                index = side * 4 + slot
-                copy = pltpu.make_async_copy(src, self.own.at[index], self.load_sem.at[index])
-                copy.start()
-                self.loads.append(copy)
 
     def middle(self):
         here = self.here
         self.second = []
         for side in (0, 1):
             target = here.plane(0, 0, 1) if side == 0 else here.plane(1, 0, 0)
+            chip = (0, 1) if side == 0 else (1, 0)
             for slot in (2, 3):
                 index = side * 4 + slot
-                self.loads[index].wait()
+                two = side * 2 + slot - 2
+                mine = self.part(chip[0], chip[1], slot - 2, side)
                 self.first[index].wait_recv()
-                self.own[index] = (
-                    self.own[index].astype(F32) + self.got[index].astype(F32)
-                ).astype(BF16)
-                two = side * 2 + slot - 2
+                mine[...] = (mine[...].astype(F32) + self.got[index].astype(F32)).astype(BF16)
                 self.second.append(
                     push(
-                        self.own.at[index],
+                        mine,
                         self.got_two.at[two],
                         self.two_sem.at[0, two],
                         self.two_sem.at[1, two],
@@ -674,11 +666,10 @@
             for slot in (0, 1):
                 index = side * 4 + slot
                 two = side * 2 + slot
-                self.loads[index].wait()
                 self.first[index].wait_recv()
                 self.second[two].wait_recv()
                 self.final[slot, :, side * HALF : side * HALF + HALF, :] = (
-                    self.own[index].astype(F32) + self.got[index].astype(F32)
+                    self.part(0, 0, slot, side)[...].astype(F32) + self.got[index].astype(F32)
                 ) + self.got_two[two].astype(F32)
         if self.by_rows:
             where = self.total.at[:, :, block(here.c, CHUNK)]
@@ -694,22 +685,22 @@
             here.plane(*PARTNER),
         )
 
+    def sent(self):
+        self.keep.wait()
+        self.give.wait_send()
+
     def finish(self):
         for copy in self.first:
             copy.wait_send()
         for copy in self.second:
             copy.wait_send()
-        self.keep.wait()
-        self.give.wait()
+        self.give.wait_recv()
 
 
 def scatter_scratch(width):
     return [
         pltpu.VMEM((8, width, HALF, CHUNK), BF16),
-        pltpu.VMEM((8, width, HALF, CHUNK), BF16),
         pltpu.VMEM((4, width, HALF, CHUNK), BF16),
-        pltpu.VMEM((2, width, CHUNK, CHUNK), F32),
-        pltpu.SemaphoreType.DMA((8,)),
         pltpu.SemaphoreType.DMA((2, 8)),
         pltpu.SemaphoreType.DMA((2, 4)),
         pltpu.SemaphoreType.DMA((2,)),
@@ -717,7 +708,7 @@
     ]
 
 
-SCATTER = 9
+SCATTER = 6
 
 
 class TensorSum:
@@ -876,8 +867,6 @@
     for i in range(4):
         loads.append(pltpu.make_async_copy(masters[i], raws[i], raw_sem.at[i]))
         loads[i].start()
-    table = tables.at[here.c]
-    fill_table(table, position[...], bucket[...], head_count[0])
     me = here.chunk(0, 0, 0)
     lane = lax.broadcasted_iota(jnp.int32, (1, CHUNK), 1)
     counts = jnp.zeros((1, CHUNK), F32)
@@ -887,13 +876,13 @@
     packs[pl.ds(me, 1)] = jnp.concatenate(
         [norm_master[...].astype(BF16).astype(F32), counts, jnp.zeros((3, CHUNK), F32)], 0
     )[None]
-    greet(here, PLANE, (1, 2, 3))
     gathers = [
         Gather(here, i in (0, 2), shards[i], wholes[i], *gather_refs[i * 3 : i * 3 + 3])
         for i in range(4)
     ]
     loads[0].wait()
     cast_rows(raws[0], shards[0])
+    greet(here, PLANE, (1, 2, 3))
     gathers[0].start()
     packed = []
     for index, peer in enumerate(PLANE):
@@ -904,6 +893,8 @@
             )
         )
     partner = here.plane(*PARTNER)
+    table = tables.at[here.c]
+    fill_table(table, position[...], bucket[...], head_count[0])
     shared = [
         push(table, table, pair.at[0, 0], pair.at[1, 0], partner),
         push(cot, both_cot.at[here.c], pair.at[0, 1], pair.at[1, 1], partner),
@@ -926,10 +917,10 @@
 
     lax.fori_loop(0, tok.shape[0] // 32, rows_step, 0)
     shared.append(push(mine, mine, pair.at[0, 2], pair.at[1, 2], partner))
+    gathers[1].start()
     gathers[0].forward()
-    gathers[1].start()
+    gathers[1].forward()
     gathers[0].finish()
-    gathers[1].forward()
     gathers[2].start()
     gathers[3].start()
     shared[0].wait_recv()
@@ -1027,99 +1018,74 @@
     )
 
 
-def third_kernel(
-    dn2, ffn, mid, cot, packs, gu, gd,
-    gm, dmid, out_own, sums, up_sum, down_sum,
-    gm_own, *rest,
-):
-    here = Here()
-    greet(here, [(1, 0, 0), (0, 0, 1), PARTNER], (1, 2, 3))
-    back = TensorSum(here, dn2, rest[0:5])
-    branch = TensorSum(here, ffn, rest[5:10])
-    scatter_u = Scatter(here, True, gu, up_sum, rest[13 : 13 + SCATTER])
-    scatter_d = Scatter(here, False, gd, down_sum, rest[13 + SCATTER : 13 + 2 * SCATTER])
-    back.start()
-    branch.start()
-    scatter_u.start()
-    scatter_d.start()
-    back.spread()
-    branch.spread()
-    grad_n2 = back.result().astype(BF16).astype(F32)
-    middle = mid[...]
-    hat, inv_std = normed(middle)
-    grad_mid, gain_sum, shift_sum = norm_back(grad_n2, hat, inv_std, norm_row(packs, 2))
-    grad_mid = cot[...].astype(F32) + grad_mid
-    dmid[...] = grad_mid
-    gm_own[...] = grad_mid.astype(BF16)
-    gather = TensorGather(here, gm_own, gm, *rest[10:13])
-    gather.start()
-    sums[0:1, :] = gain_sum
-    sums[1:2, :] = shift_sum
-    scatter_u.middle()
-    scatter_d.middle()
-    out_own[...] = (mid[...] + branch.result().astype(BF16).astype(F32)).astype(BF16)
-    gather.forward()
-    scatter_u.last()
-    scatter_d.last()
-    back.finish()
-    branch.finish()
-    gather.finish()
-    scatter_u.finish()
-    scatter_d.finish()
-
-
-def third_call(dn2, ffn, mid, cot, packs, gu, gd):
-    _, length, width = dn2.shape
-    return pl.pallas_call(
-        third_kernel,
-        out_shape=(
-            jax.ShapeDtypeStruct((2, length, width), BF16),
-            jax.ShapeDtypeStruct((ROWS, width), F32),
-            jax.ShapeDtypeStruct((ROWS, width), BF16),
-            jax.ShapeDtypeStruct((2, width), F32),
-            jax.ShapeDtypeStruct((gu.shape[0], CHUNK, 2 * CHUNK), F32),
-            jax.ShapeDtypeStruct((gd.shape[0], 2 * CHUNK, CHUNK), F32),
-        ),
-        in_specs=[VM, VM, VM, VM, VM, ANY, ANY],
-        out_specs=(ANY, VM, VM, VM, ANY, ANY),
-        scratch_shapes=[pltpu.VMEM((ROWS, width), BF16)]
-        + sum_scratch(length, width)
-        + sum_scratch(length, width)
-        + tensor_gather_sems()
-        + scatter_scratch(gu.shape[0])
-        + scatter_scratch(gd.shape[0]),
-        compiler_params=params(3),
-        name="scatter_ffn",
-    )(dn2, ffn, mid, cot, packs, gu, gd)
-
-
-def fourth_kernel(
-    dn1, tok, dmid, sums, packs, gq, go,
-    ig_own, norm_total, q_sum, o_sum,
-    slices, heard, plane_sum, heard_z, ns, nz, *rest,
-):
-    here = Here()
-    greet(here, PLANE, (1, 2, 3))
-    back = TensorSum(here, dn1, rest[0:5])
-    scatter_q = Scatter(here, True, gq, q_sum, rest[5 : 5 + SCATTER])
-    scatter_o = Scatter(here, False, go, o_sum, rest[5 + SCATTER : 5 + 2 * SCATTER])
-    back.start()
-    scatter_q.start()
-    scatter_o.start()
-    back.spread()
-    grad_n1 = back.result()
-    hat, inv_std = normed(tok[...].astype(F32))
-    grad_in, gain_sum, shift_sum = norm_back(grad_n1, hat, inv_std, norm_row(packs, 0))
-    ig_own[...] = (dmid[...] + grad_in).astype(BF16)
+def ffn_hidden(r, n2, cot, bucket, wu, wd, squares, grad_hidden):
+    width = n2.shape[2]
+    hidden = dot(n2[...].reshape(-1, width), wu[r])
+    live = bucket >= jnp.float32(r)
+    rectified = jnp.maximum(jnp.where(live, hidden, 0.0), 0.0)
+    squares[r] = (rectified * rectified).astype(BF16)
+    grad_square = dot(cot[...].reshape(-1, width), wd[r], ((1,), (1,)))
+    grad_hidden[r] = (grad_square * 2.0 * rectified).astype(BF16)
+
+
+def ffn_rows(s, left, right, part, transposed):
+    length, width = part.shape[1:]
+    rows = pl.ds(pl.multiple_of(s * length, length), length)
+    for n in range(width // (2 * CHUNK)):
+        cols = slice(n * 2 * CHUNK, (n + 1) * 2 * CHUNK)
+        total = None
+        for r in range(4):
+            if transposed:
+                term = dot(left[r, rows, :], right[r, cols, :], ((1,), (1,)))
+            else:
+                term = dot(left[r, rows, :], right[r, :, cols])
+            total = term if total is None else total + term
+        part[s, :, cols] = total.astype(BF16)
+
+
+def attend_back_body(head0, gm, qkva, wq, wo, tables, dp, part):
+    length = tables.shape[2]
+    width = gm.shape[2]
+    q_rows, k_rows, v_rows = qkva.at[0], qkva.at[1], qkva.at[2]
+    grad_att = dot(gm[...].reshape(2 * length, width), wo[...], ((1,), (1,))).astype(BF16)
+    for s in range(2):
+        rows = slice(s * length, (s + 1) * length)
+        cosine, sine = tables[s, 0], tables[s, 1]
+        lowest = tables[s, 2, :, 0:1]
+        for h in range(2):
+            cols = slice(h * HEAD_DIM, (h + 1) * HEAD_DIM)
+            active = tables[s, 4] > (head0 + h).astype(F32)
+            grad_heads = jnp.where(active, grad_att[rows, cols].astype(F32), 0.0).astype(BF16)
+            queries, key_rows, value_rows = q_rows[rows, cols], k_rows[rows, cols], v_rows[rows, cols]
+            weights = attention_weights(queries, key_rows, lowest)
+            grad_weights = dot(grad_heads, value_rows, ((1,), (1,)))
+            inner = jnp.sum(weights * grad_weights, -1, keepdims=True)
+            grad_scores = (weights * (grad_weights - inner)).astype(BF16)
+            grad_query = dot(grad_scores, key_rows) * HEAD_DIM ** (-0.5)
+            grad_keys = dot(grad_scores, queries, ((0,), (0,)))
+            grad_values = dot(weights.astype(BF16), grad_heads, ((0,), (0,)))
+            dp[0, rows, cols] = turn(grad_query, cosine, -sine).astype(BF16)
+            dp[1, rows, cols] = turn(grad_keys, cosine, -sine).astype(BF16)
+            dp[2, rows, cols] = grad_values.astype(BF16)
+
+
+def attend_back_rows(s, dp, wq, part):
+    length = part.shape[1]
+    rows = pl.ds(pl.multiple_of(s * length, length), length)
+    total = dot(dp[0, rows, :], wq[0], ((1,), (1,)))
+    total = total + dot(dp[1, rows, :], wq[1], ((1,), (1,)))
+    total = total + dot(dp[2, rows, :], wq[2], ((1,), (1,)))
+    part[s] = total.astype(BF16)
+
+
+def norm_share(here, values, bufs):
+    slices, heard, plane_sum, heard_z, ns, nz = bufs
     for k in range(8):
-        cols = slice(k * CHUNK, (k + 1) * CHUNK)
-        slices[k, 0:1, :] = gain_sum[:, cols]
-        slices[k, 1:2, :] = shift_sum[:, cols]
-        slices[k, 2:4, :] = sums[:, cols]
+        slices[k, 0:4, :] = values[:, k * CHUNK : (k + 1) * CHUNK]
         slices[k, 4:8, :] = jnp.zeros((4, CHUNK), F32)
-    norm_copies = []
+    copies = []
     for index, peer in enumerate(PLANE):
-        norm_copies.append(
+        copies.append(
             push(
                 slices.at[here.chunk(*peer)],
                 heard.at[index],
@@ -1128,16 +1094,19 @@
                 here.plane(*peer),
             )
         )
-    scatter_q.middle()
-    scatter_o.middle()
+    return copies
+
+
+def norm_share_along(here, copies, bufs):
+    slices, heard, plane_sum, heard_z, ns, nz = bufs
     mine = slices[here.chunk(0, 0, 0)]
     for index in range(7):
-        norm_copies[index].wait()
+        copies[index].wait()
         mine = mine + heard[index]
     plane_sum[...] = mine
-    z_copies = []
+    onward = []
     for step in (1, 2, 3):
-        z_copies.append(
+        onward.append(
             push(
                 plane_sum,
                 heard_z.at[here.z],
@@ -1147,29 +1116,188 @@
             )
         )
     heard_z[pl.ds(here.z, 1)] = mine[None]
+    return onward
+
+
+def back_kernel(*refs):
+    n2, cot, tables, packs, mid = refs[0:5]
+    tok, wq, wo, wu, wd, n1, q_rows, k_rows, v_rows, a_rows = refs[5:15]
+    out_all, ig_own, norm_total, q_sum, o_sum, u_sum, d_sum = refs[15:22]
+    wu_v, wd_v, qkva, tok_own, load_sem, squares, grad_hidden, part, part_f, dp = refs[22:32]
+    gu, gd, gq, go, gm, gm_own, dmid, sums, out_own = refs[32:41]
+    back_bufs, branch_bufs, final_one, final_two = refs[41:46], refs[46:51], refs[51], refs[52]
+    gm_sems, out_sems, norm_bufs = refs[53:56], refs[56:58], refs[58:64]
+    rest = refs[64:]
+    here = Here()
+    loads = []
+
+    def load(src, dst):
+        copy = pltpu.make_async_copy(src, dst, load_sem.at[len(loads)])
+        copy.start()
+        loads.append(copy)
+        return copy
+
+    first = [(load(wu.at[r], wu_v.at[r]), load(wd.at[r], wd_v.at[r])) for r in range(4)]
+    small = [load(src, qkva.at[i]) for i, src in enumerate((q_rows, k_rows, v_rows, a_rows))]
+    place = block(here.z, ROWS)
+    small.append(load(tok.at[place, :], tok_own))
+    scatters = [
+        Scatter(here, by_rows, grad, total, rest[i * SCATTER : (i + 1) * SCATTER] + (final,))
+        for i, (by_rows, grad, total, final) in enumerate(
+            (
+                (True, gu, u_sum, final_one),
+                (False, gd, d_sum, final_two),
+                (True, gq, q_sum, final_one.at[:, 0:3]),
+                (False, go, o_sum, final_one.at[:, 3:4]),
+            )
+        )
+    ]
+    scatter_u, scatter_d, scatter_q, scatter_o = scatters
+    bucket = jnp.concatenate([tables[0, 3, :, 0:1], tables[1, 3, :, 0:1]], 0)
+    for r in range(4):
+        first[r][0].wait()
+        first[r][1].wait()
+        ffn_hidden(r, n2, cot, bucket, wu_v, wd_v, squares, grad_hidden)
+    other = 1 - here.c
+    back = TensorSum(here, part, back_bufs)
+    ffn_rows(other, grad_hidden, wu_v, part, True)
+    greet(here, PLANE, (1, 2, 3))
+    back.start()
+    ffn_rows(here.c, grad_hidden, wu_v, part, True)
+    back.spread()
+    load_q = load(wq, wu_v.at[0:3])
+    length, width = n2.shape[1:]
+    rows_in = n2[...].reshape(2 * length, width)
+    for r in range(4):
+        gu[r] = dot(rows_in, grad_hidden[r], ((0,), (0,))).astype(BF16)
+    scatter_u.start()
+    grads_in = cot[...].reshape(2 * length, width)
+    for r in range(4):
+        gd[r] = dot(squares[r], grads_in, ((0,), (0,))).astype(BF16)
+    scatter_d.start()
+    branch = TensorSum(here, part_f, branch_bufs)
+    ffn_rows(other, squares, wd_v, part_f, False)
+    branch.start()
+    ffn_rows(here.c, squares, wd_v, part_f, False)
+    load_n1 = load(n1, wd_v.at[0:2])
+    load_o = load(wo, wd_v.at[2:3])
+    grad_n2 = back.result().astype(BF16).astype(F32)
+    hat, inv_std = normed(mid[...])
+    grad_mid, gain_sum, shift_sum = norm_back(grad_n2, hat, inv_std, norm_row(packs, 2))
+    grad_mid = cot[here.c, place, :].astype(F32) + grad_mid
+    dmid[...] = grad_mid
+    gm_own[...] = grad_mid.astype(BF16)
+    gather = TensorGather(here, gm_own, gm, *gm_sems)
+    gather.start()
+    sums[0:1, :] = gain_sum
+    sums[1:2, :] = shift_sum
+    scatter_u.middle()
+    gather.forward()
+    branch.spread()
+    for copy in small:
+        copy.wait()
+    load_o.wait()
+    load_q.wait()
+    load_n1.wait()
+    gather.finish()
+    back.finish()
+    head0 = here.z * 4 + here.c * 2
+    attend_back_body(head0, gm, qkva, wu_v, wd_v.at[2], tables, dp, part)
+    last = TensorSum(here, part, back_bufs)
+    attend_back_rows(other, dp, wu_v, part)
+    last.start()
+    attend_back_rows(here.c, dp, wu_v, part)
+    last.spread()
+    rows_in = wd_v[0:2].reshape(2 * length, width)
+    for j in range(3):
+        gq[j] = dot(rows_in, dp[j], ((0,), (0,))).astype(BF16)
+    scatter_q.start()
+    go[0] = dot(qkva[3], gm[...].reshape(2 * length, width), ((0,), (0,))).astype(BF16)
+    scatter_o.start()
+    scatter_d.middle()
+    out_own[...] = (mid[...] + branch.result().astype(BF16).astype(F32)).astype(BF16)
+    out_place = out_all.at[place, :]
+    out_copies = [
+        push(
+            out_own, out_place, out_sems[0].at[0, step - 1], out_sems[0].at[1, step - 1],
+            here.along(step),
+        )
+        for step in (2, 1, 3)
+    ]
+    keep = pltpu.make_async_copy(out_own, out_place, out_sems[1])
+    keep.start()
+    grad_n1 = last.result()
+    hat, inv_std = normed(tok_own[...].astype(F32))
+    grad_in, gain_sum, shift_sum = norm_back(grad_n1, hat, inv_std, norm_row(packs, 0))
+    ig_own[...] = (dmid[...] + grad_in).astype(BF16)
+    norm_copies = norm_share(
+        here, jnp.concatenate([gain_sum, shift_sum, sums[...]], 0), norm_bufs
+    )
+    scatter_u.last()
+    scatter_q.middle()
+    scatter_o.middle()
+    onward = norm_share_along(here, norm_copies, norm_bufs)
+    scatter_d.last()
+    for copy in onward:
+        copy.wait()
+    heard_z = norm_bufs[3]
+    norm_total[...] = ((heard_z[0] + heard_z[1]) + heard_z[2]) + heard_z[3]
+    scatter_u.sent()
     scatter_q.last()
     scatter_o.last()
-    for copy in z_copies:
+    branch.finish()
+    last.finish()
+    keep.wait()
+    for copy in out_copies:
         copy.wait()
-    norm_total[...] = ((heard_z[0] + heard_z[1]) + heard_z[2]) + heard_z[3]
-    back.finish()
-    scatter_q.finish()
-    scatter_o.finish()
-
-
-def fourth_call(dn1, tok, dmid, sums, packs, gq, go):
-    _, length, width = dn1.shape
-    return pl.pallas_call(
-        fourth_kernel,
-        out_shape=(
+    for scatter in scatters[1:]:
+        scatter.sent()
+    for scatter in scatters:
+        scatter.finish()
+
+
+def back_call(n2, cot, tables, packs, mid, tok, wq, wo, wu, wd, n1, rows):
+    _, length, width = n2.shape
+    both = pltpu.VMEM((2, length, width), BF16)
+    results = pl.pallas_call(
+        back_kernel,
+        out_shape=[
+            jax.ShapeDtypeStruct((length, width), BF16),
             jax.ShapeDtypeStruct((ROWS, width), BF16),
             jax.ShapeDtypeStruct((8, CHUNK), F32),
-            jax.ShapeDtypeStruct((gq.shape[0], CHUNK, 2 * CHUNK), F32),
+            jax.ShapeDtypeStruct((3, CHUNK, 2 * CHUNK), F32),
             jax.ShapeDtypeStruct((1, 2 * CHUNK, CHUNK), F32),
-        ),
-        in_specs=[VM] * 5 + [ANY, ANY],
-        out_specs=(VM, VM, ANY, ANY),
+            jax.ShapeDtypeStruct((4, CHUNK, 2 * CHUNK), F32),
+            jax.ShapeDtypeStruct((4, 2 * CHUNK, CHUNK), F32),
+        ],
+        in_specs=[VM] * 5 + [ANY] * 10,
+        out_specs=[ANY, VM, VM, ANY, ANY, ANY, ANY],
         scratch_shapes=[
+            pltpu.VMEM(wu.shape, BF16),
+            pltpu.VMEM(wd.shape, BF16),
+            pltpu.VMEM((4, 2 * length, CHUNK), BF16),
+            pltpu.VMEM((ROWS, width), BF16),
+            pltpu.SemaphoreType.DMA((16,)),
+            pltpu.VMEM((4, 2 * length, CHUNK), BF16),
+            pltpu.VMEM((4, 2 * length, CHUNK), BF16),
+            both,
+            both,
+            pltpu.VMEM((3, 2 * length, CHUNK), BF16),
+            pltpu.VMEM(wu.shape, BF16),
+            pltpu.VMEM(wd.shape, BF16),
+            pltpu.VMEM(wq.shape, BF16),
+            pltpu.VMEM(wo.shape, BF16),
+            both,
+            pltpu.VMEM((ROWS, width), BF16),
+            pltpu.VMEM((ROWS, width), F32),
+            pltpu.VMEM((2, width), F32),
+            pltpu.VMEM((ROWS, width), BF16),
+        ]
+        + sum_scratch(length, width) * 2
+        + [pltpu.VMEM((2, 4, CHUNK, CHUNK), F32)] * 2
+        + tensor_gather_sems()
+        + [pltpu.SemaphoreType.DMA((2, 3)), pltpu.SemaphoreType.DMA]
+        + [
             pltpu.VMEM((8, 8, CHUNK), F32),
             pltpu.VMEM((7, 8, CHUNK), F32),
             pltpu.VMEM((8, CHUNK), F32),
@@ -1177,12 +1305,14 @@
             pltpu.SemaphoreType.DMA((2, 7)),
             pltpu.SemaphoreType.DMA((2, 3)),
         ]
-        + sum_scratch(length, width)
-        + scatter_scratch(gq.shape[0])
+        + scatter_scratch(4)
+        + scatter_scratch(4)
+        + scatter_scratch(3)
         + scatter_scratch(1),
-        compiler_params=params(4),
-        name="scatter_attention",
-    )(dn1, tok, dmid, sums, packs, gq, go)
+        compiler_params=params(3),
+        name="back",
+    )(n2, cot, tables, packs, mid, tok, wq, wo, wu, wd, n1, *rows)
+    return results
 
 
 FIRST_SCALE = 1.0 / (1.0 - BETA_FIRST**STEP)
@@ -1208,17 +1338,26 @@
     return (update, first_new, second_new)
 
 
+AHEAD = 4
+
+
 def adam_kernel(*refs):
     sources = [refs[kind * 5 : kind * 5 + 4] for kind in range(4)]
     norm_grad, norm_master, norm_first, norm_second = [refs[kind * 5 + 4] for kind in range(4)]
-    outs = [refs[20 + kind * 5 : 24 + kind * 5] for kind in range(3)]
-    norm_outs = [refs[24 + kind * 5] for kind in range(3)]
-    tile = refs[35]
-    held = [refs[36 + kind * 4 : 40 + kind * 4] for kind in range(4)]
-    load_sem, store_sem = refs[52:54]
+    out_all = refs[20]
+    outs = [refs[21 + kind * 5 : 25 + kind * 5] for kind in range(3)]
+    norm_outs = [refs[25 + kind * 5] for kind in range(3)]
+    tile, output = refs[36:38]
+    held = [refs[38 + kind * 4 : 42 + kind * 4] for kind in range(4)]
+    load_sem, store_sem = refs[54:56]
     blocks = [(i, j) for i in range(4) for j in range(sources[0][i].shape[0])]
     loads = []
-    for index, (i, j) in enumerate(blocks):
+
+    def load():
+        index = len(loads)
+        if index == len(blocks):
+            return
+        i, j = blocks[index]
         loads.append([])
         for kind in range(4):
             copy = pltpu.make_async_copy(
@@ -1226,6 +1365,10 @@
             )
             copy.start()
             loads[index].append(copy)
+
+    for _ in range(AHEAD):
+        load()
+    output[...] = out_all[...].astype(F32)
     weight = norm_master[...]
     update, first_new, second_new = updated(
         weight, norm_grad[0:4, :], norm_first[...], norm_second[...]
@@ -1242,6 +1385,7 @@
             sums = (jnp.zeros((8, 128), F32), jnp.zeros((8, 128), F32))
         for copy in loads[index]:
             copy.wait()
+        load()
         grads, masters, firsts, seconds = [held[kind][i] for kind in range(4)]
 
         def step(k, carry):
@@ -1269,22 +1413,23 @@
         copy.wait()
 
 
-def adam_call(grads, masters, firsts, seconds):
+def adam_call(grads, masters, firsts, seconds, out_all):
     shapes = [master.shape for master in masters]
     like = [jax.ShapeDtypeStruct(shape, F32) for shape in shapes]
     specs = [ANY] * 4 + [VM]
     count = sum(shape[0] for shape in shapes[:4])
     results = pl.pallas_call(
         adam_kernel,
-        out_shape=like * 3 + [jax.ShapeDtypeStruct((16, 128), F32)],
-        in_specs=specs * 4,
-        out_specs=specs * 3 + [VM],
+        out_shape=like * 3
+        + [jax.ShapeDtypeStruct((16, 128), F32), jax.ShapeDtypeStruct(out_all.shape, F32)],
+        in_specs=specs * 4 + [VM],
+        out_specs=specs * 3 + [VM, VM],
         scratch_shapes=[pltpu.VMEM(shape, F32) for shape in shapes[:4]] * 4
         + [pltpu.SemaphoreType.DMA((4, count)), pltpu.SemaphoreType.DMA((3, count))],
-        compiler_params=local_params(),
+        compiler_params=local_params(60),
         name="adam",
-    )(*grads, *masters, *firsts, *seconds)
-    return results[0:5], results[5:10], results[10:15], results[15]
+    )(*grads, *masters, *firsts, *seconds, out_all)
+    return results[0:5], results[5:10], results[10:15], results[15], results[16]
 
 
 def total_kernel(tile, norms, tiles_z, plane_tile, tiles, zs, ps):
@@ -1334,13 +1479,20 @@
 
 
 def weight_kernel(*refs):
-    norms, updates, masters = refs[0], refs[1:6], refs[6:11]
-    outs = refs[11:16]
-    held = (refs[16:20], refs[20:24])
-    load_sem, store_sem = refs[24:26]
+    norms, updates, masters, packs = refs[0], refs[1:6], refs[6:11], refs[11]
+    ig_rows = refs[12:16]
+    outs = refs[16:21]
+    igrad, lamb_norms, share = refs[21:24]
+    held = (refs[24:28], refs[28:32])
+    load_sem, store_sem = refs[32:34]
     blocks = [(i, j) for i in range(4) for j in range(updates[i].shape[0])]
     loads = []
-    for index, (i, j) in enumerate(blocks):
+
+    def load():
+        index = len(loads)
+        if index == len(blocks):
+            return
+        i, j = blocks[index]
         loads.append([])
         for kind, source in enumerate((updates, masters)):
             copy = pltpu.make_async_copy(
@@ -1348,12 +1500,28 @@
             )
             copy.start()
             loads[index].append(copy)
+
+    for _ in range(AHEAD):
+        load()
     scales = LEARN_RATE * (norms[0:8, 0:1] / norms[8:16, 0:1])
     outs[4][...] = masters[4][...] - scales[4:8, :] * updates[4][...]
+    row = lax.broadcasted_iota(jnp.int32, norms.shape, 0)
+    lane = lax.broadcasted_iota(jnp.int32, norms.shape, 1)
+    flat = jnp.sum(jnp.where(row == lane, norms[...], 0.0), 0, keepdims=True)
+    lamb_norms[0:1, :] = flat[:, 0:8]
+    lamb_norms[1:2, :] = flat[:, 8:16]
+    counts = packs[0, 4:5, :]
+    for k in range(1, 8):
+        counts = counts + packs[k, 4:5, :]
+    share[...] = counts[:, 0:4] / (igrad.shape[0] * 8)
+    here = Here()
+    for step in range(4):
+        igrad[block(here.behind(step), ROWS), :] = ig_rows[step][...].astype(F32)
     stores = []
     for index, (i, j) in enumerate(blocks):
         for copy in loads[index]:
             copy.wait()
+        load()
         held[1][i][j] = held[1][i][j] - scales[i : i + 1, :] * held[0][i][j]
         copy = pltpu.make_async_copy(held[1][i].at[j], outs[i].at[j], store_sem.at[index])
         copy.start()
@@ -1362,20 +1530,26 @@
         copy.wait()
 
 
-def weight_call(norms, updates, masters):
+def weight_call(norms, updates, masters, packs, ig_rows):
     shapes = [master.shape for master in masters]
     specs = [ANY] * 4 + [VM]
     count = sum(shape[0] for shape in shapes[:4])
+    rows, width = ig_rows[0].shape
     return pl.pallas_call(
         weight_kernel,
-        out_shape=[jax.ShapeDtypeStruct(shape, F32) for shape in shapes],
-        in_specs=[VM] + specs * 2,
-        out_specs=specs,
+        out_shape=[jax.ShapeDtypeStruct(shape, F32) for shape in shapes]
+        + [
+            jax.ShapeDtypeStruct((4 * rows, width), F32),
+            jax.ShapeDtypeStruct((2, 8), F32),
+            jax.ShapeDtypeStruct((1, 4), F32),
+        ],
+        in_specs=[VM] + specs * 2 + [VM] * 5,
+        out_specs=specs + [VM, VM, VM],
         scratch_shapes=[pltpu.VMEM(shape, F32) for shape in shapes[:4]] * 2
         + [pltpu.SemaphoreType.DMA((2, count)), pltpu.SemaphoreType.DMA((count,))],
-        compiler_params=local_params(),
+        compiler_params=local_params(60),
         name="new_weights",
-    )(norms, *updates, *masters)
+    )(norms, *updates, *masters, packs, *ig_rows)
 
 
 def turn(values, cosine, sine):
@@ -1446,127 +1620,8 @@
     table[4] = jnp.broadcast_to(head_count.astype(F32), (length, HALF))
 
 
-def local_params():
-    return pltpu.CompilerParams(vmem_limit_bytes=60 << 20)
-
-
-def ffn_kernel(n2, cot, bucket, wu, wd, dn2, ffn, gu, gd, back_sum, ffn_sum):
-    quarter = pl.program_id(0)
-
-    @pl.when(quarter == 0)
-    def _():
-        back_sum[...] = jnp.zeros_like(back_sum)
-        ffn_sum[...] = jnp.zeros_like(ffn_sum)
-
-    rows_in = n2[...]
-    grads_in = cot[...]
-    hidden = dot(rows_in, wu[0])
-    live = bucket[:, 0:1] >= quarter.astype(F32)
-    rectified = jnp.maximum(jnp.where(live, hidden, 0.0), 0.0)
-    squared = (rectified * rectified).astype(BF16)
-    grad_square = dot(grads_in, wd[0], ((1,), (1,)))
-    grad_hidden = (grad_square * 2.0 * rectified).astype(BF16)
-    ffn_sum[...] += dot(squared, wd[0])
-    back_sum[...] += dot(grad_hidden, wu[0], ((1,), (1,)))
-    gu[0] = dot(rows_in, grad_hidden, ((0,), (0,))).astype(BF16)
-    gd[0] = dot(squared, grads_in, ((0,), (0,))).astype(BF16)
-
-    @pl.when(quarter == 3)
-    def _():
-        dn2[...] = back_sum[...].astype(dn2.dtype)
-        ffn[...] = ffn_sum[...].astype(ffn.dtype)
-
-
-def ffn_call(n2, cot, bucket, wu, wd):
-    _, length, width = n2.shape
-    total = 2 * length
-    whole = lambda shape: pl.BlockSpec(shape, lambda r: (0,) * len(shape))
-    per = lambda shape: pl.BlockSpec((1,) + shape, lambda r: (r, 0, 0))
-    dn2, ffn, gu, gd = pl.pallas_call(
-        ffn_kernel,
-        grid=(4,),
-        out_shape=(
-            jax.ShapeDtypeStruct((total, width), BF16),
-            jax.ShapeDtypeStruct((total, width), BF16),
-            jax.ShapeDtypeStruct((4, width, CHUNK), BF16),
-            jax.ShapeDtypeStruct((4, CHUNK, width), BF16),
-        ),
-        in_specs=[
-            whole((total, width)),
-            whole((total, width)),
-            whole((total, HALF)),
-            per((width, CHUNK)),
-            per((CHUNK, width)),
-        ],
-        out_specs=(
-            whole((total, width)),
-            whole((total, width)),
-            per((width, CHUNK)),
-            per((CHUNK, width)),
-        ),
-        scratch_shapes=[pltpu.VMEM((total, width), F32), pltpu.VMEM((total, width), F32)],
-        compiler_params=local_params(),
-        name="ffn",
-    )(n2.reshape(total, width), cot.reshape(total, width), bucket, wu, wd)
-    return dn2.reshape(2, length, width), ffn.reshape(2, length, width), gu, gd
-
-
-def attend_back_kernel(
-    head0, gm, n1, a_rows, q_rows, k_rows, v_rows, wq, wo, tables,
-    dn1, gq, go, dp,
-):
-    length = tables.shape[2]
-    grads = gm[...]
-    go[0] = dot(a_rows[...], grads, ((0,), (0,))).astype(BF16)
-    grad_att = dot(grads, wo[0], ((1,), (1,))).astype(BF16)
-    for s in range(2):
-        rows = slice(s * length, (s + 1) * length)
-        cosine, sine = tables[s, 0], tables[s, 1]
-        lowest = tables[s, 2, :, 0:1]
-        for h in range(2):
-            cols = slice(h * HEAD_DIM, (h + 1) * HEAD_DIM)
-            active = tables[s, 4] > (head0[0] + h).astype(F32)
-            grad_heads = jnp.where(active, grad_att[rows, cols].astype(F32), 0.0).astype(BF16)
-            queries, key_rows, value_rows = q_rows[rows, cols], k_rows[rows, cols], v_rows[rows, cols]
-            weights = attention_weights(queries, key_rows, lowest)
-            grad_weights = dot(grad_heads, value_rows, ((1,), (1,)))
-            inner = jnp.sum(weights * grad_weights, -1, keepdims=True)
-            grad_scores = (weights * (grad_weights - inner)).astype(BF16)
-            grad_query = dot(grad_scores, key_rows) * HEAD_DIM ** (-0.5)
-            grad_keys = dot(grad_scores, queries, ((0,), (0,)))
-            grad_values = dot(weights.astype(BF16), grad_heads, ((0,), (0,)))
-            dp[0, rows, cols] = turn(grad_query, cosine, -sine).astype(BF16)
-            dp[1, rows, cols] = turn(grad_keys, cosine, -sine).astype(BF16)
-            dp[2, rows, cols] = grad_values.astype(BF16)
-    for s in range(2):
-        rows = slice(s * length, (s + 1) * length)
-        total = dot(dp[0, rows, :], wq[0], ((1,), (1,)))
-        total = total + dot(dp[1, rows, :], wq[1], ((1,), (1,)))
-        total = total + dot(dp[2, rows, :], wq[2], ((1,), (1,)))
-        dn1[s] = total.astype(dn1.dtype)
-    rows_in = n1[...]
-    for j in range(3):
-        gq[j] = dot(rows_in, dp[j], ((0,), (0,))).astype(BF16)
-
-
-def attend_back_call(head0, gm, n1, a_rows, q_rows, k_rows, v_rows, wq, wo, tables):
-    _, length, width = n1.shape
-    return pl.pallas_call(
-        attend_back_kernel,
-        out_shape=(
-            jax.ShapeDtypeStruct((2, length, width), BF16),
-            jax.ShapeDtypeStruct((3, width, CHUNK), BF16),
-            jax.ShapeDtypeStruct((1, CHUNK, width), BF16),
-        ),
-        in_specs=[SM] + [VM] * 9,
-        out_specs=(VM,) * 3,
-        scratch_shapes=[pltpu.VMEM((3, 2 * length, CHUNK), BF16)],
-        compiler_params=local_params(),
-        name="attend_back",
-    )(
-        head0, gm.reshape(2 * length, width), n1.reshape(2 * length, width),
-        a_rows, q_rows, k_rows, v_rows, wq, wo, tables,
-    )
+def local_params(limit):
+    return pltpu.CompilerParams(vmem_limit_bytes=limit << 20)
 
 
 def fast_body(
@@ -1575,42 +1630,35 @@
     in_first, out_first, up_first, down_first, norm_first,
     in_second, out_second, up_second, down_second, norm_second,
 ):
-    length = tokens.shape[1]
-    groups_data = lax.axis_size("dp") * lax.axis_size("expert")
     tok, cot = tokens[0], cotangent[0]
     (n1, both_cot, tables, packs, n2, mid, q_rows, k_rows, v_rows, a_rows), (wq, wo, wu, wd) = front_call(
         head_counts, positions, buckets, tok, cot, norm_master,
         (in_master, out_master[None], up_master, down_master),
     )
-    bucket_share = jnp.sum(packs[:, 4, :4], 0) / (length * groups_data)
-    heads_here = 2 * CHUNK // HEAD_DIM
-    core = lax.rem(lax.axis_index("dp"), 2)
-    head0 = (lax.axis_index("tensor") * heads_here + core * (heads_here // 2))[None].astype(jnp.int32)
-    place = lax.axis_index("tensor") * ROWS
-    tok_own = lax.dynamic_slice_in_dim(tok, place, ROWS, 0)
-    cot_own = lax.dynamic_slice_in_dim(cot, place, ROWS, 0)
-    bucket = tables[:, 3].reshape(2 * length, HALF)
-    dn2, ffn, gu, gd = ffn_call(n2, both_cot, bucket, wu, wd)
-    gm, dmid, out_own, sums, up_sum, down_sum = third_call(dn2, ffn, mid, cot_own, packs, gu, gd)
-    dn1, gq, go = attend_back_call(head0, gm, n1, a_rows, q_rows, k_rows, v_rows, wq, wo, tables)
-    gather_tensor = lambda rows: lax.all_gather(rows, "tensor", axis=0, tiled=True).astype(F32)
-    output = gather_tensor(out_own)
-    ig_own, norm_sum, in_sum, out_sum = fourth_call(dn1, tok_own, dmid, sums, packs, gq, go)
-    input_grad = gather_tensor(ig_own)
+    out_all, ig_own, norm_sum, in_sum, out_sum, up_sum, down_sum = back_call(
+        n2, both_cot, tables, packs, mid, tok, wq, wo, wu, wd, n1,
+        (q_rows, k_rows, v_rows, a_rows),
+    )
+    ig_rows = [ig_own] + [
+        lax.ppermute(ig_own, "tensor", [(i, (i + step) % 4) for i in range(4)])
+        for step in (1, 2, 3)
+    ]
     masters = (in_master, out_master[None], up_master, down_master, norm_master)
     firsts = (in_first, out_first[None], up_first, down_first, norm_first)
     seconds = (in_second, out_second[None], up_second, down_second, norm_second)
-    updates, moments, squares, tile = adam_call(
-        (in_sum, out_sum, up_sum, down_sum, norm_sum), masters, firsts, seconds
+    updates, moments, squares, tile, output = adam_call(
+        (in_sum, out_sum, up_sum, down_sum, norm_sum), masters, firsts, seconds, out_all
     )
     norms = total_call(tile)
-    weights = weight_call(norms, updates, masters)
+    *weights, input_grad, lamb_norms, share = weight_call(
+        norms, updates, masters, packs, ig_rows
+    )
     flat = lambda group: (group[0], group[1][0], group[2], group[3], group[4])
     return (
         output[None],
         input_grad[None],
-        bucket_share,
-        norms[:, 0].reshape(2, 8),
+        share[0],
+        lamb_norms,
         *flat(weights),
         *flat(moments),
         *flat(squares),

time: 363 us -> 309 us (0.85)
  Pallas kernels: 323 us -> 302 us
  between operations: 14.8 us -> 1.54 us
  waiting for transfers between devices: 12.9 us -> 0.01 us
  other arithmetic: 6.88 us -> 0 us
  local copies, waits for them, and re-layouts: 5 us -> 0.84 us
  starting transfers between devices: 0.08 us -> 3.99 us
    pallas_call x4 -> x1, Pallas kernels: 158 us -> 140 us  [back_call(): pl.pallas_call(back_kernel, out_shape=[jax.ShapeDtypeStruct((length, widt...]
    all_gather x2 -> x0, waiting for transfers between devices: 12.2 us -> none  [fast_body(): lax.all_gather(rows, 'tensor', axis=0, tiled=True).astype(F32)]
    broadcast_in_dim x2 -> x0, other arithmetic: 5.58 us -> none  [the longest x1 2.79 us: fast_body(): input_grad[None]]
    ppermute x0 -> x3, starting transfers between devices: none -> 3.99 us  [fast_body(): lax.ppermute(ig_own, 'tensor', [(i, (i + step) % 4) for i in range(4)])]
    pallas_call x1, Pallas kernels: 15.7 us -> 11.8 us  [total_call(): pl.pallas_call(total_kernel, out_shape=jax.ShapeDtypeStruct((16, 128), F3...]
  transfers between devices with their start and end apart: 2 -> 3, of which waited for: 1 -> 0; matrix products, arithmetic and copies ran while one was open for 2% -> 0% of each run, Pallas kernels for 12% -> 10%
where the time goes in v3:
time: 309 us
  Pallas kernels  302 us (98%)
  starting transfers between devices  3.99 us (1%)
    pallas_call x1, Pallas kernels, back_call(): pl.pallas_call(back_kernel, out_shape=[jax.ShapeDtypeStruct((length, widt...  140 us
    pallas_call x1, Pallas kernels, front_call(): pl.pallas_call(front_kernel, out_shape=[both, both, jax.ShapeDtypeStruct(...  121 us
    pallas_call x1, Pallas kernels, adam_call(): pl.pallas_call(adam_kernel, out_shape=like * 3 + [jax.ShapeDtypeStruct((1...  19.2 us
    pallas_call x1, Pallas kernels, total_call(): pl.pallas_call(total_kernel, out_shape=jax.ShapeDtypeStruct((16, 128), F3...  11.8 us
    pallas_call x1, Pallas kernels, weight_call(): pl.pallas_call(weight_kernel, out_shape=[jax.ShapeDtypeStruct(shape, F32)...  10.2 us
  transfers between devices with their start and end apart: 3, of which 0 were waited for; matrix products, arithmetic and copies ran while one was open for 0% of the time, Pallas kernels for 10%

profile of v3, /device:TPU:0, one launch (start us, length us, event | category | flops | bytes accessed | tf_op | source)
XLA Modules:
  0.0 308.6 jit_solution(1627840027497819857)
XLA Ops:
  1.3 121.1 %front.1 = (bf16[2,256,2048]{2,1,0:T(8,128)(2,1)}, bf16[2,256,2048]{2,1,0:T(8,128)(2,1)}, f32[2,5,256,128]{3,2,1,0:T(8,128)}, f32[8,8,256]{2,1,0:T(8,128)}, bf16...) custom-call(s32[1]{0:T(128)S(6)} %copy.39.refs_0_, ...), custom_call_target="tpu_custom_call" | custom-call | tf_op jit(solution)/shard_map/front/pallas_call | solution.py:966
  122.4 140.0 %back.1 = (bf16[256,2048]{1,0:T(8,128)(2,1)}, bf16[64,2048]{1,0:T(8,128)(2,1)}, f32[8,256]{1,0:T(8,128)}, f32[3,256,512]{2,1,0:T(8,128)}, f32[1,512,256]{2,1,0:T...) custom-call(bf16[2,256,2048]{2,1,0:T(8,128)(2,1)} %get-tuple-element.65.refs_0_, ...), custom_call_target="tpu_custom_call" | custom-call | tf_op jit(solution)/shard_map/back/pallas_call | solution.py:1262
  262.4 0.8 collective-permute-start.2
  263.2 3.2 %collective-permute-start.1 = (bf16[64,2048]{1,0:T(8,128)(2,1)}, bf16[64,2048]{1,0:T(8,128)(2,1)S(1)}, u32[]{:S(2)}, u32[]{:S(2)}) collective-permute-start(bf16[64,2048]{1,0:T(8,128)(2,1)} %get-tuple-element.92.refs_12_), channel_id=1, source_target_pairs={{0,2},{1,3},{2,0},{3,1},{4,6},{5,7},{6,4},{7,5},{8,10},{9,11},{10,... | collective-permute-start | bytes 786440 | tf_op jit(solution)/shard_map/ppermute | solution.py:1643
  266.4 0.0 collective-permute-start
  266.4 19.2 %adam.1 = (f32[3,256,512]{2,1,0:T(8,128)}, f32[1,512,256]{2,1,0:T(8,128)}, f32[4,256,512]{2,1,0:T(8,128)}, f32[4,512,256]{2,1,0:T(8,128)}, f32[4,256]{1,0:T(4,12...) custom-call(f32[3,256,512]{2,1,0:T(8,128)} %get-tuple-element.79.ref, ...), custom_call_target="tpu_custom_call" | custom-call | tf_op jit(solution)/shard_map/adam/pallas_call | solution.py:1421
  285.6 11.8 %norm_totals.1.refs_0_ = f32[16,128]{1,0:T(8,128)} custom-call(f32[16,128]{1,0:T(8,128)} %get-tuple-element.86.tile), custom_call_target="tpu_custom_call" | custom-call | tf_op jit(solution)/shard_map/norm_totals/pallas_call | solution.py:1464
  297.3 0.0 collective-permute-done.2.refs_15_
  297.3 0.0 copy-start
  297.4 0.0 collective-permute-done.1.refs_14_
  297.4 0.0 copy-start.1
  297.4 0.0 collective-permute-done.refs_13_
  297.4 0.0 copy-start.2
  297.4 0.7 copy-done
  298.1 0.1 copy-done.1
  298.1 0.1 copy-done.2
  298.2 10.2 %new_weights.1 = (f32[3,256,512]{2,1,0:T(8,128)}, f32[1,512,256]{2,1,0:T(8,128)}, f32[4,256,512]{2,1,0:T(8,128)}, f32[4,512,256]{2,1,0:T(8,128)}, f32[4,256]{1,0...) custom-call(f32[16,128]{1,0:T(8,128)} %norm_totals.1.refs_0_, ...), custom_call_target="tpu_custom_call" | custom-call | tf_op jit(solution)/shard_map/new_weights/pallas_call | solution.py:1538
Async XLA Ops:
  262.4 34.9 %collective-permute-start.2 = (bf16[64,2048]{1,0:T(8,128)(2,1)}, bf16[64,2048]{1,0:T(8,128)(2,1)S(1)}, u32[]{:S(2)}, u32[]{:S(2)}) collective-permute-start(bf16[64,2048]{1,0:T(8,128)(2,1)} %get-tuple-element.92.refs_12_), channel_id=1, source_target_pairs={{0,3},{1,0},{2,1},{3,2},{4,7},{5,4},{6,5},{7,6},{8,11},{9,8},{10,9... | collective-permute-start | bytes 786440 | tf_op jit(solution)/shard_map/ppermute | solution.py:1643
  263.2 34.1 %collective-permute-start.1 = (bf16[64,2048]{1,0:T(8,128)(2,1)}, bf16[64,2048]{1,0:T(8,128)(2,1)S(1)}, u32[]{:S(2)}, u32[]{:S(2)}) collective-permute-start(bf16[64,2048]{1,0:T(8,128)(2,1)} %get-tuple-element.92.refs_12_), channel_id=1, source_target_pairs={{0,2},{1,3},{2,0},{3,1},{4,6},{5,7},{6,4},{7,5},{8,10},{9,11},{10,... | collective-permute-start | bytes 786440 | tf_op jit(solution)/shard_map/ppermute | solution.py:1643
  266.4 31.0 %collective-permute-start = (bf16[64,2048]{1,0:T(8,128)(2,1)}, bf16[64,2048]{1,0:T(8,128)(2,1)S(1)}, u32[]{:S(2)}, u32[]{:S(2)}) collective-permute-start(bf16[64,2048]{1,0:T(8,128)(2,1)} %get-tuple-element.92.refs_12_), channel_id=1, source_target_pairs={{0,1},{1,2},{2,3},{3,0},{4,5},{5,6},{6,7},{7,4},{8,9},{9,10},{10,1... | collective-permute-start | bytes 786440 | tf_op jit(solution)/shard_map/ppermute | solution.py:1643
  297.3 0.7 copy-start
  297.4 0.8 copy-start.1
  297.4 0.8 copy-start.2
